TPU v7x, 32 devices: a whole 2x2x4 slice. The times are simulated.
32 devices in a mesh: head: 4 (over y, x), blk: 8 (over z, core).
Axes of the slice: x: 2, y: 2, z: 4, core: 2. Of those that a mesh axis runs over, the one named last changes fastest.
Arguments:
- tokens: bfloat16 [8, 6144, 512], P('blk', 'head'), may hold values from -6 to 6
- cotangent: bfloat16 [8, 6144, 512], P('blk', 'head'), may hold values from -6 to 6
- doc_lengths: int32 [49], replicated, may hold values from 1 to 62, 1536 in all
- norm_gain1: bfloat16 [512], P(('head', 'blk')), may hold values from 0.25 to 1.75
- w_qkv: bfloat16 [512, 1536], P('head', 'blk'), may hold values from -0.25 to 0.25
- w_out: bfloat16 [512, 512], P('head', 'blk'), may hold values from -0.75 to 0.75
- b_out: bfloat16 [512], P(('head', 'blk')), may hold values from -3 to 3
- norm_gain2: bfloat16 [512], P(('head', 'blk')), may hold values from 0.25 to 1.75
- w_in: bfloat16 [512, 2048], P('head', 'blk'), may hold values from -0.25 to 0.25
- b_in: bfloat16 [2048], P(('head', 'blk')), may hold values from -3 to 3
- w_down: bfloat16 [2048, 512], P('head', 'blk'), may hold values from -0.125 to 0.125
- b_down: bfloat16 [512], P(('head', 'blk')), may hold values from -3 to 3
- w_sort: bfloat16 [512, 64], P('head', 'blk'), may hold values from -6 to 6
Outputs:
- output: bfloat16 [8, 6144, 512], P('blk', 'head')
- input_grad: float32 [8, 6144, 512], P('blk', 'head')
- grad_norm_gain1: float32 [512], P(('head', 'blk'))
- grad_w_qkv: float32 [512, 1536], P('head', 'blk')
- grad_w_out: float32 [512, 512], P('head', 'blk')
- grad_b_out: float32 [512], P(('head', 'blk'))
- grad_norm_gain2: float32 [512], P(('head', 'blk'))
- grad_w_in: float32 [512, 2048], P('head', 'blk')
- grad_b_in: float32 [2048], P(('head', 'blk'))
- grad_w_down: float32 [2048, 512], P('head', 'blk')
- grad_b_down: float32 [512], P(('head', 'blk'))
- grad_w_sort: float32 [512, 64], P('head', 'blk')
Inputs may be any that keep to these rules, and one draw needn't show every extreme that they name: `doc_lengths`: document lengths in blocks of 32 tokens; they sum to 1536 and the longest has exactly 62 blocks.
All inputs are finite; a program needn't handle non-finite values.
Results may differ from a plain program's by a relative error of at most 0.02.
The roundings to bfloat16 on the way count: a program that leaves them out, or rounds other values in their place, can miss the bound.
Values may be sent and summed in bfloat16 or wider, within the bound.
No kernel may reach another device: no remote copies, remote signals or barrier semaphores. Data moves between devices by JAX's collectives and lax.ppermute only.
A program may use at most 192 MiB of HBM per device.

v0:
```python
import functools

import jax
import jax.numpy as jnp
from jax import lax
from jax.experimental import pallas as pl
from jax.experimental.pallas import tpu as pltpu
from jax.sharding import Mesh
from jax.sharding import PartitionSpec as P

D = 512
HEADS = 8
HEAD_DIM = 64
FF = 2048
BLOCK = 32
SINK_ITERS = 8
DOC_MOST = 62
LANES = 128
PAIRS = HEADS // 2
HALO = 64
GROUPS = 4
CHEAP = pl.CostEstimate(flops=0, transcendentals=0, bytes_accessed=0)
EPSILON = 1e-05
NEGATIVE = -1e30
FLOOR = -1e20
LOG2E = 1.4426950408889634
TINY = 1e-37
F32 = jnp.float32
BF16 = jnp.bfloat16
NT = (((1,), (1,)), ((), ()))
NN = (((1,), (0,)), ((), ()))
TN = (((0,), (0,)), ((), ()))


def mm(a, b, dims=NN):
    return lax.dot_general(a, b, dims, preferred_element_type=F32)


def vmem(limit=56):
    return pltpu.CompilerParams(vmem_limit_bytes=limit * 1024 * 1024)


def once(shape):
    return pl.BlockSpec(shape, lambda *i: (0,) * len(shape), pipeline_mode=pl.Buffered(1))


def halves(value):
    high = value.astype(BF16)
    return high, (value - high.astype(F32)).astype(BF16)


def mm3(a, b, dims):
    (da,), (db,) = dims[0]
    ah, al = halves(a)
    bh, bl = halves(b)
    return mm(
        jnp.concatenate([ah, al, ah], axis=da), jnp.concatenate([bh, bh, bl], axis=db), dims
    )


def sink_mask(docn_ref, docc_ref, window, context):
    first = context
    fold = window - LANES
    lane = lax.broadcasted_iota(jnp.int32, (1, LANES), 1)
    docn = docn_ref[...]
    row = lax.broadcasted_iota(jnp.int32, (window, 1), 0)
    col = jnp.where((row >= first) & (lane < fold), lane + LANES, lane)
    docc = jnp.where(row >= first, docc_ref[1:2, :], docc_ref[0:1, :])
    return (docn == docc) & (docn >= 0) & (col < row)


def fold_pair(top, low, fold, join):
    lane = lax.broadcasted_iota(jnp.int32, (1, LANES), 1)
    both = join(top, low)
    return jnp.where(lane < fold, top, both), jnp.where(lane < fold, low, both)


def sink_weight(pair, odd):
    lane = lax.broadcasted_iota(jnp.int32, pair.shape, 1)
    zero = jnp.zeros_like(pair)
    if odd:
        return jnp.concatenate([zero, jnp.where(lane >= HEAD_DIM, pair, zero)], axis=0)
    return jnp.concatenate([jnp.where(lane < HEAD_DIM, pair, zero), zero], axis=0)


def refold(keys, fold):
    return jnp.concatenate([keys[LANES:], keys[fold:LANES]], axis=0)


def row_step(values):
    highest = jnp.maximum(jnp.max(values, axis=1, keepdims=True), FLOOR)
    total = jnp.sum(jnp.exp2(values - highest), axis=1, keepdims=True)
    return values - (highest + LOG2E * jnp.log(jnp.maximum(total, TINY)))


def column_step(values, context, fold):
    top, low = values[:context], values[context:]
    h1, h2 = fold_pair(
        jnp.max(top, axis=0, keepdims=True),
        jnp.max(low, axis=0, keepdims=True),
        fold,
        jnp.maximum,
    )
    h1, h2 = jnp.maximum(h1, FLOOR), jnp.maximum(h2, FLOOR)
    e1, e2 = jnp.exp2(top - h1), jnp.exp2(low - h2)
    t1, t2 = fold_pair(
        jnp.sum(e1, axis=0, keepdims=True), jnp.sum(e2, axis=0, keepdims=True), fold, jnp.add
    )
    t1, t2 = jnp.maximum(t1, TINY), jnp.maximum(t2, TINY)
    moved = jnp.concatenate(
        [top - (h1 + LOG2E * jnp.log(t1)), low - (h2 + LOG2E * jnp.log(t2))], axis=0
    )
    scales = jnp.concatenate([jnp.exp2(h1), jnp.exp2(h2), 1.0 / t1, 1.0 / t2], axis=0)
    return moved, e1, e2, scales


def sink_forward_kernel(
    own, context, a, b, c, d, e, w_ref, docn_ref, docc_ref, plan_ref, kept_ref, scale_ref, proj_ref,
    q_ref, k_ref, vals, kept, sems,
):
    window = q_ref.shape[1]
    fold = window - LANES
    at = 0
    for piece in (a, b, c, d, e):
        rows = piece.shape[0]
        for pair in range(PAIRS):
            q_ref[pair, at : at + rows, :] = piece[:, pair * LANES : (pair + 1) * LANES]
            k_ref[pair, at : at + rows, :] = piece[:, D + pair * LANES : D + (pair + 1) * LANES]
        at += rows

    def logits(pair, carry):
        permitted = sink_mask(docn_ref, docc_ref, window, context)
        queries, keys = q_ref[pair], k_ref[pair]
        keys_two = refold(keys, fold)
        for odd in range(2):
            projected = mm3(queries, sink_weight(w_ref[pair], odd), NT)
            proj_ref[2 * pair + odd] = projected
            top = mm3(projected[:context], keys[:LANES], NT)
            low = mm3(projected[context:], keys_two, NT)
            vals[2 * pair + odd] = jnp.where(
                permitted, LOG2E * jnp.concatenate([top, low], axis=0), NEGATIVE
            )
        return carry

    lax.fori_loop(0, PAIRS, logits, 0)

    def send(step):
        return pltpu.make_async_copy(kept.at[step], kept_ref.at[step], sems.at[step])

    def step(turn, carry):
        for head in range(HEADS):
            moved, top, low, scales = column_step(row_step(vals[head]), context, fold)
            kept[turn, head, :context, :] = top
            kept[turn, head, context:, :] = low
            scale_ref[turn, head] = scales
            vals[head] = moved
        send(turn).start()
        return carry

    lax.fori_loop(0, SINK_ITERS, step, 0)
    for head in range(HEADS):
        plan_ref[head] = (
            kept[SINK_ITERS - 1, head, context - own : context, :]
            * scale_ref[SINK_ITERS - 1, head, 2:3, :]
        ).astype(BF16)
    lax.fori_loop(0, SINK_ITERS, lambda turn, carry: (send(turn).wait(), carry)[1], 0)


def sink_backward_kernel(
    own, context, a, b, c, d, e, w_ref, kept_ref, scale_ref, proj, gl_ref, gh_ref,
    gm_ref, gw_ref, sa, sb, sd, se, q_ref, k_ref, vals, gq, gk, kept, sems,
):
    window = q_ref.shape[1]
    fold = window - LANES

    def fetch(step):
        return pltpu.make_async_copy(kept_ref.at[step], kept.at[step], sems.at[step])

    def begin(turn, carry):
        fetch(SINK_ITERS - 1 - turn).start()
        return carry

    lax.fori_loop(0, SINK_ITERS, begin, 0)
    at = 0
    for piece in (a, b, c, d, e):
        rows = piece.shape[0]
        for pair in range(PAIRS):
            q_ref[pair, at : at + rows, :] = piece[:, pair * LANES : (pair + 1) * LANES]
            k_ref[pair, at : at + rows, :] = piece[:, D + pair * LANES : D + (pair + 1) * LANES]
        at += rows

    def back(turn, carry):
        at = SINK_ITERS - 1 - turn
        fetch(at).wait()

        @pl.when(turn == 0)
        def _():
            for head in range(HEADS):
                ref = gl_ref if head < HEADS // 2 else gh_ref
                vals[head, : context - own, :] = jnp.zeros((context - own, LANES), F32)
                vals[head, context - own : context, :] = (
                    ref[head % (HEADS // 2)]
                    * kept[SINK_ITERS - 1, head, context - own : context, :]
                    * scale_ref[SINK_ITERS - 1, head, 2:3, :]
                )
                vals[head, context:, :] = jnp.zeros((window - context, LANES), F32)

        for head in range(HEADS):
            g1, g2 = vals[head, :context, :], vals[head, context:, :]
            s1, s2 = fold_pair(
                jnp.sum(g1, axis=0, keepdims=True),
                jnp.sum(g2, axis=0, keepdims=True),
                fold,
                jnp.add,
            )
            scales = scale_ref[at, head]
            e1, e2 = kept[at, head, :context, :], kept[at, head, context:, :]
            g1, g2 = g1 - e1 * (s1 * scales[2:3]), g2 - e2 * (s2 * scales[3:4])
            r1, r2 = jnp.sum(g1, axis=1, keepdims=True), jnp.sum(g2, axis=1, keepdims=True)
            vals[head, :context, :] = g1 - (e1 * scales[0:1]) * r1
            vals[head, context:, :] = g2 - (e2 * scales[1:2]) * r2
        return carry

    lax.fori_loop(0, SINK_ITERS, back, 0)

    def products(pair, carry):
        queries, keys = q_ref[pair], k_ref[pair]
        keys_two = refold(keys, fold)
        turned = []
        gq_total = jnp.zeros((window, LANES), F32)
        gk_total = jnp.zeros((window, LANES), F32)
        for odd in range(2):
            head = 2 * pair + odd
            g1, g2 = vals[head, :context, :], vals[head, context:, :]
            against = jnp.concatenate(
                [mm3(g1, keys[:LANES], NN), mm3(g2, keys_two, NN)], axis=0
            )
            gq_total = gq_total + mm3(against, sink_weight(w_ref[pair], odd), NN)
            u1 = mm3(g1, proj[head, :context, :], TN)
            u2 = mm3(g2, proj[head, context:, :], TN)
            gk_total = gk_total + jnp.concatenate(
                [u1[:fold], u1[fold:] + u2[fold:], u2[:fold]], axis=0
            )
            turned.append(mm3(against, queries, TN))
        half = lax.broadcasted_iota(jnp.int32, (HEAD_DIM, LANES), 1) < HEAD_DIM
        gw_ref[pair] = jnp.where(half, turned[0][:HEAD_DIM], turned[1][HEAD_DIM:])
        gq[pair] = gq_total * (1.0 / BLOCK)
        gk[pair] = gk_total * (1.0 / BLOCK)
        return carry

    lax.fori_loop(0, PAIRS, products, 0)
    for pair in range(PAIRS):
        gm_ref[:, pair * LANES : (pair + 1) * LANES] = gq[pair]
        gm_ref[:, D + pair * LANES : D + (pair + 1) * LANES] = gk[pair]
    at = 0
    for piece, ref in ((a, sa), (b, sb), (c, None), (d, sd), (e, se)):
        if ref is not None:
            ref[...] = gm_ref[at : at + piece.shape[0], :].astype(BF16)
        at += piece.shape[0]


HBM = pl.BlockSpec(memory_space=pl.ANY)
VMEM = pl.BlockSpec(memory_space=pltpu.VMEM)
SMEM = pl.BlockSpec(memory_space=pltpu.SMEM)


def sink_forward(pieces, weight, docn, docc, own, context):
    window = sum(piece.shape[0] for piece in pieces)
    kept = (SINK_ITERS, HEADS, window, LANES)
    return pl.pallas_call(
        functools.partial(sink_forward_kernel, own, context),
        in_specs=[VMEM] * 8,
        out_specs=[VMEM, HBM, VMEM, VMEM],
        out_shape=[
            jax.ShapeDtypeStruct((HEADS, own, LANES), BF16),
            jax.ShapeDtypeStruct(kept, F32),
            jax.ShapeDtypeStruct((SINK_ITERS, HEADS, 4, LANES), F32),
            jax.ShapeDtypeStruct((HEADS, window, LANES), F32),
        ],
        scratch_shapes=[
            pltpu.VMEM((PAIRS, window, LANES), F32),
            pltpu.VMEM((PAIRS, window, LANES), F32),
            pltpu.VMEM((HEADS, window, LANES), F32),
            pltpu.VMEM(kept, F32),
            pltpu.SemaphoreType.DMA((SINK_ITERS,)),
        ],
        cost_estimate=CHEAP,
        compiler_params=vmem(),
        name="sink_forward",
    )(*pieces, weight, docn, docc)


def sink_backward(pieces, weight, kept, scales, projected, low, high, own, context):
    window = sum(piece.shape[0] for piece in pieces)
    return pl.pallas_call(
        functools.partial(sink_backward_kernel, own, context),
        in_specs=[VMEM] * 6 + [HBM] + [VMEM] * 4,
        out_shape=[
            jax.ShapeDtypeStruct((window, 2 * D), F32),
            jax.ShapeDtypeStruct((PAIRS, HEAD_DIM, LANES), F32),
            *(
                jax.ShapeDtypeStruct((pieces[i].shape[0], 2 * D), BF16)
                for i in (0, 1, 3, 4)
            ),
        ],
        scratch_shapes=[
            *[pltpu.VMEM((PAIRS, window, LANES), F32)] * 2,
            pltpu.VMEM((HEADS, window, LANES), F32),
            *[pltpu.VMEM((PAIRS, window, LANES), F32)] * 2,
            pltpu.VMEM(kept.shape, F32),
            pltpu.SemaphoreType.DMA((SINK_ITERS,)),
        ],
        cost_estimate=CHEAP,
        compiler_params=vmem(),
        name="sink_backward",
    )(*pieces, weight, kept, scales, projected, low, high)


def normalise(values):
    centre = values - jnp.mean(values, axis=-1, keepdims=True)
    spread = jnp.mean(centre * centre, axis=-1, keepdims=True)
    return centre * lax.rsqrt(spread + EPSILON)


def context_kernel(halo_blocks, far_ref, near_ref, x_ref, gain_ref, w_ref, kvx_ref, nh_ref):
    x = jnp.concatenate([far_ref[...], near_ref[...], x_ref[...]], axis=0)
    blocks = x.shape[0]
    normed = normalise(x.astype(F32)) * gain_ref[...].reshape(1, 1, D)
    normed = normed.astype(BF16).reshape(blocks * 8, D)
    row = lax.broadcasted_iota(jnp.int32, (LANES, LANES), 0)
    lane = lax.broadcasted_iota(jnp.int32, (LANES, LANES), 1)
    turn = (lane == (row % 16) * 8 + row // 16).astype(F32).astype(BF16)
    turned = [
        mm(turn, normed[i * LANES : (i + 1) * LANES]).astype(BF16) for i in range(blocks // 16)
    ]
    rows = []
    for b in range(8):
        part = jnp.concatenate([part[b * 16 : (b + 1) * 16] for part in turned], axis=0)
        nh_ref[b] = part[:halo_blocks]
        rows.append(part)
    rows = jnp.concatenate(rows, axis=0)
    for head in range(0, HEADS, 2):
        out = mm(rows, w_ref[head * LANES : (head + 2) * LANES, :], NT).astype(BF16)
        for b in range(8):
            for e in range(2):
                kvx_ref[head + e, :, b * LANES : (b + 1) * LANES] = out[
                    b * blocks : (b + 1) * blocks, e * LANES : (e + 1) * LANES
                ]


def context_project(far, near, x, gain, w_kv):
    halo_blocks = far.shape[0] + near.shape[0]
    blocks = halo_blocks + x.shape[0]
    return pl.pallas_call(
        functools.partial(context_kernel, halo_blocks),
        grid=(BLOCK // 8,),
        in_specs=[
            *(pl.BlockSpec((v.shape[0], 8, D), lambda i: (0, i, 0)) for v in (far, near, x)),
            pl.BlockSpec((1, D), lambda i: (0, 0)),
            pl.BlockSpec((2 * D, D), lambda i: (0, 0)),
        ],
        out_specs=[
            pl.BlockSpec((HEADS, blocks, 8 * LANES), lambda i: (0, 0, i)),
            pl.BlockSpec((8, halo_blocks, D), lambda i: (i, 0, 0)),
        ],
        out_shape=[
            jax.ShapeDtypeStruct((HEADS, blocks, BLOCK * LANES), BF16),
            jax.ShapeDtypeStruct((BLOCK, halo_blocks, D), BF16),
        ],
        cost_estimate=CHEAP,
        compiler_params=vmem(),
        name="context_project",
    )(far, near, x, gain, w_kv)


def compact(values, lane_block):
    out = values[:BLOCK]
    for j in range(1, 4):
        out = jnp.where(lane_block == j, values[j * BLOCK : (j + 1) * BLOCK], out)
    return out


def spread(values, lane_block):
    zero = jnp.zeros_like(values)
    return jnp.concatenate([jnp.where(lane_block == j, values, zero) for j in range(4)], axis=0)


def softmax_pair(local, chosen, live):
    lane = lax.broadcasted_iota(jnp.int32, (BLOCK, LANES), 1)
    row = lax.broadcasted_iota(jnp.int32, (BLOCK, LANES), 0)
    local = jnp.where(row <= lax.rem(lane, BLOCK), local, NEGATIVE)
    chosen = jnp.where(live, chosen, NEGATIVE)
    highest = jnp.maximum(
        jnp.max(local, axis=0, keepdims=True), jnp.max(chosen, axis=0, keepdims=True)
    )
    el, es = jnp.exp(local - highest), jnp.exp(chosen - highest)
    total = jnp.sum(el, axis=0, keepdims=True) + jnp.sum(es, axis=0, keepdims=True)
    inverse = 1.0 / total
    return el * inverse, es * inverse


def half_mask(first):
    lane = lax.broadcasted_iota(jnp.int32, (LANES, LANES), 1)
    return (lane < HEAD_DIM) if first else (lane >= HEAD_DIM)


def attend_kernel(q_ref, kv_ref, kvx_ref, plan_ref, live_ref, att_ref, skv_ref, even_ref, odd_ref):
    own = plan_ref.shape[1]
    blocks = kvx_ref.shape[1]
    held = (even_ref, odd_ref)
    for e in range(2):
        plan = plan_ref[e][:, :blocks]
        for chunk in range(4):
            out = mm(plan, kvx_ref[e, :, chunk * 8 * LANES : (chunk + 1) * 8 * LANES])
            for b in range(8):
                at = (chunk * 8 + b) * (own + 1)
                held[e][at : at + own, :] = out[:, b * LANES : (b + 1) * LANES]
    lane_block = lax.broadcasted_iota(jnp.int32, (BLOCK, LANES), 1) // BLOCK
    lane_half = [half_mask(True), half_mask(False)]

    def group(turn, carry):
        chains = [(turn * GROUPS + i, e) for i in range(GROUPS) for e in range(2)]
        starts = [pl.multiple_of(g * LANES, LANES) for g, _ in chains]
        both, scores = [], []
        for (g, e), start in zip(chains, starts):
            local = kv_ref[pl.ds(start, LANES), e * LANES : (e + 1) * LANES]
            chosen = jnp.concatenate(
                [held[e][pl.ds(4 * g + i, BLOCK, stride=own + 1), :] for i in range(4)], axis=0
            ).astype(BF16)
            skv_ref[pl.ds(start, LANES), e * LANES : (e + 1) * LANES] = chosen
            both.append(jnp.concatenate([local, chosen], axis=0))
        for (g, e), start, kv in zip(chains, starts, both):
            q = q_ref[pl.ds(start, LANES), :] * 0.125
            qm = jnp.where(lane_half[e], q, jnp.zeros_like(q))
            out = mm(kv, qm, NT)
            scores.append((compact(out[:LANES], lane_block), compact(out[LANES:], lane_block)))
        weights = []
        for (g, e), (local, chosen) in zip(chains, scores):
            weights.append(softmax_pair(local, chosen, live_ref[pl.ds(g, 1), :] > 0.0))
        outs = []
        for (g, e), kv, (wl, ws) in zip(chains, both, weights):
            wide = jnp.concatenate(
                [spread(wl.astype(BF16), lane_block), spread(ws.astype(BF16), lane_block)], axis=0
            )
            turned = kv.T
            outs.append(mm(turned[HEAD_DIM:] if e == 0 else turned[:HEAD_DIM], wide))
        for i in range(GROUPS):
            att_ref[pl.ds(starts[2 * i], LANES), :] = jnp.concatenate(
                outs[2 * i : 2 * i + 2], axis=0
            ).T.astype(BF16)
        return carry

    lax.fori_loop(0, own // 4 // GROUPS, group, 0)


def attend(q, kv, kvx, plan, live):
    tok, own, blocks = q.shape[0], plan.shape[1], kvx.shape[1]
    return pl.pallas_call(
        attend_kernel,
        grid=(PAIRS,),
        in_specs=[
            pl.BlockSpec((tok, LANES), lambda j: (0, j)),
            pl.BlockSpec((tok, 2 * LANES), lambda j: (0, j)),
            pl.BlockSpec((2, blocks, BLOCK * LANES), lambda j: (j, 0, 0)),
            pl.BlockSpec((2, own, LANES), lambda j: (j, 0, 0)),
            pl.BlockSpec((tok // LANES, LANES), lambda j: (0, 0)),
        ],
        out_specs=[
            pl.BlockSpec((tok, LANES), lambda j: (0, j)),
            pl.BlockSpec((tok, 2 * LANES), lambda j: (0, j)),
        ],
        out_shape=[
            jax.ShapeDtypeStruct((tok, D), BF16),
            jax.ShapeDtypeStruct((tok, 2 * D), BF16),
        ],
        scratch_shapes=[pltpu.VMEM((BLOCK * (own + 1), LANES), F32)] * 2,
        cost_estimate=CHEAP,
        compiler_params=vmem(),
        name="attend",
    )(q, kv, kvx, plan, live)


def attend_back_kernel(
    q_ref, kv_ref, skv_ref, go_ref, kvx_ref, plan_ref, live_ref,
    gq_ref, gkv_ref, gh_ref, gp_ref, even_ref, odd_ref, leven_ref, lodd_ref,
):
    own = plan_ref.shape[1]
    blocks = kvx_ref.shape[1]
    halo = blocks - own
    held = (even_ref, odd_ref)
    lheld = (leven_ref, lodd_ref)
    lane_block = lax.broadcasted_iota(jnp.int32, (BLOCK, LANES), 1) // BLOCK
    lane_half = [half_mask(True), half_mask(False)]

    def group(turn, carry):
        chains = [(turn * GROUPS + i, e) for i in range(GROUPS) for e in range(2)]
        starts = [pl.multiple_of(g * LANES, LANES) for g, _ in chains]
        both, right, scores = [], [], []
        for (g, e), start in zip(chains, starts):
            lanes = slice(e * LANES, (e + 1) * LANES)
            rows = pl.ds(start, LANES)
            both.append(jnp.concatenate([kv_ref[rows, lanes], skv_ref[rows, lanes]], axis=0))
            q = q_ref[rows, :] * 0.125
            go = go_ref[rows, :]
            go = jnp.concatenate([go[:, HEAD_DIM:], go[:, :HEAD_DIM]], axis=1)
            qm = jnp.where(lane_half[e], q, jnp.zeros_like(q))
            gm = jnp.where(lane_half[1 - e], go, jnp.zeros_like(go))
            right.append(jnp.concatenate([qm, gm], axis=0))
        for kv, other in zip(both, right):
            out = mm(kv, other, NT)
            scores.append(
                [
                    compact(out[rows, lanes], lane_block)
                    for lanes in (slice(0, LANES), slice(LANES, 2 * LANES))
                    for rows in (slice(0, LANES), slice(LANES, 2 * LANES))
                ]
            )
        wides = []
        for (g, e), (sl, ss, dl, ds) in zip(chains, scores):
            wl, ws = softmax_pair(sl, ss, live_ref[pl.ds(g, 1), :] > 0.0)
            inner = jnp.sum(wl * dl + ws * ds, axis=0, keepdims=True)
            low = [v.astype(BF16) for v in (wl, ws, wl * (dl - inner), ws * (ds - inner))]
            wides.append(low)
        outs = []
        for (g, e), start, kv, other, (wl, ws, gl, gs) in zip(chains, starts, both, right, wides):
            weights = jnp.concatenate([spread(wl, lane_block), spread(ws, lane_block)], axis=0)
            gscore = jnp.concatenate([spread(gl, lane_block), spread(gs, lane_block)], axis=0)
            gboth = mm(jnp.concatenate([gscore, weights], axis=1), other)
            lheld[e][pl.ds(start, LANES), :] = gboth[:LANES]
            for i in range(4):
                held[e][pl.ds(4 * g + i, BLOCK, stride=own + 1), :] = gboth[
                    LANES + i * BLOCK : LANES + (i + 1) * BLOCK
                ]
            turned = kv.T
            outs.append(mm(turned[:HEAD_DIM] if e == 0 else turned[HEAD_DIM:], gscore))
        for i in range(GROUPS):
            gq_ref[pl.ds(starts[2 * i], LANES), :] = (
                jnp.concatenate(outs[2 * i : 2 * i + 2], axis=0).T * 0.125
            ).astype(BF16)
        return carry

    lax.fori_loop(0, own // 4 // GROUPS, group, 0)
    for e in range(2):
        plan = plan_ref[e][:, :blocks]
        gplan = jnp.zeros((own, blocks), F32)
        for chunk in range(4):
            lanes = slice(chunk * 8 * LANES, (chunk + 1) * 8 * LANES)
            grads = jnp.concatenate(
                [
                    held[e][(chunk * 8 + b) * (own + 1) : (chunk * 8 + b) * (own + 1) + own, :]
                    for b in range(8)
                ],
                axis=1,
            ).astype(BF16)
            gplan = gplan + mm(grads, kvx_ref[e, :, lanes], NT)
            gcontext = mm(plan, grads, TN)
            gh_ref[e, :, lanes] = gcontext[:halo].astype(BF16)
            for b in range(8):
                at = (chunk * 8 + b) * (own + 1)
                held[e][at : at + own, :] = gcontext[halo:, b * LANES : (b + 1) * LANES]
        gp_ref[e] = jnp.concatenate([gplan, jnp.zeros((own, LANES - blocks), F32)], axis=1)

    def finish(g, carry):
        start = pl.multiple_of(g * LANES, LANES)
        for e in range(2):
            rest = jnp.concatenate(
                [held[e][pl.ds(4 * g + i, BLOCK, stride=own + 1), :] for i in range(4)], axis=0
            )
            gkv_ref[pl.ds(start, LANES), e * LANES : (e + 1) * LANES] = (
                rest + lheld[e][pl.ds(start, LANES), :]
            ).astype(BF16)
        return carry

    lax.fori_loop(0, own // 4, finish, 0)


def attend_back(q, kv, skv, go, kvx, plan, live, first, pairs):
    tok, own, blocks = q.shape[0], plan.shape[1], kvx.shape[1]
    halo = blocks - own
    return pl.pallas_call(
        attend_back_kernel,
        grid=(pairs,),
        in_specs=[
            pl.BlockSpec((tok, LANES), lambda j: (0, j + first)),
            pl.BlockSpec((tok, 2 * LANES), lambda j: (0, j + first)),
            pl.BlockSpec((tok, 2 * LANES), lambda j: (0, j + first)),
            pl.BlockSpec((tok, LANES), lambda j: (0, j + first)),
            pl.BlockSpec((2, blocks, BLOCK * LANES), lambda j: (j + first, 0, 0)),
            pl.BlockSpec((2, own, LANES), lambda j: (j + first, 0, 0)),
            pl.BlockSpec((tok // LANES, LANES), lambda j: (0, 0)),
        ],
        out_specs=[
            pl.BlockSpec((tok, LANES), lambda j: (0, j)),
            pl.BlockSpec((tok, 2 * LANES), lambda j: (0, j)),
            pl.BlockSpec((2, halo, BLOCK * LANES), lambda j: (j, 0, 0)),
            pl.BlockSpec((2, own, LANES), lambda j: (j, 0, 0)),
        ],
        out_shape=[
            jax.ShapeDtypeStruct((tok, pairs * LANES), BF16),
            jax.ShapeDtypeStruct((tok, 2 * pairs * LANES), BF16),
            jax.ShapeDtypeStruct((2 * pairs, halo, BLOCK * LANES), BF16),
            jax.ShapeDtypeStruct((2 * pairs, own, LANES), F32),
        ],
        scratch_shapes=[pltpu.VMEM((BLOCK * (own + 1), LANES), F32)] * 4,
        cost_estimate=CHEAP,
        compiler_params=vmem(),
        name="attend_back",
    )(q, kv, skv, go, kvx, plan, live)


def halo_kernel(low_ref, high_ref, nh_ref, w_ref, far_ref, near_ref, gw_ref):
    halo = low_ref.shape[1]
    far = far_ref.shape[1]

    @pl.when(pl.program_id(0) == 0)
    def _():
        gw_ref[...] = jnp.zeros_like(gw_ref)

    rows = jnp.concatenate(
        [
            jnp.concatenate(
                [
                    ref[head, :, b * LANES : (b + 1) * LANES]
                    for ref in (low_ref, high_ref)
                    for head in range(ref.shape[0])
                ],
                axis=1,
            )
            for b in range(8)
        ],
        axis=0,
    )
    out = mm(rows, w_ref[...]).astype(BF16).reshape(8, halo, D)
    far_ref[...] = out[:, :far]
    near_ref[...] = out[:, far:]
    gw_ref[...] += mm(rows, nh_ref[...].reshape(8 * halo, D), TN)


def halo_back(low, high, nh, w_kv, far):
    halo = low.shape[1]
    half = pl.BlockSpec((HEADS // 2, halo, 8 * LANES), lambda i: (0, 0, i))
    return pl.pallas_call(
        halo_kernel,
        grid=(BLOCK // 8,),
        in_specs=[
            half,
            half,
            pl.BlockSpec((8, halo, D), lambda i: (i, 0, 0)),
            pl.BlockSpec((2 * D, D), lambda i: (0, 0)),
        ],
        out_specs=[
            pl.BlockSpec((8, far, D), lambda i: (i, 0, 0)),
            pl.BlockSpec((8, halo - far, D), lambda i: (i, 0, 0)),
            pl.BlockSpec((2 * D, D), lambda i: (0, 0)),
        ],
        out_shape=[
            jax.ShapeDtypeStruct((BLOCK, far, D), BF16),
            jax.ShapeDtypeStruct((BLOCK, halo - far, D), BF16),
            jax.ShapeDtypeStruct((2 * D, D), F32),
        ],
        cost_estimate=CHEAP,
        compiler_params=vmem(),
        name="halo_back",
    )(low, high, nh, w_kv)


def project_kernel(x_ref, gain_ref, wq_ref, wkv_ref, n_ref, q_ref, kv_ref, m_ref, head_ref, tail_ref):
    rows = x_ref.shape[0]
    blocks = rows // BLOCK
    normed = (normalise(x_ref[...].astype(F32)) * gain_ref[...]).astype(BF16)
    n_ref[...] = normed
    q = mm(normed, wq_ref[...], NT).astype(BF16)
    q_ref[...] = q
    kv = mm(normed, wkv_ref[...], NT).astype(BF16)
    kv_ref[...] = kv
    half = lax.broadcasted_iota(jnp.int32, (1, LANES), 1) < HEAD_DIM
    m_ref[:, :D] = jnp.mean(q.astype(F32).reshape(blocks, BLOCK, D), axis=1)
    for pair in range(PAIRS):
        even = kv[:, 2 * pair * LANES : (2 * pair + 1) * LANES]
        odd = kv[:, (2 * pair + 1) * LANES : (2 * pair + 2) * LANES]
        keys = jnp.where(half, even.astype(F32), odd.astype(F32))
        m_ref[:, D + pair * LANES : D + (pair + 1) * LANES] = jnp.mean(
            keys.reshape(blocks, BLOCK, LANES), axis=1
        )
    m_ref[:, 2 * D :] = jnp.mean(normed.astype(F32).reshape(blocks, BLOCK, D), axis=1)
    at = pl.program_id(0)
    ends = head_ref.shape[0] // blocks
    for ref, first in ((head_ref, 0), (tail_ref, pl.num_programs(0) - ends)):

        @pl.when((at >= first) & (at < first + ends))
        def _():
            ref[pl.ds(pl.multiple_of((at - first) * blocks, 8), blocks), :] = m_ref[...]


def project(x, gain, wt_q, wt_kv, ends):
    tok = x.shape[0]
    tile = 8 * BLOCK
    return pl.pallas_call(
        project_kernel,
        grid=(tok // tile,),
        in_specs=[
            pl.BlockSpec((tile, D), lambda i: (i, 0)),
            pl.BlockSpec((1, D), lambda i: (0, 0)),
            pl.BlockSpec((D, D), lambda i: (0, 0)),
            pl.BlockSpec((2 * D, D), lambda i: (0, 0)),
        ],
        out_specs=[
            pl.BlockSpec((tile, D), lambda i: (i, 0)),
            pl.BlockSpec((tile, D), lambda i: (i, 0)),
            pl.BlockSpec((tile, 2 * D), lambda i: (i, 0)),
            pl.BlockSpec((8, 3 * D), lambda i: (i, 0)),
            once((ends, 3 * D)),
            once((ends, 3 * D)),
        ],
        out_shape=[
            jax.ShapeDtypeStruct((tok, D), BF16),
            jax.ShapeDtypeStruct((tok, D), BF16),
            jax.ShapeDtypeStruct((tok, 2 * D), BF16),
            jax.ShapeDtypeStruct((tok // BLOCK, 3 * D), F32),
            jax.ShapeDtypeStruct((ends, 3 * D), F32),
            jax.ShapeDtypeStruct((ends, 3 * D), F32),
        ],
        cost_estimate=CHEAP,
        compiler_params=vmem(),
        name="project",
    )(x, gain, wt_q, wt_kv)


PIECE_ONE = 208
PIECE_TWO = 576
PARTS_TWO = 592


def place(vector, start):
    size = vector.shape[1]
    row = lax.broadcasted_iota(jnp.int32, (size, LANES), 0)
    lane = lax.broadcasted_iota(jnp.int32, (size, LANES), 1)
    pick = (lane == row + start).astype(F32).astype(BF16)
    return mm(jnp.broadcast_to(vector.astype(F32), (16, size)).astype(BF16), pick)


def pack_kernel(wqkv_ref, wsort_ref, g1, bo, g2, bi, bd, win_ref, wdown_ref, wout_ref, one_ref, two_ref):
    one_ref[:192, :] = wqkv_ref[...]
    row = place(g1[...], 0) + place(bo[...], 16) + place(g2[...], 32)
    row = row + place(bi[...], 48) + place(bd[...], 112)
    one_ref[192:, :] = jnp.concatenate([wsort_ref[...].astype(F32), row[:8]], axis=0).astype(BF16)
    two_ref[:256, :] = win_ref[...].astype(F32).T.astype(BF16)
    for k in range(4):
        two_ref[256 + k * 64 : 256 + (k + 1) * 64, :] = wdown_ref[:, k * LANES : (k + 1) * LANES]
    two_ref[512:, :] = wout_ref[...]


def pack(w_qkv, w_sort, vectors, w_in, w_down, w_out):
    return pl.pallas_call(
        pack_kernel,
        out_shape=[
            jax.ShapeDtypeStruct((PIECE_ONE, LANES), BF16),
            jax.ShapeDtypeStruct((PIECE_TWO, LANES), BF16),
        ],
        cost_estimate=CHEAP,
        compiler_params=vmem(),
        name="pack",
    )(w_qkv.T, w_sort.T, *(v.reshape(1, -1) for v in vectors), w_in, w_down.T, w_out.T)


def rows_at(start, size):
    return pl.ds(pl.multiple_of(start * size, size), size)


def each_owner(at_ref, visit):
    def planes(z, carry):
        for other in range(2):
            c = at_ref[2] ^ other
            for h in range(4):
                visit(other == 0, h, z, 2 * z + c, c)
        return carry

    lax.fori_loop(0, 4, planes, 0)


def each_piece(at_ref, mine_ref, other_ref, visit):
    def owner(own, h, z, b, c):
        source = mine_ref if own else other_ref
        visit(h, b, c, source.at[at_ref[1] ^ z, at_ref[0] ^ h])

    each_owner(at_ref, owner)


def widen(vecs, start, size):
    total = 32 * size
    lane = lax.broadcasted_iota(jnp.int32, (LANES, total), 1)
    row = lax.broadcasted_iota(jnp.int32, (LANES, total), 0)
    pick = (row == start + lax.rem(lane, size)).astype(F32).astype(BF16)
    every = mm(vecs, pick)
    owner = lax.broadcasted_iota(jnp.int32, (32, total), 0)
    lane = lax.broadcasted_iota(jnp.int32, (32, total), 1)
    return jnp.sum(jnp.where(owner == lane // size, every, 0.0), axis=0, keepdims=True)


def assemble_kernel(
    at_ref, mine_ref, other_ref, wq_ref, wkv_ref, ws_ref, g1_ref, bo_ref, g2_ref, bi_ref, bd_ref,
    vecs_ref,
):
    def visit(h, b, c, piece):
        lanes = slice(h * LANES, (h + 1) * LANES)
        wq_ref[rows_at(b, 64), lanes] = piece[:64, :]
        wkv_ref[rows_at(2 * b + c, 64), lanes] = piece[64:128, :]
        wkv_ref[rows_at(2 * b + 1 - c, 64), lanes] = piece[128:192, :]
        tail = piece[192:208, :].astype(F32)
        ws_ref[h, rows_at(b, 8), :] = tail[:8]
        vecs_ref[pl.ds(h * 8 + b, 1), :] = tail[8:9]

    each_piece(at_ref, mine_ref, other_ref, visit)
    vecs = vecs_ref[...].astype(BF16)
    g1_ref[...] = widen(vecs, 0, 16)
    bo_ref[...] = widen(vecs, 16, 16)
    g2_ref[...] = widen(vecs, 32, 16)
    bi_ref[...] = widen(vecs, 48, 64)
    bd_ref[...] = widen(vecs, 112, 16)


def assemble(at, mine, other):
    row = jax.ShapeDtypeStruct((1, D), F32)
    return pl.pallas_call(
        assemble_kernel,
        in_specs=[SMEM, VMEM, VMEM],
        out_shape=[
            jax.ShapeDtypeStruct((D, D), BF16),
            jax.ShapeDtypeStruct((2 * D, D), BF16),
            jax.ShapeDtypeStruct((PAIRS, HEAD_DIM, LANES), F32),
            row, row, row, jax.ShapeDtypeStruct((1, FF), F32), row,
        ],
        scratch_shapes=[pltpu.VMEM((32, LANES), F32)],
        cost_estimate=CHEAP,
        compiler_params=vmem(),
        name="assemble",
    )(at, mine, other)


GELU_A = 0.7978845608028654
GELU_B = 0.044715


def feed_tile(x, att, g, bo, g2, bi, bd, win, wdown, wout, acc_in, acc_down, acc_out, sums):
    middle = x.astype(F32) + mm(att, wout[...], NT) + bo
    centre = middle - jnp.mean(middle, axis=-1, keepdims=True)
    spread_ = jnp.mean(centre * centre, axis=-1, keepdims=True)
    inverse = lax.rsqrt(spread_ + EPSILON)
    hat = centre * inverse
    normed = (hat * g2).astype(BF16)
    normed_t = normed.T
    g_t = g.T
    out = jnp.zeros(middle.shape, F32)
    u = jnp.zeros(middle.shape, F32)
    cut = 512
    for k in range(FF // cut):
        cols = slice(k * cut, (k + 1) * cut)
        pre = mm(normed, win[cols, :], NT) + bi[:, cols]
        square = pre * pre
        t = jnp.tanh(GELU_A * pre * (1.0 + GELU_B * square))
        half = 0.5 * (1.0 + t)
        hidden = (pre * half).astype(BF16)
        slope = half + (0.5 * GELU_A) * pre * (1.0 - t * t) * (1.0 + (3.0 * GELU_B) * square)
        g_pre = (mm(g, wdown[:, cols], NN) * slope).astype(BF16)
        out = out + mm(hidden, wdown[:, cols], NT)
        u = u + mm(g_pre, win[cols, :], NN)
        part = mm(normed_t, g_pre)
        for i in range(2):
            acc_in[2 * k + i] += part[:, i * 256 : (i + 1) * 256]
        acc_down[:, cols] += mm(g_t, hidden)
        sums[4:5, cols] += jnp.sum(g_pre.astype(F32), axis=0, keepdims=True)
    gf = g.astype(F32)
    sums[1:2, :D] += jnp.sum(u * hat, axis=0, keepdims=True)
    sums[3:4, :D] += jnp.sum(gf, axis=0, keepdims=True)
    du = u * g2
    inner = jnp.mean(du * hat, axis=-1, keepdims=True)
    g_middle = gf + inverse * (du - jnp.mean(du, axis=-1, keepdims=True) - hat * inner)
    branch = g_middle.astype(BF16)
    sums[0:1, :D] += jnp.sum(branch.astype(F32), axis=0, keepdims=True)
    acc_out[...] += mm(branch.T, att)
    return (middle + out + bd).astype(BF16), g_middle, mm(branch, wout[...], NN).astype(BF16)


def clear(*refs):
    for ref in refs:
        ref[...] = jnp.zeros_like(ref)


def narrow(sums):
    total = jnp.zeros((32, LANES), F32)
    for index, start, size in ((0, 16, 16), (1, 32, 16), (4, 48, 64), (3, 112, 16)):
        width = 32 * size
        owner = lax.broadcasted_iota(jnp.int32, (32, width), 0)
        lane = lax.broadcasted_iota(jnp.int32, (32, width), 1)
        kept = jnp.where(owner == lane // size, sums[index : index + 1, :width], 0.0)
        row = lax.broadcasted_iota(jnp.int32, (width, LANES), 0)
        lane = lax.broadcasted_iota(jnp.int32, (width, LANES), 1)
        pick = (lane == start + lax.rem(row, size)).astype(F32).astype(BF16)
        total = total + mm(kept.astype(BF16), pick)
    return total


def feed_fast_kernel(
    at_ref, x_ref, att_ref, g_ref, bo_ref, g2_ref, bi_ref, bd_ref, mine_ref, other_ref,
    out_ref, gm_ref, ga_ref, keep_ref, send_ref,
    win, wdown, wout, acc_in, acc_down, acc_out, sums, vecs,
):
    @pl.when(pl.program_id(0) == 0)
    def _():
        def visit(h, b, c, piece):
            win[rows_at(b, 256), h * LANES : (h + 1) * LANES] = piece[:256, :]
            for k in range(4):
                lanes = slice(h * 512 + k * LANES, h * 512 + (k + 1) * LANES)
                wdown[rows_at(b, 64), lanes] = piece[256 + k * 64 : 320 + k * 64, :]
            wout[rows_at(b, 64), h * LANES : (h + 1) * LANES] = piece[512:576, :]

        each_piece(at_ref, mine_ref, other_ref, visit)
        clear(acc_in, acc_down, acc_out, sums)

    out_ref[...], gm_ref[...], ga_ref[...] = feed_tile(
        x_ref[...], att_ref[...], g_ref[...], bo_ref[...], g2_ref[...], bi_ref[...], bd_ref[...],
        win, wdown, wout, acc_in, acc_down, acc_out, sums,
    )

    @pl.when(pl.program_id(0) == pl.num_programs(0) - 1)
    def _():
        vecs[...] = narrow(sums)

        def owner(own, h, z, b, c):
            ref = keep_ref if own else send_ref
            for k in range(2):
                ref[z, h, k * LANES : (k + 1) * LANES, :] = acc_in[
                    b, h * LANES : (h + 1) * LANES, k * LANES : (k + 1) * LANES
                ].astype(BF16)
            for k in range(4):
                ref[z, h, 256 + k * 64 : 320 + k * 64, :] = acc_down[
                    rows_at(b, 64), h * 512 + k * LANES : h * 512 + (k + 1) * LANES
                ].astype(BF16)
            ref[z, h, 512:576, :] = acc_out[
                rows_at(b, 64), h * LANES : (h + 1) * LANES
            ].astype(BF16)
            ref[z, h, 576:592, :] = jnp.broadcast_to(
                vecs[pl.ds(h * 8 + b, 1), :], (16, LANES)
            ).astype(BF16)

        each_owner(at_ref, owner)


def feed_fast(at, x, att, g, bo, g2, bi, bd, mine, other):
    tok = x.shape[0]
    tile = 512
    tiled = pl.BlockSpec((tile, D), lambda i: (i, 0))
    parts = (4, 4, PARTS_TWO, LANES)
    return pl.pallas_call(
        feed_fast_kernel,
        grid=(tok // tile,),
        in_specs=[
            SMEM, tiled, tiled, tiled, once((1, D)), once((1, D)), once((1, FF)), once((1, D)),
            once(mine.shape), once(other.shape),
        ],
        out_specs=[tiled, tiled, tiled, once(parts), once(parts)],
        out_shape=[
            jax.ShapeDtypeStruct((tok, D), BF16),
            jax.ShapeDtypeStruct((tok, D), F32),
            jax.ShapeDtypeStruct((tok, D), BF16),
            jax.ShapeDtypeStruct(parts, BF16),
            jax.ShapeDtypeStruct(parts, BF16),
        ],
        scratch_shapes=[
            pltpu.VMEM((FF, D), BF16), pltpu.VMEM((D, FF), BF16), pltpu.VMEM((D, D), BF16),
            pltpu.VMEM((8, D, FF // 8), F32), pltpu.VMEM((D, FF), F32), pltpu.VMEM((D, D), F32),
            pltpu.VMEM((8, FF), F32), pltpu.VMEM((32, LANES), F32),
        ],
        cost_estimate=CHEAP,
        compiler_params=vmem(60),
        name="feed",
    )(at, x, att, g, bo, g2, bi, bd, mine, other)


def feed_slow_kernel(
    x_ref, att_ref, g_ref, bo_ref, g2_ref, bi_ref, bd_ref, win, wdown, wout,
    out_ref, gm_ref, ga_ref, acc_in, acc_down, acc_out, sums,
):
    @pl.when(pl.program_id(0) == 0)
    def _():
        clear(acc_in, acc_down, acc_out, sums)

    out_ref[...], gm_ref[...], ga_ref[...] = feed_tile(
        x_ref[...], att_ref[...], g_ref[...], bo_ref[...], g2_ref[...], bi_ref[...], bd_ref[...],
        win, wdown, wout, acc_in, acc_down, acc_out, sums,
    )


def feed_slow(x, att, g, bo, g2, bi, bd, win, wdown, wout):
    tok = x.shape[0]
    tile = 512
    tiled = pl.BlockSpec((tile, D), lambda i: (i, 0))
    wide, square, rows, cut = (D, FF), (D, D), (8, FF), (8, D, FF // 8)
    return pl.pallas_call(
        feed_slow_kernel,
        grid=(tok // tile,),
        in_specs=[
            tiled, tiled, tiled, once((1, D)), once((1, D)), once((1, FF)), once((1, D)),
            once((FF, D)), once(wide), once(square),
        ],
        out_specs=[tiled, tiled, tiled, once(cut), once(wide), once(square), once(rows)],
        out_shape=[
            jax.ShapeDtypeStruct((tok, D), BF16),
            jax.ShapeDtypeStruct((tok, D), F32),
            jax.ShapeDtypeStruct((tok, D), BF16),
            jax.ShapeDtypeStruct(cut, F32),
            jax.ShapeDtypeStruct(wide, F32),
            jax.ShapeDtypeStruct(square, F32),
            jax.ShapeDtypeStruct(rows, F32),
        ],
        cost_estimate=CHEAP,
        compiler_params=vmem(60),
        name="feed_whole",
    )(x, att, g, bo, g2, bi, bd, win, wdown, wout)


def split_kernel(which, at_ref, keep_ref, got_ref, *outs):
    for r, out in enumerate(outs):
        i = at_ref[which] ^ r
        out[0] = (keep_ref[i, 0].astype(F32) + got_ref[i, 0].astype(F32)).astype(BF16)


def split_sum(at, which, keep, got):
    one, two, rows, lanes = keep.shape
    block = pl.BlockSpec((one, 1, rows, lanes), lambda i: (0, i, 0, 0))
    return pl.pallas_call(
        functools.partial(split_kernel, which),
        grid=(two,),
        in_specs=[SMEM, block, block],
        out_specs=[pl.BlockSpec((1, rows, lanes), lambda i: (i, 0, 0))] * one,
        out_shape=[jax.ShapeDtypeStruct((two, rows, lanes), BF16)] * one,
        cost_estimate=CHEAP,
        compiler_params=vmem(),
        name="split_sum",
    )(at, keep, got)


def merge_kernel(which, at_ref, a_ref, b_ref, c_ref, d_ref, *outs):
    for r, out in enumerate(outs):
        i = at_ref[which] ^ r
        total = a_ref[i].astype(F32) + b_ref[i].astype(F32)
        out[...] = (total + c_ref[i].astype(F32) + d_ref[i].astype(F32)).astype(BF16)


def merge_sum(at, which, pieces):
    count, rows, lanes = pieces[0].shape
    return pl.pallas_call(
        functools.partial(merge_kernel, which),
        in_specs=[SMEM] + [VMEM] * 4,
        out_shape=[jax.ShapeDtypeStruct((rows, lanes), BF16)] * count,
        cost_estimate=CHEAP,
        compiler_params=vmem(),
        name="merge_sum",
    )(at, *pieces)


def last_two_kernel(a_ref, b_ref, c_ref, d_ref, gin_ref, gdown_ref, gout_ref, bo, g2, bi, bd):
    total = a_ref[...].astype(F32) + b_ref[...].astype(F32)
    total = total + c_ref[...].astype(F32) + d_ref[...].astype(F32)
    for k in range(2):
        gin_ref[:, k * LANES : (k + 1) * LANES] = total[k * LANES : (k + 1) * LANES]
    for k in range(4):
        gdown_ref[:, k * LANES : (k + 1) * LANES] = total[256 + k * 64 : 320 + k * 64]
    gout_ref[...] = total[512:576]
    row = total[576:577]
    bo[...], g2[...], bi[...], bd[...] = row[:, 16:32], row[:, 32:48], row[:, 48:112], row[:, 112:]


def last_two(pieces):
    return pl.pallas_call(
        last_two_kernel,
        out_shape=[
            jax.ShapeDtypeStruct((LANES, 256), F32),
            jax.ShapeDtypeStruct((64, 512), F32),
            jax.ShapeDtypeStruct((64, LANES), F32),
            *(jax.ShapeDtypeStruct((1, n), F32) for n in (16, 16, 64, 16)),
        ],
        cost_estimate=CHEAP,
        compiler_params=vmem(),
        name="last_two",
    )(*pieces)


def last_one_kernel(a_ref, b_ref, c_ref, d_ref, gw_ref, gs_ref, g1_ref):
    total = a_ref[...].astype(F32) + b_ref[...].astype(F32)
    total = total + c_ref[...].astype(F32) + d_ref[...].astype(F32)
    gw_ref[...] = total[:192]
    gs_ref[...] = total[192:200]
    g1_ref[...] = total[200:201, :16]


def last_one(pieces):
    return pl.pallas_call(
        last_one_kernel,
        out_shape=[
            jax.ShapeDtypeStruct((192, LANES), F32),
            jax.ShapeDtypeStruct((8, LANES), F32),
            jax.ShapeDtypeStruct((1, 16), F32),
        ],
        cost_estimate=CHEAP,
        compiler_params=vmem(),
        name="last_one",
    )(*pieces)


def widen_keys(gmk):
    half = lax.broadcasted_iota(jnp.int32, (gmk.shape[0], LANES), 1) < HEAD_DIM
    zero = jnp.zeros((gmk.shape[0], LANES), gmk.dtype)
    wide = []
    for pair in range(PAIRS):
        tile = gmk[:, pair * LANES : (pair + 1) * LANES]
        wide += [jnp.where(half, tile, zero), jnp.where(half, zero, tile)]
    return jnp.concatenate(wide, axis=1)


def weight_kernel(
    fast, at_ref, ql_ref, qh_ref, kvl_ref, kvh_ref, n_ref, wq_ref, wkv_ref, gm_ref,
    pa, pb, pc, pd, pe, halo_ref, gain_ref, gs_ref, keep_ref, send_ref, acc_q, acc_kv,
):
    @pl.when(pl.program_id(0) == 0)
    def _():
        means = jnp.concatenate([ref[:, 2 * D :] for ref in (pa, pb, pc, pd, pe)], axis=0)
        means = means.astype(BF16)
        grads = (gm_ref[...] * float(BLOCK)).astype(BF16)
        acc_q[...] = mm(grads[:, :D], means, TN)
        acc_kv[...] = halo_ref[...] + mm(widen_keys(grads[:, D:]), means, TN)

    normed = n_ref[...]
    for i, (q_ref, kv_ref) in enumerate(((ql_ref, kvl_ref), (qh_ref, kvh_ref))):
        acc_q[i * 256 : (i + 1) * 256, :] += mm(q_ref[...].T, normed)
        acc_kv[i * 512 : (i + 1) * 512, :] += mm(kv_ref[...].T, normed)

    @pl.when(pl.program_id(0) == pl.num_programs(0) - 1)
    def _():
        gain = jnp.sum(acc_q[...] * wq_ref[...].astype(F32), axis=0, keepdims=True)
        gain = gain + jnp.sum(acc_kv[...] * wkv_ref[...].astype(F32), axis=0, keepdims=True)
        gain = gain / gain_ref[...]
        if not fast:
            keep_ref[:D, :] = acc_q[...]
            keep_ref[D:, :] = acc_kv[...]
            send_ref[...] = jnp.broadcast_to(gain, (8, D))
            return
        def owner(own, h, z, b, c):
            ref = keep_ref if own else send_ref
            lanes = slice(h * LANES, (h + 1) * LANES)
            ref[h, z, :64, :] = acc_q[rows_at(b, 64), lanes].astype(BF16)
            ref[h, z, 64:128, :] = acc_kv[rows_at(2 * b + c, 64), lanes].astype(BF16)
            ref[h, z, 128:192, :] = acc_kv[rows_at(2 * b + 1 - c, 64), lanes].astype(BF16)
            share = pltpu.roll(
                jnp.broadcast_to(gain[:, lanes], (8, LANES)), lax.rem(LANES - 16 * b, LANES), 1
            )
            ref[h, z, 192:208, :] = jnp.concatenate(
                [gs_ref[h, rows_at(b, 8), :], share], axis=0
            ).astype(BF16)

        each_owner(at_ref, owner)


def weight_back(at, gq, gkv, normed, wt_q, wt_kv, gm, pieces, halo, gain, gsort, fast):
    tok = normed.shape[0]
    tile = 512
    parts = (4, 4, PIECE_ONE, LANES)
    shapes = (parts, parts) if fast else ((3 * D, D), (8, D))
    kind = BF16 if fast else F32
    rows = lambda width: pl.BlockSpec((tile, width), lambda i: (i, 0))
    return pl.pallas_call(
        functools.partial(weight_kernel, fast),
        grid=(tok // tile,),
        in_specs=[
            SMEM, rows(D // 2), rows(D // 2), rows(D), rows(D), rows(D), once((D, D)),
            once((2 * D, D)), once(gm.shape), *(once(p.shape) for p in pieces),
            once((2 * D, D)), once((1, D)), once(gsort.shape),
        ],
        out_specs=[once(shapes[0]), once(shapes[1])],
        out_shape=[
            jax.ShapeDtypeStruct(shapes[0], kind),
            jax.ShapeDtypeStruct(shapes[1], kind),
        ],
        scratch_shapes=[pltpu.VMEM((D, D), F32), pltpu.VMEM((2 * D, D), F32)],
        cost_estimate=CHEAP,
        compiler_params=vmem(),
        name="weight_back",
    )(at, *gq, *gkv, normed, wt_q, wt_kv, gm, *pieces, halo, gain, gsort)


def finish_kernel(
    skip, x_ref, ql_ref, qh_ref, kvl_ref, kvh_ref, wq_ref, wkv_ref, gm_ref, fa, fb, fd, fe,
    one_ref, two_ref, g_ref, gain_ref, out_ref, total, blocks_ref,
):
    rows = x_ref.shape[0]
    per = rows // BLOCK

    @pl.when(pl.program_id(0) == 0)
    def _():
        own, ends = fb.shape[0], fa.shape[0]
        halo = own + ends
        blocks_ref[...] = gm_ref[halo : halo + own, :] + fb[...].astype(F32) + fd[...].astype(F32)
        blocks_ref[own - ends :, :] += fa[...].astype(F32)
        blocks_ref[:ends, :] += fe[...].astype(F32)

    at = lax.broadcasted_iota(jnp.int32, (rows, rows), 0)
    lane = lax.broadcasted_iota(jnp.int32, (rows, rows), 1)
    order = (lane == lax.rem(at, BLOCK) * 8 + at // BLOCK).astype(F32).astype(BF16)
    value = mm(order, one_ref[...].reshape(rows, D))
    value = value + mm(ql_ref[...], wq_ref[: D // 2, :]) + mm(qh_ref[...], wq_ref[D // 2 :, :])
    value = value + mm(kvl_ref[...], wkv_ref[:D, :]) + mm(kvh_ref[...], wkv_ref[D:, :])
    grads = blocks_ref[pl.ds(pl.multiple_of(pl.program_id(0) * per, per), per), :].astype(BF16)
    block = mm(grads[:, :D], wq_ref[...]) + mm(widen_keys(grads[:, D:]), wkv_ref[...])
    value = value + jnp.broadcast_to(block[:, None, :], (per, BLOCK, D)).reshape(rows, D)
    total[...] = value

    @pl.when(pl.program_id(0) >= skip)
    def _():
        total[...] += mm(order, two_ref[...].reshape(rows, D))

    x = x_ref[...].astype(F32)
    centre = x - jnp.mean(x, axis=-1, keepdims=True)
    inverse = lax.rsqrt(jnp.mean(centre * centre, axis=-1, keepdims=True) + EPSILON)
    hat = centre * inverse
    du = total[...] * gain_ref[...]
    inner = jnp.mean(du * hat, axis=-1, keepdims=True)
    out_ref[...] = g_ref[...] + inverse * (
        du - jnp.mean(du, axis=-1, keepdims=True) - hat * inner
    )


def finish(x, gq, gkv, wt_q, wt_kv, gm, far, one, two, g_middle, gain):
    tok = x.shape[0]
    tile = 8 * BLOCK
    skip = (tok // BLOCK - two.shape[1]) // 8
    rows = lambda width: pl.BlockSpec((tile, width), lambda i: (i, 0))
    return pl.pallas_call(
        functools.partial(finish_kernel, skip),
        grid=(tok // tile,),
        in_specs=[
            rows(D), rows(D // 2), rows(D // 2), rows(D), rows(D), once((D, D)), once((2 * D, D)),
            once(gm.shape), *(once(f.shape) for f in far),
            pl.BlockSpec((BLOCK, 8, D), lambda i: (0, i, 0)),
            pl.BlockSpec((BLOCK, 8, D), lambda i: (0, jnp.maximum(i - skip, 0), 0)),
            rows(D), once((1, D)),
        ],
        out_specs=rows(D),
        out_shape=jax.ShapeDtypeStruct((tok, D), F32),
        scratch_shapes=[
            pltpu.VMEM((tile, D), F32),
            pltpu.VMEM((tok // BLOCK, 2 * D), F32),
        ],
        cost_estimate=CHEAP,
        compiler_params=vmem(),
        name="finish",
    )(x, *gq, *gkv, wt_q, wt_kv, gm, *far, one, two, g_middle, gain)


class Grid:
    def __init__(self):
        self.heads = lax.axis_size("head")
        self.planes = lax.axis_size("plane")
        self.cycles = 2 * self.planes
        self.head = lax.axis_index("head")
        self.plane = lax.axis_index("plane")
        self.core = lax.axis_index("core")
        self.cycle = 2 * self.plane + self.core
        self.place = self.cycle * self.heads + self.head

    def send(self, value, pairs):
        return lax.ppermute(value, ("head", "plane", "core"), pairs)

    def number(self, head, cycle):
        return head * self.cycles + cycle

    def along(self, steps):
        count = self.heads * self.cycles
        at = lambda place: self.number(place % self.heads, place // self.heads)
        return [(at(i), at(i + steps)) for i in range(count) if 0 <= i + steps < count]

    def swap_head(self, flip):
        return [
            (self.number(h, b), self.number(h ^ flip, b))
            for h in range(self.heads)
            for b in range(self.cycles)
        ]

    def swap_plane(self, flip):
        return [
            (self.number(h, b), self.number(h, b ^ (2 * flip)))
            for h in range(self.heads)
            for b in range(self.cycles)
        ]

    def swap_core(self):
        return [
            (self.number(h, b), self.number(h, b ^ 1))
            for h in range(self.heads)
            for b in range(self.cycles)
        ]


def in_order(pieces, index):
    stacked = jnp.stack(pieces)
    count = len(pieces)
    bit = 1
    while bit < count:
        swapped = jnp.stack([stacked[i ^ bit] for i in range(count)])
        stacked = jnp.where((index & bit) != 0, swapped, stacked)
        bit *= 2
    return stacked


def gather_all(grid, piece):
    got = [piece] + [grid.send(piece, grid.swap_plane(r)) for r in range(1, grid.planes)]
    got = in_order(got, grid.plane)
    got = [got] + [grid.send(got, grid.swap_head(r)) for r in range(1, grid.heads)]
    got = in_order(got, grid.head)
    got = in_order([got, grid.send(got, grid.swap_core())], grid.core)
    got = got.transpose(1, 2, 0, *range(3, got.ndim))
    return got.reshape(grid.heads, grid.cycles, *piece.shape)


def across_planes(parts):
    return lax.all_to_all(parts, "plane", 0, 0, tiled=True)


def across_heads(parts):
    return lax.all_to_all(parts, "head", 0, 0, tiled=True)


def scatter_sum(grid, parts):
    mine = lax.dynamic_index_in_dim(parts, grid.core, 0, keepdims=False)
    other = lax.dynamic_index_in_dim(parts, 1 - grid.core, 0, keepdims=False)
    got = grid.send(other, grid.swap_core())
    total = (mine.astype(F32) + got.astype(F32)).astype(BF16)
    total = jnp.sum(across_heads(total).astype(F32), axis=0).astype(BF16)
    return jnp.sum(across_planes(total).astype(F32), axis=0)


def as_rows(value):
    flat = value.reshape(-1)
    short = -flat.shape[0] % LANES
    return jnp.pad(flat, (0, short)).reshape(-1, LANES)


def by_owner(grid, value):
    columns, rows = value.shape
    cut = value.reshape(grid.planes, 2, columns // grid.cycles, grid.heads, rows // grid.heads)
    return cut.transpose(1, 3, 0, 2, 4)


def vector_by_owner(grid, value):
    cut = value.reshape(grid.heads, grid.planes, 2, -1)
    return cut.transpose(2, 0, 1, 3)


def rows_of(value):
    lead = value.shape[:3]
    flat = value.reshape(*lead, -1)
    short = -flat.shape[-1] % LANES
    flat = jnp.pad(flat, ((0, 0),) * 3 + ((0, short),))
    return flat.reshape(*lead, -1, LANES)


def after(value, *others):
    return lax.optimization_barrier((value, *others))[0]


def weights_slow(grid, vectors, parameters):
    w_qkv, w_sort, w_in, w_down, w_out = parameters
    heads, cycles = grid.heads, grid.cycles
    first = jnp.concatenate([as_rows(w_qkv.T), as_rows(w_sort), as_rows(jnp.concatenate(vectors))])
    wide, sort_rows = as_rows(w_qkv.T).shape[0], as_rows(w_sort).shape[0]
    got = gather_all(grid, first)
    span = w_qkv.shape[1]
    wt_qkv = (
        got[:, :, :wide]
        .reshape(heads, cycles, span, D // heads)
        .transpose(1, 2, 0, 3)
        .reshape(HEADS, 3, HEAD_DIM, D)
    )
    wt_q = wt_qkv[:, 0].reshape(D, D)
    paired = wt_qkv.reshape(PAIRS, 2, 3, HEAD_DIM, D)
    wt_kv = jnp.stack(
        [paired[:, 0, 1], paired[:, 0, 2], paired[:, 1, 2], paired[:, 1, 1]], axis=1
    ).reshape(2 * D, D)
    size = w_sort.shape[0] * w_sort.shape[1]
    w_pairs = (
        got[:, :, wide : wide + sort_rows]
        .reshape(heads, cycles, -1)[:, :, :size]
        .reshape(heads, cycles, *w_sort.shape)
        .transpose(1, 3, 0, 2)
        .reshape(HEAD_DIM, PAIRS, LANES)
        .transpose(1, 0, 2)
        .astype(F32)
    )
    flat = got[:, :, wide + sort_rows :].reshape(heads, cycles, -1)
    sizes = [v.shape[0] for v in vectors]
    cuts = [sum(sizes[:i]) for i in range(len(sizes) + 1)]
    rows = [
        flat[:, :, cuts[i] : cuts[i + 1]].reshape(1, -1).astype(F32) for i in range(len(sizes))
    ]
    second = jnp.concatenate([as_rows(w_in.T), as_rows(w_down.T), as_rows(w_out.T)])
    in_rows, down_rows = as_rows(w_in.T).shape[0], as_rows(w_down.T).shape[0]
    got = gather_all(grid, second)

    def whole(depth, columns, part):
        return (
            part.reshape(heads, cycles, -1)[:, :, : columns // cycles * (depth // heads)]
            .reshape(heads, cycles, columns // cycles, depth // heads)
            .transpose(1, 2, 0, 3)
            .reshape(columns, depth)
        )

    feed = (
        whole(D, FF, got[:, :, :in_rows]),
        whole(FF, D, got[:, :, in_rows : in_rows + down_rows]),
        whole(D, D, got[:, :, in_rows + down_rows :]),
    )
    return wt_q, wt_kv, w_pairs, rows, feed


def matrix(rows, shape):
    flat = rows.reshape(-1)[: shape[0] * shape[1]]
    return flat.reshape(shape[1], shape[0]).T


def gradients_two_slow(grid, acc_in, acc_down, acc_out, sums, parameters, vectors):
    w_qkv, w_sort, w_in, w_down, w_out = parameters
    low = [
        rows_of(by_owner(grid, v.astype(BF16))) for v in (acc_in.transpose(0, 2, 1).reshape(FF, D), acc_down, acc_out)
    ]
    order = ((0, D), (1, D), (4, FF), (3, D))
    small = [vector_by_owner(grid, sums[i, :n]) for i, n in order]
    low.append(rows_of(jnp.concatenate(small, axis=-1).astype(BF16)))
    total = scatter_sum(grid, jnp.concatenate(low, axis=3))
    cuts = [0]
    for item in low:
        cuts.append(cuts[-1] + item.shape[3])
    g_in, g_down, g_out = (
        matrix(total[cuts[i] : cuts[i + 1]], w.shape) for i, w in enumerate((w_in, w_down, w_out))
    )
    flat = total[cuts[3] :].reshape(-1)
    sizes = [v.shape[0] for v in vectors[1:]]
    at = [sum(sizes[:i]) for i in range(5)]
    return g_in, g_down, g_out, *(flat[at[i] : at[i + 1]] for i in range(4))


def gradients_one_slow(grid, both, gain, gsort, parameters, vectors):
    w_qkv, w_sort = parameters[:2]
    q = both[:D].reshape(HEADS, HEAD_DIM, D)
    kv = both[D:].reshape(PAIRS, 4, HEAD_DIM, D)
    k = jnp.stack([kv[:, 0], kv[:, 3]], axis=1).reshape(HEADS, HEAD_DIM, D)
    v = jnp.stack([kv[:, 1], kv[:, 2]], axis=1).reshape(HEADS, HEAD_DIM, D)
    wide = jnp.stack([q, k, v], axis=1).reshape(3 * D, D)
    sort = gsort.transpose(0, 2, 1).reshape(grid.heads, D // grid.heads, grid.planes, 2, -1)
    low = [
        rows_of(by_owner(grid, wide.astype(BF16))),
        rows_of(sort.transpose(3, 0, 2, 1, 4).astype(BF16)),
        rows_of(vector_by_owner(grid, gain[0]).astype(BF16)),
    ]
    total = scatter_sum(grid, jnp.concatenate(low, axis=3))
    one, two = low[0].shape[3], low[0].shape[3] + low[1].shape[3]
    size = w_sort.shape[0] * w_sort.shape[1]
    return (
        matrix(total[:one], w_qkv.shape),
        total[one:two].reshape(-1)[:size].reshape(w_sort.shape),
        total[two:].reshape(-1)[: vectors[0].shape[0]],
    )


def per_device(
    tokens, cotangent, doc_lengths, norm_gain1, w_qkv, w_out, b_out, norm_gain2, w_in, b_in,
    w_down, b_down, w_sort,
):
    grid = Grid()
    heads = grid.heads
    x = tokens[0]
    upstream = cotangent[0]
    tok = x.shape[0]
    own = tok // BLOCK
    context = HALO + own
    window = HALO + own + HALO
    second = HALO - own
    fast = heads == 4 and grid.cycles == 8
    at = jnp.stack([grid.head, grid.plane, grid.core]).astype(jnp.int32)
    vectors = (norm_gain1, b_out, norm_gain2, b_in, b_down)
    parameters = (w_qkv, w_sort, w_in, w_down, w_out)

    three = range(1, 4)
    if fast:
        one, two = pack(w_qkv, w_sort, vectors, w_in, w_down, w_out)
        ones = [one] + [grid.send(one, grid.swap_head(r)) for r in three]
        x_send = after(x, *ones)
        ones = jnp.stack(ones)
        ones = [ones] + [grid.send(ones, grid.swap_plane(r)) for r in three]
    else:
        x_send = x
    halo_one = grid.send(x_send, grid.along(1))
    halo_two = grid.send(x_send[tok - second * BLOCK :], grid.along(2))
    if fast:
        two = after(two, *ones)
        ones = jnp.stack(ones)
        other = grid.send(ones, grid.swap_core())
        twos = [two] + [grid.send(two, grid.swap_plane(r)) for r in three]
        wt_q, wt_kv, w_pairs, *rows = assemble(at, ones, other)
    else:
        wt_q, wt_kv, w_pairs, rows, feed_weights = weights_slow(grid, vectors, parameters)
    gain_one, bias_out, gain_two, bias_in, bias_down = rows

    normed, q, kv, means, means_head, means_tail = project(x, gain_one, wt_q, wt_kv, second)
    means_send, means_head, means_tail = lax.optimization_barrier(
        (means, means_head, means_tail, halo_one, halo_two)
    )[:3]
    pieces = (
        grid.send(means_tail, grid.along(2)),
        grid.send(means_send, grid.along(1)),
        means,
        grid.send(means_send, grid.along(-1)),
        grid.send(means_head, grid.along(-2)),
    )
    blocked = lambda value: value.reshape(-1, BLOCK, D)
    kvx, normed_halo = context_project(
        blocked(halo_two), blocked(halo_one), blocked(x), gain_one, wt_kv
    )
    if fast:
        twos = jnp.stack(lax.optimization_barrier((*twos, *pieces))[:4])
        twos = [twos] + [grid.send(twos, grid.swap_head(r)) for r in three]

    begin = grid.place * own
    position = begin - HALO + jnp.arange(window, dtype=jnp.int32)
    doc_ends = jnp.cumsum(doc_lengths, dtype=jnp.int32)
    ended = jnp.sum(
        (doc_ends[None, :] <= position[:, None]).astype(jnp.int32), axis=1, dtype=jnp.int32
    )
    span_end = (grid.cycle + 1) * heads * own
    doc = jnp.where((position >= 0) & (position < span_end), ended, -1)
    fold = window - LANES
    docc = jnp.stack([doc[:LANES], jnp.concatenate([doc[LANES:], doc[fold:LANES]])])
    docn = doc[:, None]
    live = (doc[HALO:context] == doc[HALO - 1 : context - 1]) & (doc[HALO:context] >= 0)
    live = jnp.repeat(live.astype(F32), BLOCK).reshape(tok // LANES, LANES)

    plan, *kept = sink_forward(pieces, after(w_pairs, kvx), docn, docc, own, context)
    if fast:
        twos = jnp.stack(lax.optimization_barrier((*twos, plan))[:4], axis=1)
        feed_weights = (twos, grid.send(twos, grid.swap_core()))
    attended, skv = attend(q, kv, kvx, plan, live)

    if fast:
        output, g_middle, g_att, keep, send = feed_fast(
            at, x, attended, upstream, bias_out, gain_two, bias_in, bias_down, *feed_weights
        )
        got = grid.send(send, grid.swap_core())
    else:
        output, g_middle, g_att, *sums = feed_slow(
            x, attended, upstream, bias_out, gain_two, bias_in, bias_down, *feed_weights
        )
        g_in, g_down, g_out, g_b_out, g_gain_two, g_b_in, g_b_down = gradients_two_slow(
            grid, *sums, parameters, vectors
        )

    gq_low, gkv_low, gh_low, gplan_low = attend_back(
        q, kv, skv, g_att, kvx, plan, live, 0, PAIRS // 2
    )
    if fast:
        twos = split_sum(at, 1, after(keep, gh_low), got)
        g_att = after(g_att, *twos)
        twos = [twos[0]] + [grid.send(twos[r], grid.swap_plane(r)) for r in three]
    gq_high, gkv_high, gh_high, gplan_high = attend_back(
        q, kv, skv, g_att, kvx, plan, live, PAIRS // 2, PAIRS // 2
    )
    gq, gkv = (gq_low, gq_high), (gkv_low, gkv_high)
    gn_far, gn_near, g_kv_halo = halo_back(gh_low, gh_high, normed_halo, wt_kv, second)
    back_one = grid.send(gn_near, grid.along(-1))
    back_two = grid.send(gn_far, grid.along(-2))
    gmeans, gsort, *sends = sink_backward(
        pieces, w_pairs, *kept, gplan_low, after(gplan_high, gn_near), own, context
    )
    gmeans_here = after(gmeans, *twos) if fast else gmeans
    keep, send = weight_back(
        at, gq, gkv, normed, wt_q, wt_kv, gmeans_here, pieces, g_kv_halo, gain_one, gsort, fast
    )
    if fast:
        got = grid.send(send, grid.swap_core())
        ones = split_sum(at, 0, keep, got)
        ones = [ones[0]] + [grid.send(ones[r], grid.swap_head(r)) for r in three]
        sends = lax.optimization_barrier((*sends, ones[0]))[:4]
        twos = merge_sum(at, 0, lax.optimization_barrier((*twos, ones[0]))[:4])
        twos = [twos[0]] + [grid.send(twos[r], grid.swap_head(r)) for r in three]
    steps = (-2, -1, 1, 2)
    far = [grid.send(value, grid.along(step)) for value, step in zip(sends, steps)]
    if fast:
        ones = merge_sum(at, 1, ones)
        ones = [ones[0]] + [grid.send(ones[r], grid.swap_plane(r)) for r in three]
    input_grad = finish(
        x, gq, gkv, wt_q, wt_kv, gmeans, far, back_one, back_two, g_middle, gain_one
    )
    if fast:
        g_wqkv, g_sort, g_gain_one = last_one(ones)
        g_in, g_down, g_out, *small = last_two(twos)
        g_wqkv, g_sort, g_down, g_out = g_wqkv.T, g_sort.T, g_down.T, g_out.T
        g_gain_one = g_gain_one[0]
        g_b_out, g_gain_two, g_b_in, g_b_down = (value[0] for value in small)
    else:
        g_wqkv, g_sort, g_gain_one = gradients_one_slow(
            grid, keep, send, gsort, parameters, vectors
        )
    return (
        output[None], input_grad[None], g_gain_one, g_wqkv, g_out, g_b_out, g_gain_two, g_in,
        g_b_in, g_down, g_b_down, g_sort,
    )


def solution(mesh):
    heads, cycles = mesh.shape["head"], mesh.shape["blk"]
    fine = Mesh(mesh.devices.reshape(heads, cycles // 2, 2), ("head", "plane", "core"))
    both = P(("head", "plane", "core"))
    split = P("head", ("plane", "core"))
    stream = P(("plane", "core"), "head", None)
    return jax.shard_map(
        per_device,
        mesh=fine,
        in_specs=(
            stream, stream, P(), both, split, split, both, both, split, both, split, both, split,
        ),
        out_specs=(
            stream, stream, both, split, split, both, both, split, both, split, both, split,
        ),
        check_vma=False,
    )
```

profile of v0, /device:TPU:12, one launch (start us, length us, event | category | flops | bytes accessed | tf_op | source)
XLA Modules:
  0.0 330.5 jit_solution(3439194981720123638)
XLA Ops:
  17.2 11.8 %collective-permute-done.5 = bf16[4,208,128]{2,1,0:T(8,128)(2,1)S(1)} collective-permute-done((bf16[4,208,128]{2,1,0:T(8,128)(2,1)S(1)}, bf16[4,208,128]{2,1,0:T(8,128)(2,1)S(1)}, u32[]{:S(2)}, u32[]{:S(2)}) %collective-permute-start.5) | collective-permute-done | bytes 213024 | tf_op jit(solution)/shard_map/ppermute | solution.py:1271
  36.4 4.3 %collective-permute-start.14 = (bf16[576,128]{1,0:T(8,128)(2,1)S(1)}, bf16[576,128]{1,0:T(8,128)(2,1)}, u32[]{:S(2)}, u32[]{:S(2)}) collective-permute-start(bf16[576,128]{1,0:T(8,128)(2,1)S(1)} %copy-done.21), channel_id=1, source_target_pairs={{0,4},{1,5},{2,6},{3,7},{4,0},{5,1},{6,2},{7,3},{8,12},{9,13},{10,... | collective-permute-start | bytes 442376 | tf_op jit(solution)/shard_map/ppermute | solution.py:1271
  45.5 8.3 %project.1 = (bf16[1536,512]{1,0:T(8,128)(2,1)}, bf16[1536,512]{1,0:T(8,128)(2,1)}, bf16[1536,1024]{1,0:T(8,128)(2,1)}, f32[48,1536]{1,0:T(8,128)}, f32[16,1536]{1,0:T(8,128)}, /*index=5*/f32[16,1536]{1,0:T(8,128)}) custom-call(bf16[1536,512]{1,0:T(8,128)(2,1)} %bitcast.59, f32[1,512]{1,0:T(1,128)} %get-tuple-element.113.gain_ref, ...), custom_call_target="tpu_custom_call" | custom-call | tf_op jit(solution)/shard_map/project/pallas_call | solution.py:698
  53.8 5.0 %collective-permute-done.7 = bf16[512,512]{1,0:T(8,128)(2,1)} collective-permute-done((bf16[512,512]{1,0:T(8,128)(2,1)}, bf16[512,512]{1,0:T(8,128)(2,1)}, u32[]{:S(2)}, u32[]{:S(2)}) %collective-permute-start.7) | collective-permute-done | bytes 524320 | tf_op jit(solution)/shard_map/ppermute | solution.py:1271
  59.9 16.4 %collective-permute-start.11 = (f32[48,1536]{1,0:T(8,128)}, f32[48,1536]{1,0:T(8,128)S(1)}, u32[]{:S(2)}, u32[]{:S(2)}) collective-permute-start(f32[48,1536]{1,0:T(8,128)} %get-tuple-element.124.c.pc), channel_id=1, source_target_pairs={{8,0},{16,8},{24,16},{1,24},{9,1},{17,9},{25,17},{2,25},{10,2},{18... | collective-permute-start | bytes 884744 | tf_op jit(solution)/shard_map/ppermute | solution.py:1271
  81.8 3.9 %collective-permute-start.12 = (f32[16,1536]{1,0:T(8,128)}, f32[16,1536]{1,0:T(8,128)S(1)}, u32[]{:S(2)}, u32[]{:S(2)}) collective-permute-start(f32[16,1536]{1,0:T(8,128)} %get-tuple-element.125), channel_id=1, source_target_pairs={{16,0},{24,8},{1,16},{9,24},{17,1},{25,9},{2,17},{10,25},{18,2},{2... | collective-permute-start | bytes 294920 | tf_op jit(solution)/shard_map/ppermute | solution.py:1271
  85.7 7.3 %collective-permute-done.9.a.pa = f32[16,1536]{1,0:T(8,128)S(1)} collective-permute-done((f32[16,1536]{1,0:T(8,128)}, f32[16,1536]{1,0:T(8,128)S(1)}, u32[]{:S(2)}, u32[]{:S(2)}) %collective-permute-start.9) | collective-permute-done | bytes 98336 | tf_op jit(solution)/shard_map/ppermute | solution.py:1271
  100.1 11.2 %context_project.1 = (bf16[8,112,4096]{2,1,0:T(8,128)(2,1)}, bf16[32,64,512]{2,1,0:T(8,128)(2,1)}) custom-call(bf16[16,32,512]{2,1,0:T(8,128)(2,1)} %bitcast.21.far_ref, bf16[48,32,512]{2,1,0:T(8,128)(2,1)} %bitcast.65, bf16[48,32,512]{2,1,0:T(8,128)(2,1)} %bitcast.60, f32[1,512]{1,0:T(1,128)} %get-tuple-element.113.gain_ref, ...), custom_call_target="tpu_custom_call" | custom-call | tf_op jit(solution)/shard_map/context_project/pallas_call | solution.py:354
  111.3 12.5 %sink_forward.1 = (bf16[8,48,128]{2,1,0:T(8,128)(2,1)}, f32[8,8,176,128]{3,2,1,0:T(8,128)}, f32[8,8,4,128]{3,2,1,0:T(4,128)}, f32[8,176,128]{2,1,0:T(8,128)}) custom-call(f32[16,1536]{1,0:T(8,128)} %copy-done.7, f32[48,1536]{1,0:T(8,128)} %copy-done.3, f32[48,1536]{1,0:T(8,128)} %get-tuple-element.124.c.pc, f32[48,1536]{1,0:T(8,128)} %copy-done.2, ...), custom_call_target="tpu_custom_call" | custom-call | tf_op jit(solution)/shard_map/sink_forward/pallas_call | solution.py:270
  127.0 12.3 %attend.1 = (bf16[1536,512]{1,0:T(8,128)(2,1)}, bf16[1536,1024]{1,0:T(8,128)(2,1)}) custom-call(bf16[1536,512]{1,0:T(8,128)(2,1)} %get-tuple-element.116.q_ref, bf16[1536,1024]{1,0:T(8,128)(2,1)} %get-tuple-element.117.kv_ref, bf16[8,112,4096]{2,1,0:T(8,128)(2,1)} %get-tuple-element.119.kvx_ref, bf16[8,48,128]{2,1,0:T(8,128)(2,1)} %get-tuple-element.128.plan_ref, ...), custom_call_target="tpu_custom_call" | custom-call | tf_op jit(solution)/shard_map/attend/pallas_call | solution.py:458
  139.3 38.4 %feed.1 = (bf16[1536,512]{1,0:T(8,128)(2,1)}, f32[1536,512]{1,0:T(8,128)}, bf16[1536,512]{1,0:T(8,128)(2,1)}, bf16[4,4,592,128]{3,2,1,0:T(8,128)(2,1)}, bf16[4,4,592,128]{3,2,1,0:T(8,128)(2,1)}) custom-call(s32[3]{0:T(128)} %pad_add_fusion.1.at_ref, bf16[1536,512]{1,0:T(8,128)(2,1)} %bitcast.61, bf16[1536,512]{1,0:T(8,128)(2,1)} %get-tuple-element.129.att_ref, ...), custom_call_target="tpu_custom_call" | custom-call | tf_op jit(solution)/shard_map/feed/pallas_call | solution.py:954
  178.0 12.8 %attend_back.2 = (bf16[1536,256]{1,0:T(8,128)(2,1)}, bf16[1536,512]{1,0:T(8,128)(2,1)}, bf16[4,64,4096]{2,1,0:T(8,128)(2,1)}, f32[4,48,128]{2,1,0:T(8,128)}) custom-call(bf16[1536,512]{1,0:T(8,128)(2,1)} %get-tuple-element.116.q_ref, bf16[1536,1024]{1,0:T(8,128)(2,1)} %get-tuple-element.117.kv_ref, bf16[1536,1024]{1,0:T(8,128)(2,1)} %get-tuple-element.145.skv_ref, ...), custom_call_target="tpu_custom_call" | custom-call | tf_op jit(solution)/shard_map/attend_back/pallas_call | solution.py:580
  192.2 4.4 %split_sum.2 = (bf16[4,592,128]{2,1,0:T(8,128)(2,1)}, bf16[4,592,128]{2,1,0:T(8,128)(2,1)}, bf16[4,592,128]{2,1,0:T(8,128)(2,1)}, bf16[4,592,128]{2,1,0:T(8,128)(2,1)}) custom-call(s32[3]{0:T(128)} %pad_add_fusion.1.at_ref, bf16[4,4,592,128]{3,2,1,0:T(8,128)(2,1)} %get-tuple-element.150.keep_ref, bf16[4,4,592,128]{3,2,1,0:T(8,128)(2,1)} %copy-done.4), custom_call_target="tpu_custom_call" | custom-call | tf_op jit(solution)/shard_map/split_sum/pallas_call | solution.py:1031
  200.1 12.8 %attend_back.3 = (bf16[1536,256]{1,0:T(8,128)(2,1)}, bf16[1536,512]{1,0:T(8,128)(2,1)}, bf16[4,64,4096]{2,1,0:T(8,128)(2,1)}, f32[4,48,128]{2,1,0:T(8,128)}) custom-call(bf16[1536,512]{1,0:T(8,128)(2,1)} %get-tuple-element.116.q_ref, bf16[1536,1024]{1,0:T(8,128)(2,1)} %get-tuple-element.117.kv_ref, bf16[1536,1024]{1,0:T(8,128)(2,1)} %get-tuple-element.145.skv_ref, ...), custom_call_target="tpu_custom_call" | custom-call | tf_op jit(solution)/shard_map/attend_back/pallas_call | solution.py:580
  212.9 8.5 %halo_back.1 = (bf16[32,16,512]{2,1,0:T(8,128)(2,1)}, bf16[32,48,512]{2,1,0:T(8,128)(2,1)}, f32[1024,512]{1,0:T(8,128)}) custom-call(bf16[4,64,4096]{2,1,0:T(8,128)(2,1)} %get-tuple-element.149.low_ref, bf16[4,64,4096]{2,1,0:T(8,128)(2,1)} %get-tuple-element.165.high_ref, bf16[32,64,512]{2,1,0:T(8,128)(2,1)} %get-tuple-element.166.nh_ref, ...), custom_call_target="tpu_custom_call" | custom-call | tf_op jit(solution)/shard_map/halo_back/pallas_call | solution.py:642
  223.4 9.2 %sink_backward.1 = (f32[176,1024]{1,0:T(8,128)}, f32[4,64,128]{2,1,0:T(8,128)}, bf16[16,1024]{1,0:T(8,128)(2,1)}, bf16[48,1024]{1,0:T(8,128)(2,1)}, bf16[48,1024]{1,0:T(8,128)(2,1)}, /*index=5*/bf16[16,1024]{1,0:T(8,128)(2,1)}) custom-call(f32[16,1536]{1,0:T(8,128)} %copy-done.7, f32[48,1536]{1,0:T(8,128)} %copy-done.3, f32[48,1536]{1,0:T(8,128)} %get-tuple-element.124.c.pc, ...), custom_call_target="tpu_custom_call" | custom-call | tf_op jit(solution)/shard_map/sink_backward/pallas_call | solution.py:295
  232.6 7.7 %collective-permute-done.22.c_ref = bf16[4,592,128]{2,1,0:T(8,128)(2,1)S(1)} collective-permute-done((bf16[4,592,128]{2,1,0:T(8,128)(2,1)}, bf16[4,592,128]{2,1,0:T(8,128)(2,1)S(1)}, u32[]{:S(2)}, u32[]{:S(2)}) %collective-permute-start.22) | collective-permute-done | bytes 606240 | tf_op jit(solution)/shard_map/ppermute | solution.py:1271
  240.3 12.7 %collective-permute-done.23.d_ref = bf16[4,592,128]{2,1,0:T(8,128)(2,1)S(1)} collective-permute-done((bf16[4,592,128]{2,1,0:T(8,128)(2,1)}, bf16[4,592,128]{2,1,0:T(8,128)(2,1)S(1)}, u32[]{:S(2)}, u32[]{:S(2)}) %collective-permute-start.23) | collective-permute-done | bytes 606240 | tf_op jit(solution)/shard_map/ppermute | solution.py:1271
  253.0 9.7 %weight_back.1 = (bf16[4,4,208,128]{3,2,1,0:T(8,128)(2,1)}, bf16[4,4,208,128]{3,2,1,0:T(8,128)(2,1)}) custom-call(s32[3]{0:T(128)} %pad_add_fusion.1.at_ref, bf16[1536,256]{1,0:T(8,128)(2,1)} %get-tuple-element.147.ql_ref, bf16[1536,256]{1,0:T(8,128)(2,1)} %get-tuple-element.157.qh_ref, bf16[1536,512]{1,0:T(8,128)(2,1)} %get-tuple-element.158.kvl_ref, ...), custom_call_target="tpu_custom_call" | custom-call | tf_op jit(solution)/shard_map/weight_back/pallas_call | solution.py:1171
  266.4 3.5 %split_sum.3 = (bf16[4,208,128]{2,1,0:T(8,128)(2,1)}, bf16[4,208,128]{2,1,0:T(8,128)(2,1)}, bf16[4,208,128]{2,1,0:T(8,128)(2,1)}, bf16[4,208,128]{2,1,0:T(8,128)(2,1)}) custom-call(s32[3]{0:T(128)} %pad_add_fusion.1.at_ref, bf16[4,4,208,128]{3,2,1,0:T(8,128)(2,1)} %get-tuple-element.178.keep_ref, bf16[4,4,208,128]{3,2,1,0:T(8,128)(2,1)} %copy-done.10), custom_call_target="tpu_custom_call" | custom-call | tf_op jit(solution)/shard_map/split_sum/pallas_call | solution.py:1031
  272.6 9.1 %collective-permute-done.30.two_ref = bf16[32,16,512]{2,1,0:T(8,128)(2,1)S(1)} collective-permute-done((bf16[32,16,512]{2,1,0:T(8,128)(2,1)S(1)}, bf16[32,16,512]{2,1,0:T(8,128)(2,1)S(1)}, u32[]{:S(2)}, u32[]{:S(2)}) %collective-permute-start.30) | collective-permute-done | bytes 524320 | tf_op jit(solution)/shard_map/ppermute | solution.py:1271
  283.9 8.8 %collective-permute-done.28.fe = bf16[16,1024]{1,0:T(8,128)(2,1)S(1)} collective-permute-done((bf16[16,1024]{1,0:T(8,128)(2,1)S(1)}, bf16[16,1024]{1,0:T(8,128)(2,1)S(1)}, u32[]{:S(2)}, u32[]{:S(2)}) %collective-permute-start.28) | collective-permute-done | bytes 32800 | tf_op jit(solution)/shard_map/ppermute | solution.py:1271
  310.1 3.3 %collective-permute-start.36 = (bf16[208,128]{1,0:T(8,128)(2,1)}, bf16[208,128]{1,0:T(8,128)(2,1)S(1)}, u32[]{:S(2)}, u32[]{:S(2)}) collective-permute-start(bf16[208,128]{1,0:T(8,128)(2,1)} %get-tuple-element.193), channel_id=1, source_target_pairs={{0,6},{1,7},{2,4},{3,5},{4,2},{5,3},{6,0},{7,1},{8,14},{9,15},{10,... | collective-permute-start | bytes 159752 | tf_op jit(solution)/shard_map/ppermute | solution.py:1271
  313.5 12.1 %finish.1 = f32[1536,512]{1,0:T(8,128)} custom-call(bf16[1536,512]{1,0:T(8,128)(2,1)} %bitcast.62, bf16[1536,256]{1,0:T(8,128)(2,1)} %get-tuple-element.147.ql_ref, bf16[1536,256]{1,0:T(8,128)(2,1)} %get-tuple-element.157.qh_ref, bf16[1536,512]{1,0:T(8,128)(2,1)} %get-tuple-element.158.kvl_ref, bf16[1536,512]{1,0:T(8,128)(2,1)} %get-tuple-element.159.kvh_ref, ...), custom_call_target="tpu_custom_call" | custom-call | tf_op jit(solution)/shard_map/finish/pallas_call | solution.py:1237
  (170 shorter events, 83.1 us)
Async XLA Ops:
  9.7 49.1 %collective-permute-start.8 = (bf16[1536,512]{1,0:T(8,128)(2,1)}, bf16[1536,512]{1,0:T(8,128)(2,1)S(1)}, u32[]{:S(2)}, u32[]{:S(2)}) collective-permute-start(bf16[1536,512]{1,0:T(8,128)(2,1)} %bitcast.57), channel_id=1, source_target_pairs={{0,8},{8,16},{16,24},{24,1},{1,9},{9,17},{17,25},{25,2},{2,10},{10... | collective-permute-start | bytes 4718600 | tf_op jit(solution)/shard_map/ppermute | solution.py:1271
  13.0 15.9 %collective-permute-start.5 = (bf16[4,208,128]{2,1,0:T(8,128)(2,1)S(1)}, bf16[4,208,128]{2,1,0:T(8,128)(2,1)S(1)}, u32[]{:S(2)}, u32[]{:S(2)}) collective-permute-start(bf16[4,208,128]{2,1,0:T(8,128)(2,1)S(1)} %get-tuple-element.213), channel_id=1, source_target_pairs={{0,6},{1,7},{2,4},{3,5},{4,2},{5,3},{6,0},{7,1},{8,14},{9,15},{10,... | collective-permute-start | bytes 638984 | tf_op jit(solution)/shard_map/ppermute | solution.py:1271
  14.7 16.7 %collective-permute-start.4 = (bf16[4,208,128]{2,1,0:T(8,128)(2,1)S(1)}, bf16[4,208,128]{2,1,0:T(8,128)(2,1)S(1)}, u32[]{:S(2)}, u32[]{:S(2)}) collective-permute-start(bf16[4,208,128]{2,1,0:T(8,128)(2,1)S(1)} %get-tuple-element.213), channel_id=1, source_target_pairs={{0,4},{1,5},{2,6},{3,7},{4,0},{5,1},{6,2},{7,3},{8,12},{9,13},{10,... | collective-permute-start | bytes 638984 | tf_op jit(solution)/shard_map/ppermute | solution.py:1271
  33.7 25.1 %collective-permute-start.7 = (bf16[512,512]{1,0:T(8,128)(2,1)}, bf16[512,512]{1,0:T(8,128)(2,1)}, u32[]{:S(2)}, u32[]{:S(2)}) collective-permute-start(bf16[512,512]{1,0:T(8,128)(2,1)} %slice.24), channel_id=1, source_target_pairs={{0,16},{8,24},{16,1},{24,9},{1,17},{9,25},{17,2},{25,10},{2,18},{1... | collective-permute-start | bytes 1572872 | tf_op jit(solution)/shard_map/ppermute | solution.py:1271
  35.9 43.9 %collective-permute-start.15 = (bf16[576,128]{1,0:T(8,128)(2,1)S(1)}, bf16[576,128]{1,0:T(8,128)(2,1)}, u32[]{:S(2)}, u32[]{:S(2)}) collective-permute-start(bf16[576,128]{1,0:T(8,128)(2,1)S(1)} %copy-done.21), channel_id=1, source_target_pairs={{0,6},{1,7},{2,4},{3,5},{4,2},{5,3},{6,0},{7,1},{8,14},{9,15},{10,... | collective-permute-start | bytes 442376 | tf_op jit(solution)/shard_map/ppermute | solution.py:1271
  36.4 45.3 %collective-permute-start.14 = (bf16[576,128]{1,0:T(8,128)(2,1)S(1)}, bf16[576,128]{1,0:T(8,128)(2,1)}, u32[]{:S(2)}, u32[]{:S(2)}) collective-permute-start(bf16[576,128]{1,0:T(8,128)(2,1)S(1)} %copy-done.21), channel_id=1, source_target_pairs={{0,4},{1,5},{2,6},{3,7},{4,0},{5,1},{6,2},{7,3},{8,12},{9,13},{10,... | collective-permute-start | bytes 442376 | tf_op jit(solution)/shard_map/ppermute | solution.py:1271
  59.9 33.7 %collective-permute-start.11 = (f32[48,1536]{1,0:T(8,128)}, f32[48,1536]{1,0:T(8,128)S(1)}, u32[]{:S(2)}, u32[]{:S(2)}) collective-permute-start(f32[48,1536]{1,0:T(8,128)} %get-tuple-element.124.c.pc), channel_id=1, source_target_pairs={{8,0},{16,8},{24,16},{1,24},{9,1},{17,9},{25,17},{2,25},{10,2},{18... | collective-permute-start | bytes 884744 | tf_op jit(solution)/shard_map/ppermute | solution.py:1271
  76.4 17.2 %collective-permute-start.10 = (f32[48,1536]{1,0:T(8,128)}, f32[48,1536]{1,0:T(8,128)S(1)}, u32[]{:S(2)}, u32[]{:S(2)}) collective-permute-start(f32[48,1536]{1,0:T(8,128)} %get-tuple-element.124.c.pc), channel_id=1, source_target_pairs={{0,8},{8,16},{16,24},{24,1},{1,9},{9,17},{17,25},{25,2},{2,10},{10... | collective-permute-start | bytes 884744 | tf_op jit(solution)/shard_map/ppermute | solution.py:1271
  94.9 28.9 %collective-permute-start.18 = (bf16[4,576,128]{2,1,0:T(8,128)(2,1)S(1)}, bf16[4,576,128]{2,1,0:T(8,128)(2,1)}, u32[]{:S(2)}, u32[]{:S(2)}) collective-permute-start(bf16[4,576,128]{2,1,0:T(8,128)(2,1)S(1)} %pad_maximum_fusion.2), channel_id=1, source_target_pairs={{0,24},{1,25},{2,26},{3,27},{4,28},{5,29},{6,30},{7,31},{8,16},{9,... | collective-permute-start | bytes 1769480 | tf_op jit(solution)/shard_map/ppermute | solution.py:1271
  95.0 28.8 %collective-permute-start.17 = (bf16[4,576,128]{2,1,0:T(8,128)(2,1)S(1)}, bf16[4,576,128]{2,1,0:T(8,128)(2,1)}, u32[]{:S(2)}, u32[]{:S(2)}) collective-permute-start(bf16[4,576,128]{2,1,0:T(8,128)(2,1)S(1)} %pad_maximum_fusion.2), channel_id=1, source_target_pairs={{0,16},{1,17},{2,18},{3,19},{4,20},{5,21},{6,22},{7,23},{8,24},{9,... | collective-permute-start | bytes 1769480 | tf_op jit(solution)/shard_map/ppermute | solution.py:1271
  95.6 28.3 %collective-permute-start.16 = (bf16[4,576,128]{2,1,0:T(8,128)(2,1)S(1)}, bf16[4,576,128]{2,1,0:T(8,128)(2,1)}, u32[]{:S(2)}, u32[]{:S(2)}) collective-permute-start(bf16[4,576,128]{2,1,0:T(8,128)(2,1)S(1)} %pad_maximum_fusion.2), channel_id=1, source_target_pairs={{0,8},{1,9},{2,10},{3,11},{4,12},{5,13},{6,14},{7,15},{8,0},{9,1},... | collective-permute-start | bytes 1769480 | tf_op jit(solution)/shard_map/ppermute | solution.py:1271
  196.6 36.0 %collective-permute-start.21 = (bf16[4,592,128]{2,1,0:T(8,128)(2,1)}, bf16[4,592,128]{2,1,0:T(8,128)(2,1)S(1)}, u32[]{:S(2)}, u32[]{:S(2)}) collective-permute-start(bf16[4,592,128]{2,1,0:T(8,128)(2,1)} %get-tuple-element.153), channel_id=1, source_target_pairs={{0,2},{1,3},{2,0},{3,1},{4,6},{5,7},{6,4},{7,5},{8,10},{9,11},{10,... | collective-permute-start | bytes 1818632 | tf_op jit(solution)/shard_map/ppermute | solution.py:1271
  197.6 42.7 %collective-permute-start.22 = (bf16[4,592,128]{2,1,0:T(8,128)(2,1)}, bf16[4,592,128]{2,1,0:T(8,128)(2,1)S(1)}, u32[]{:S(2)}, u32[]{:S(2)}) collective-permute-start(bf16[4,592,128]{2,1,0:T(8,128)(2,1)} %get-tuple-element.154), channel_id=1, source_target_pairs={{0,4},{1,5},{2,6},{3,7},{4,0},{5,1},{6,2},{7,3},{8,12},{9,13},{10,... | collective-permute-start | bytes 1818632 | tf_op jit(solution)/shard_map/ppermute | solution.py:1271
  200.0 53.1 %collective-permute-start.23 = (bf16[4,592,128]{2,1,0:T(8,128)(2,1)}, bf16[4,592,128]{2,1,0:T(8,128)(2,1)S(1)}, u32[]{:S(2)}, u32[]{:S(2)}) collective-permute-start(bf16[4,592,128]{2,1,0:T(8,128)(2,1)} %get-tuple-element.155), channel_id=1, source_target_pairs={{0,6},{1,7},{2,4},{3,5},{4,2},{5,3},{6,0},{7,1},{8,14},{9,15},{10,... | collective-permute-start | bytes 1818632 | tf_op jit(solution)/shard_map/ppermute | solution.py:1271
  221.4 88.5 %collective-permute-start.29 = (bf16[32,48,512]{2,1,0:T(8,128)(2,1)}, bf16[32,48,512]{2,1,0:T(8,128)(2,1)S(1)}, u32[]{:S(2)}, u32[]{:S(2)}) collective-permute-start(bf16[32,48,512]{2,1,0:T(8,128)(2,1)} %get-tuple-element.167), channel_id=1, source_target_pairs={{8,0},{16,8},{24,16},{1,24},{9,1},{17,9},{25,17},{2,25},{10,2},{18... | collective-permute-start | bytes 4718600 | tf_op jit(solution)/shard_map/ppermute | solution.py:1271
  262.9 18.8 %collective-permute-start.30 = (bf16[32,16,512]{2,1,0:T(8,128)(2,1)S(1)}, bf16[32,16,512]{2,1,0:T(8,128)(2,1)S(1)}, u32[]{:S(2)}, u32[]{:S(2)}) collective-permute-start(bf16[32,16,512]{2,1,0:T(8,128)(2,1)S(1)} %copy-done.31), channel_id=1, source_target_pairs={{16,0},{24,8},{1,16},{9,24},{17,1},{25,9},{2,17},{10,25},{18,2},{2... | collective-permute-start | bytes 1572872 | tf_op jit(solution)/shard_map/ppermute | solution.py:1271
  272.3 29.2 %collective-permute-start.31 = (bf16[4,208,128]{2,1,0:T(8,128)(2,1)}, bf16[4,208,128]{2,1,0:T(8,128)(2,1)S(1)}, u32[]{:S(2)}, u32[]{:S(2)}) collective-permute-start(bf16[4,208,128]{2,1,0:T(8,128)(2,1)} %get-tuple-element.187), channel_id=1, source_target_pairs={{0,8},{1,9},{2,10},{3,11},{4,12},{5,13},{6,14},{7,15},{8,0},{9,1},... | collective-permute-start | bytes 638984 | tf_op jit(solution)/shard_map/ppermute | solution.py:1271
  272.5 31.0 %collective-permute-start.32 = (bf16[4,208,128]{2,1,0:T(8,128)(2,1)}, bf16[4,208,128]{2,1,0:T(8,128)(2,1)S(1)}, u32[]{:S(2)}, u32[]{:S(2)}) collective-permute-start(bf16[4,208,128]{2,1,0:T(8,128)(2,1)} %get-tuple-element.188), channel_id=1, source_target_pairs={{0,16},{1,17},{2,18},{3,19},{4,20},{5,21},{6,22},{7,23},{8,24},{9,... | collective-permute-start | bytes 638984 | tf_op jit(solution)/shard_map/ppermute | solution.py:1271
  281.7 23.9 %collective-permute-start.33 = (bf16[4,208,128]{2,1,0:T(8,128)(2,1)}, bf16[4,208,128]{2,1,0:T(8,128)(2,1)S(1)}, u32[]{:S(2)}, u32[]{:S(2)}) collective-permute-start(bf16[4,208,128]{2,1,0:T(8,128)(2,1)} %get-tuple-element.189), channel_id=1, source_target_pairs={{0,24},{1,25},{2,26},{3,27},{4,28},{5,29},{6,30},{7,31},{8,16},{9,... | collective-permute-start | bytes 638984 | tf_op jit(solution)/shard_map/ppermute | solution.py:1271
  303.5 22.1 %collective-permute-start.38 = (bf16[592,128]{1,0:T(8,128)(2,1)}, bf16[592,128]{1,0:T(8,128)(2,1)S(1)}, u32[]{:S(2)}, u32[]{:S(2)}) collective-permute-start(bf16[592,128]{1,0:T(8,128)(2,1)} %get-tuple-element.202), channel_id=1, source_target_pairs={{0,16},{1,17},{2,18},{3,19},{4,20},{5,21},{6,22},{7,23},{8,24},{9,... | collective-permute-start | bytes 454664 | tf_op jit(solution)/shard_map/ppermute | solution.py:1271
  305.6 20.1 %collective-permute-start.39 = (bf16[592,128]{1,0:T(8,128)(2,1)}, bf16[592,128]{1,0:T(8,128)(2,1)S(1)}, u32[]{:S(2)}, u32[]{:S(2)}) collective-permute-start(bf16[592,128]{1,0:T(8,128)(2,1)} %get-tuple-element.203), channel_id=1, source_target_pairs={{0,24},{1,25},{2,26},{3,27},{4,28},{5,29},{6,30},{7,31},{8,16},{9,... | collective-permute-start | bytes 454664 | tf_op jit(solution)/shard_map/ppermute | solution.py:1271
  309.9 18.3 %collective-permute-start.34 = (bf16[208,128]{1,0:T(8,128)(2,1)}, bf16[208,128]{1,0:T(8,128)(2,1)S(1)}, u32[]{:S(2)}, u32[]{:S(2)}) collective-permute-start(bf16[208,128]{1,0:T(8,128)(2,1)} %get-tuple-element.191), channel_id=1, source_target_pairs={{0,2},{1,3},{2,0},{3,1},{4,6},{5,7},{6,4},{7,5},{8,10},{9,11},{10,... | collective-permute-start | bytes 159752 | tf_op jit(solution)/shard_map/ppermute | solution.py:1271
  310.0 18.3 %collective-permute-start.35 = (bf16[208,128]{1,0:T(8,128)(2,1)}, bf16[208,128]{1,0:T(8,128)(2,1)S(1)}, u32[]{:S(2)}, u32[]{:S(2)}) collective-permute-start(bf16[208,128]{1,0:T(8,128)(2,1)} %get-tuple-element.192), channel_id=1, source_target_pairs={{0,4},{1,5},{2,6},{3,7},{4,0},{5,1},{6,2},{7,3},{8,12},{9,13},{10,... | collective-permute-start | bytes 159752 | tf_op jit(solution)/shard_map/ppermute | solution.py:1271
  310.1 18.2 %collective-permute-start.36 = (bf16[208,128]{1,0:T(8,128)(2,1)}, bf16[208,128]{1,0:T(8,128)(2,1)S(1)}, u32[]{:S(2)}, u32[]{:S(2)}) collective-permute-start(bf16[208,128]{1,0:T(8,128)(2,1)} %get-tuple-element.193), channel_id=1, source_target_pairs={{0,6},{1,7},{2,4},{3,5},{4,2},{5,3},{6,0},{7,1},{8,14},{9,15},{10,... | collective-permute-start | bytes 159752 | tf_op jit(solution)/shard_map/ppermute | solution.py:1271
  (52 other events, 705.5 us)
where the time goes:
time: 334 us; the launch traced here: 330 us
  Pallas kernels  169 us (51%)
  starting transfers between devices  72.7 us (22%)
  waiting for transfers between devices  71.9 us (22%)
  local copies, waits for them, and re-layouts  9.67 us (3%)
  other arithmetic  6.18 us (2%)
    ppermute x40, starting transfers between devices, send(): return lax.ppermute(value, ('head', 'plane', 'core'), pairs)  72.7 us
    ppermute x40, waiting for transfers between devices, send(): return lax.ppermute(value, ('head', 'plane', 'core'), pairs)  71.9 us
    pallas_call x1, Pallas kernels, feed_fast(): pl.pallas_call(feed_fast_kernel, grid=(tok // tile,), in_specs=[SMEM, til...  38.4 us
    pallas_call x2, Pallas kernels, attend_back(): pl.pallas_call(attend_back_kernel, grid=(pairs,), in_specs=[pl.BlockSpec(...  25.5 us
    pallas_call x1, Pallas kernels, sink_forward(): pl.pallas_call(functools.partial(sink_forward_kernel, own, context), in_s...  12.5 us
    pallas_call x1, Pallas kernels, attend(): pl.pallas_call(attend_kernel, grid=(PAIRS,), in_specs=[pl.BlockSpec((tok,...  12.3 us
    pallas_call x1, Pallas kernels, finish(): pl.pallas_call(functools.partial(finish_kernel, skip), grid=(tok // tile,...  12.1 us
    pallas_call x1, Pallas kernels, context_project(): pl.pallas_call(functools.partial(context_kernel, halo_blocks), grid=(BLOC...  11.2 us
  transfers between devices with their start and end apart: 40, of which 16 were waited for; matrix products, arithmetic and copies ran while one was open for 2% of the time, Pallas kernels for 37%

commit v1 on v0

--- a/solution.py
+++ b/solution.py
@@ -168,7 +168,7 @@
 
 def sink_backward_kernel(
     own, context, a, b, c, d, e, w_ref, kept_ref, scale_ref, proj, gl_ref, gh_ref,
-    gm_ref, gw_ref, sa, sb, sd, se, q_ref, k_ref, vals, gq, gk, kept, sems,
+    gm_ref, gw_ref, sd, se, q_ref, k_ref, vals, gq, gk, kept, sems,
 ):
     window = q_ref.shape[1]
     fold = window - LANES
@@ -196,10 +196,11 @@
         @pl.when(turn == 0)
         def _():
             for head in range(HEADS):
-                ref = gl_ref if head < HEADS // 2 else gh_ref
+                low = gl_ref.shape[0]
+                ref, index = (gl_ref, head) if head < low else (gh_ref, head - low)
                 vals[head, : context - own, :] = jnp.zeros((context - own, LANES), F32)
                 vals[head, context - own : context, :] = (
-                    ref[head % (HEADS // 2)]
+                    ref[index]
                     * kept[SINK_ITERS - 1, head, context - own : context, :]
                     * scale_ref[SINK_ITERS - 1, head, 2:3, :]
                 )
@@ -252,11 +253,8 @@
     for pair in range(PAIRS):
         gm_ref[:, pair * LANES : (pair + 1) * LANES] = gq[pair]
         gm_ref[:, D + pair * LANES : D + (pair + 1) * LANES] = gk[pair]
-    at = 0
-    for piece, ref in ((a, sa), (b, sb), (c, None), (d, sd), (e, se)):
-        if ref is not None:
-            ref[...] = gm_ref[at : at + piece.shape[0], :].astype(BF16)
-        at += piece.shape[0]
+    sd[...] = gm_ref[context : context + d.shape[0], :].astype(BF16)
+    se[...] = gm_ref[context + d.shape[0] :, :].astype(BF16)
 
 
 HBM = pl.BlockSpec(memory_space=pl.ANY)
@@ -300,7 +298,7 @@
             jax.ShapeDtypeStruct((PAIRS, HEAD_DIM, LANES), F32),
             *(
                 jax.ShapeDtypeStruct((pieces[i].shape[0], 2 * D), BF16)
-                for i in (0, 1, 3, 4)
+                for i in (3, 4)
             ),
         ],
         scratch_shapes=[
@@ -322,8 +320,9 @@
     return centre * lax.rsqrt(spread + EPSILON)
 
 
-def context_kernel(halo_blocks, far_ref, near_ref, x_ref, gain_ref, w_ref, kvx_ref, nh_ref):
-    x = jnp.concatenate([far_ref[...], near_ref[...], x_ref[...]], axis=0)
+def context_kernel(count, keep, *refs):
+    gain_ref, w_ref, kvx_ref = refs[count : count + 3]
+    x = jnp.concatenate([ref[...] for ref in refs[:count]], axis=0)
     blocks = x.shape[0]
     normed = normalise(x.astype(F32)) * gain_ref[...].reshape(1, 1, D)
     normed = normed.astype(BF16).reshape(blocks * 8, D)
@@ -336,7 +335,8 @@
     rows = []
     for b in range(8):
         part = jnp.concatenate([part[b * 16 : (b + 1) * 16] for part in turned], axis=0)
-        nh_ref[b] = part[:halo_blocks]
+        if keep:
+            refs[count + 3][b] = part
         rows.append(part)
     rows = jnp.concatenate(rows, axis=0)
     for head in range(0, HEADS, 2):
@@ -348,29 +348,29 @@
                 ]
 
 
-def context_project(far, near, x, gain, w_kv):
-    halo_blocks = far.shape[0] + near.shape[0]
-    blocks = halo_blocks + x.shape[0]
+def context_project(values, gain, w_kv, keep):
+    blocks = sum(v.shape[0] for v in values)
+    outs = 2 if keep else 1
     return pl.pallas_call(
-        functools.partial(context_kernel, halo_blocks),
+        functools.partial(context_kernel, len(values), keep),
         grid=(BLOCK // 8,),
         in_specs=[
-            *(pl.BlockSpec((v.shape[0], 8, D), lambda i: (0, i, 0)) for v in (far, near, x)),
+            *(pl.BlockSpec((v.shape[0], 8, D), lambda i: (0, i, 0)) for v in values),
             pl.BlockSpec((1, D), lambda i: (0, 0)),
             pl.BlockSpec((2 * D, D), lambda i: (0, 0)),
         ],
         out_specs=[
             pl.BlockSpec((HEADS, blocks, 8 * LANES), lambda i: (0, 0, i)),
-            pl.BlockSpec((8, halo_blocks, D), lambda i: (i, 0, 0)),
-        ],
+            pl.BlockSpec((8, blocks, D), lambda i: (i, 0, 0)),
+        ][:outs],
         out_shape=[
             jax.ShapeDtypeStruct((HEADS, blocks, BLOCK * LANES), BF16),
-            jax.ShapeDtypeStruct((BLOCK, halo_blocks, D), BF16),
-        ],
+            jax.ShapeDtypeStruct((BLOCK, blocks, D), BF16),
+        ][:outs],
         cost_estimate=CHEAP,
         compiler_params=vmem(),
-        name="context_project",
-    )(far, near, x, gain, w_kv)
+        name="context_halo" if keep else "context_own",
+    )(*values, gain, w_kv)
 
 
 def compact(values, lane_block):
@@ -404,14 +404,17 @@
     return (lane < HEAD_DIM) if first else (lane >= HEAD_DIM)
 
 
-def attend_kernel(q_ref, kv_ref, kvx_ref, plan_ref, live_ref, att_ref, skv_ref, even_ref, odd_ref):
+def attend_kernel(
+    q_ref, kv_ref, kvh_ref, kvo_ref, plan_ref, live_ref, att_ref, skv_ref, even_ref, odd_ref
+):
     own = plan_ref.shape[1]
-    blocks = kvx_ref.shape[1]
+    blocks = kvh_ref.shape[1] + own
     held = (even_ref, odd_ref)
     for e in range(2):
         plan = plan_ref[e][:, :blocks]
         for chunk in range(4):
-            out = mm(plan, kvx_ref[e, :, chunk * 8 * LANES : (chunk + 1) * 8 * LANES])
+            lanes = slice(chunk * 8 * LANES, (chunk + 1) * 8 * LANES)
+            out = mm(plan, jnp.concatenate([kvh_ref[e, :, lanes], kvo_ref[e, :, lanes]], axis=0))
             for b in range(8):
                 at = (chunk * 8 + b) * (own + 1)
                 held[e][at : at + own, :] = out[:, b * LANES : (b + 1) * LANES]
@@ -453,15 +456,16 @@
     lax.fori_loop(0, own // 4 // GROUPS, group, 0)
 
 
-def attend(q, kv, kvx, plan, live):
-    tok, own, blocks = q.shape[0], plan.shape[1], kvx.shape[1]
+def attend(q, kv, kvh, kvo, plan, live):
+    tok, own, halo = q.shape[0], plan.shape[1], kvh.shape[1]
     return pl.pallas_call(
         attend_kernel,
         grid=(PAIRS,),
         in_specs=[
             pl.BlockSpec((tok, LANES), lambda j: (0, j)),
             pl.BlockSpec((tok, 2 * LANES), lambda j: (0, j)),
-            pl.BlockSpec((2, blocks, BLOCK * LANES), lambda j: (j, 0, 0)),
+            pl.BlockSpec((2, halo, BLOCK * LANES), lambda j: (j, 0, 0)),
+            pl.BlockSpec((2, own, BLOCK * LANES), lambda j: (j, 0, 0)),
             pl.BlockSpec((2, own, LANES), lambda j: (j, 0, 0)),
             pl.BlockSpec((tok // LANES, LANES), lambda j: (0, 0)),
         ],
@@ -477,16 +481,16 @@
         cost_estimate=CHEAP,
         compiler_params=vmem(),
         name="attend",
-    )(q, kv, kvx, plan, live)
+    )(q, kv, kvh, kvo, plan, live)
 
 
 def attend_back_kernel(
-    q_ref, kv_ref, skv_ref, go_ref, kvx_ref, plan_ref, live_ref,
+    q_ref, kv_ref, skv_ref, go_ref, kvh_ref, kvo_ref, plan_ref, live_ref,
     gq_ref, gkv_ref, gh_ref, gp_ref, even_ref, odd_ref, leven_ref, lodd_ref,
 ):
     own = plan_ref.shape[1]
-    blocks = kvx_ref.shape[1]
-    halo = blocks - own
+    halo = kvh_ref.shape[1]
+    blocks = halo + own
     held = (even_ref, odd_ref)
     lheld = (leven_ref, lodd_ref)
     lane_block = lax.broadcasted_iota(jnp.int32, (BLOCK, LANES), 1) // BLOCK
@@ -552,7 +556,8 @@
                 ],
                 axis=1,
             ).astype(BF16)
-            gplan = gplan + mm(grads, kvx_ref[e, :, lanes], NT)
+            here = jnp.concatenate([kvh_ref[e, :, lanes], kvo_ref[e, :, lanes]], axis=0)
+            gplan = gplan + mm(grads, here, NT)
             gcontext = mm(plan, grads, TN)
             gh_ref[e, :, lanes] = gcontext[:halo].astype(BF16)
             for b in range(8):
@@ -574,9 +579,8 @@
     lax.fori_loop(0, own // 4, finish, 0)
 
 
-def attend_back(q, kv, skv, go, kvx, plan, live, first, pairs):
-    tok, own, blocks = q.shape[0], plan.shape[1], kvx.shape[1]
-    halo = blocks - own
+def attend_back(q, kv, skv, go, kvh, kvo, plan, live, first, pairs):
+    tok, own, halo = q.shape[0], plan.shape[1], kvh.shape[1]
     return pl.pallas_call(
         attend_back_kernel,
         grid=(pairs,),
@@ -585,7 +589,8 @@
             pl.BlockSpec((tok, 2 * LANES), lambda j: (0, j + first)),
             pl.BlockSpec((tok, 2 * LANES), lambda j: (0, j + first)),
             pl.BlockSpec((tok, LANES), lambda j: (0, j + first)),
-            pl.BlockSpec((2, blocks, BLOCK * LANES), lambda j: (j + first, 0, 0)),
+            pl.BlockSpec((2, halo, BLOCK * LANES), lambda j: (j + first, 0, 0)),
+            pl.BlockSpec((2, own, BLOCK * LANES), lambda j: (j + first, 0, 0)),
             pl.BlockSpec((2, own, LANES), lambda j: (j + first, 0, 0)),
             pl.BlockSpec((tok // LANES, LANES), lambda j: (0, 0)),
         ],
@@ -605,16 +610,20 @@
         cost_estimate=CHEAP,
         compiler_params=vmem(),
         name="attend_back",
-    )(q, kv, skv, go, kvx, plan, live)
-
-
-def halo_kernel(low_ref, high_ref, nh_ref, w_ref, far_ref, near_ref, gw_ref):
+    )(q, kv, skv, go, kvh, kvo, plan, live)
+
+
+def halo_kernel(
+    low_ref, high_ref, nh_ref, wq_ref, w_ref, gm_ref, far_ref, near_ref, gw_ref, block_ref
+):
     halo = low_ref.shape[1]
     far = far_ref.shape[1]
 
     @pl.when(pl.program_id(0) == 0)
     def _():
         gw_ref[...] = jnp.zeros_like(gw_ref)
+        grads = gm_ref[...].astype(BF16)
+        block_ref[...] = mm(grads[:, :D], wq_ref[...]) + mm(widen_keys(grads[:, D:]), w_ref[...])
 
     rows = jnp.concatenate(
         [
@@ -630,23 +639,25 @@
         ],
         axis=0,
     )
-    out = mm(rows, w_ref[...]).astype(BF16).reshape(8, halo, D)
+    out = (mm(rows, w_ref[...]).reshape(8, halo, D) + block_ref[...][None]).astype(BF16)
     far_ref[...] = out[:, :far]
     near_ref[...] = out[:, far:]
     gw_ref[...] += mm(rows, nh_ref[...].reshape(8 * halo, D), TN)
 
 
-def halo_back(low, high, nh, w_kv, far):
+def halo_back(low, high, nh, w_q, w_kv, gm, far):
     halo = low.shape[1]
-    half = pl.BlockSpec((HEADS // 2, halo, 8 * LANES), lambda i: (0, 0, i))
+    part = lambda v: pl.BlockSpec((v.shape[0], halo, 8 * LANES), lambda i: (0, 0, i))
     return pl.pallas_call(
         halo_kernel,
         grid=(BLOCK // 8,),
         in_specs=[
-            half,
-            half,
+            part(low),
+            part(high),
             pl.BlockSpec((8, halo, D), lambda i: (i, 0, 0)),
-            pl.BlockSpec((2 * D, D), lambda i: (0, 0)),
+            once((D, D)),
+            once((2 * D, D)),
+            once((halo, 2 * D)),
         ],
         out_specs=[
             pl.BlockSpec((8, far, D), lambda i: (i, 0, 0)),
@@ -658,10 +669,11 @@
             jax.ShapeDtypeStruct((BLOCK, halo - far, D), BF16),
             jax.ShapeDtypeStruct((2 * D, D), F32),
         ],
+        scratch_shapes=[pltpu.VMEM((halo, D), F32)],
         cost_estimate=CHEAP,
         compiler_params=vmem(),
         name="halo_back",
-    )(low, high, nh, w_kv)
+    )(low, high, nh, w_q, w_kv, gm)
 
 
 def project_kernel(x_ref, gain_ref, wq_ref, wkv_ref, n_ref, q_ref, kv_ref, m_ref, head_ref, tail_ref):
@@ -739,7 +751,11 @@
     return mm(jnp.broadcast_to(vector.astype(F32), (16, size)).astype(BF16), pick)
 
 
-def pack_kernel(wqkv_ref, wsort_ref, g1, bo, g2, bi, bd, win_ref, wdown_ref, wout_ref, one_ref, two_ref):
+def pack_kernel(
+    wqkv_ref, wsort_ref, g1, bo, g2, bi, bd, win_ref, wdown_ref, wout_ref, x_ref,
+    one_ref, two_ref, tail_ref,
+):
+    tail_ref[...] = x_ref[...]
     one_ref[:192, :] = wqkv_ref[...]
     row = place(g1[...], 0) + place(bo[...], 16) + place(g2[...], 32)
     row = row + place(bi[...], 48) + place(bd[...], 112)
@@ -750,17 +766,21 @@
     two_ref[512:, :] = wout_ref[...]
 
 
-def pack(w_qkv, w_sort, vectors, w_in, w_down, w_out):
+def pack(w_qkv, w_sort, vectors, w_in, w_down, w_out, x, tail):
+    last = x.shape[0] // tail - 1
     return pl.pallas_call(
         pack_kernel,
+        grid=(1,),
+        in_specs=[VMEM] * 10 + [pl.BlockSpec((tail, D), lambda i: (last, 0))],
         out_shape=[
             jax.ShapeDtypeStruct((PIECE_ONE, LANES), BF16),
             jax.ShapeDtypeStruct((PIECE_TWO, LANES), BF16),
+            jax.ShapeDtypeStruct((tail, D), BF16),
         ],
         cost_estimate=CHEAP,
         compiler_params=vmem(),
         name="pack",
-    )(w_qkv.T, w_sort.T, *(v.reshape(1, -1) for v in vectors), w_in, w_down.T, w_out.T)
+    )(w_qkv.T, w_sort.T, *(v.reshape(1, -1) for v in vectors), w_in, w_down.T, w_out.T, x)
 
 
 def rows_at(start, size):
@@ -781,7 +801,7 @@
 def each_piece(at_ref, mine_ref, other_ref, visit):
     def owner(own, h, z, b, c):
         source = mine_ref if own else other_ref
-        visit(h, b, c, source.at[at_ref[1] ^ z, at_ref[0] ^ h])
+        visit(h, b, c, source.at[at_ref[0] ^ h, at_ref[1] ^ z])
 
     each_owner(at_ref, owner)
 
@@ -929,17 +949,17 @@
         def owner(own, h, z, b, c):
             ref = keep_ref if own else send_ref
             for k in range(2):
-                ref[z, h, k * LANES : (k + 1) * LANES, :] = acc_in[
+                ref[h, z, k * LANES : (k + 1) * LANES, :] = acc_in[
                     b, h * LANES : (h + 1) * LANES, k * LANES : (k + 1) * LANES
                 ].astype(BF16)
             for k in range(4):
-                ref[z, h, 256 + k * 64 : 320 + k * 64, :] = acc_down[
+                ref[h, z, 256 + k * 64 : 320 + k * 64, :] = acc_down[
                     rows_at(b, 64), h * 512 + k * LANES : h * 512 + (k + 1) * LANES
                 ].astype(BF16)
-            ref[z, h, 512:576, :] = acc_out[
+            ref[h, z, 512:576, :] = acc_out[
                 rows_at(b, 64), h * LANES : (h + 1) * LANES
             ].astype(BF16)
-            ref[z, h, 576:592, :] = jnp.broadcast_to(
+            ref[h, z, 576:592, :] = jnp.broadcast_to(
                 vecs[pl.ds(h * 8 + b, 1), :], (16, LANES)
             ).astype(BF16)
 
@@ -1131,9 +1151,11 @@
         acc_kv[...] = halo_ref[...] + mm(widen_keys(grads[:, D:]), means, TN)
 
     normed = n_ref[...]
-    for i, (q_ref, kv_ref) in enumerate(((ql_ref, kvl_ref), (qh_ref, kvh_ref))):
-        acc_q[i * 256 : (i + 1) * 256, :] += mm(q_ref[...].T, normed)
-        acc_kv[i * 512 : (i + 1) * 512, :] += mm(kv_ref[...].T, normed)
+    cut = ql_ref.shape[1]
+    for lo, q_ref, kv_ref in ((0, ql_ref, kvl_ref), (cut, qh_ref, kvh_ref)):
+        hi = lo + q_ref.shape[1]
+        acc_q[lo:hi, :] += mm(q_ref[...].T, normed)
+        acc_kv[2 * lo : 2 * hi, :] += mm(kv_ref[...].T, normed)
 
     @pl.when(pl.program_id(0) == pl.num_programs(0) - 1)
     def _():
@@ -1148,13 +1170,13 @@
         def owner(own, h, z, b, c):
             ref = keep_ref if own else send_ref
             lanes = slice(h * LANES, (h + 1) * LANES)
-            ref[h, z, :64, :] = acc_q[rows_at(b, 64), lanes].astype(BF16)
-            ref[h, z, 64:128, :] = acc_kv[rows_at(2 * b + c, 64), lanes].astype(BF16)
-            ref[h, z, 128:192, :] = acc_kv[rows_at(2 * b + 1 - c, 64), lanes].astype(BF16)
+            ref[z, h, :64, :] = acc_q[rows_at(b, 64), lanes].astype(BF16)
+            ref[z, h, 64:128, :] = acc_kv[rows_at(2 * b + c, 64), lanes].astype(BF16)
+            ref[z, h, 128:192, :] = acc_kv[rows_at(2 * b + 1 - c, 64), lanes].astype(BF16)
             share = pltpu.roll(
                 jnp.broadcast_to(gain[:, lanes], (8, LANES)), lax.rem(LANES - 16 * b, LANES), 1
             )
-            ref[h, z, 192:208, :] = jnp.concatenate(
+            ref[z, h, 192:208, :] = jnp.concatenate(
                 [gs_ref[h, rows_at(b, 8), :], share], axis=0
             ).astype(BF16)
 
@@ -1172,7 +1194,7 @@
         functools.partial(weight_kernel, fast),
         grid=(tok // tile,),
         in_specs=[
-            SMEM, rows(D // 2), rows(D // 2), rows(D), rows(D), rows(D), once((D, D)),
+            SMEM, *(rows(v.shape[1]) for v in (*gq, *gkv)), rows(D), once((D, D)),
             once((2 * D, D)), once(gm.shape), *(once(p.shape) for p in pieces),
             once((2 * D, D)), once((1, D)), once(gsort.shape),
         ],
@@ -1189,7 +1211,7 @@
 
 
 def finish_kernel(
-    skip, x_ref, ql_ref, qh_ref, kvl_ref, kvh_ref, wq_ref, wkv_ref, gm_ref, fa, fb, fd, fe,
+    skip, x_ref, ql_ref, qh_ref, kvl_ref, kvh_ref, wq_ref, wkv_ref, gm_ref, fd, fe,
     one_ref, two_ref, g_ref, gain_ref, out_ref, total, blocks_ref,
 ):
     rows = x_ref.shape[0]
@@ -1197,18 +1219,19 @@
 
     @pl.when(pl.program_id(0) == 0)
     def _():
-        own, ends = fb.shape[0], fa.shape[0]
+        own, ends = fd.shape[0], fe.shape[0]
         halo = own + ends
-        blocks_ref[...] = gm_ref[halo : halo + own, :] + fb[...].astype(F32) + fd[...].astype(F32)
-        blocks_ref[own - ends :, :] += fa[...].astype(F32)
+        blocks_ref[...] = gm_ref[halo : halo + own, :] + fd[...].astype(F32)
         blocks_ref[:ends, :] += fe[...].astype(F32)
 
     at = lax.broadcasted_iota(jnp.int32, (rows, rows), 0)
     lane = lax.broadcasted_iota(jnp.int32, (rows, rows), 1)
     order = (lane == lax.rem(at, BLOCK) * 8 + at // BLOCK).astype(F32).astype(BF16)
     value = mm(order, one_ref[...].reshape(rows, D))
-    value = value + mm(ql_ref[...], wq_ref[: D // 2, :]) + mm(qh_ref[...], wq_ref[D // 2 :, :])
-    value = value + mm(kvl_ref[...], wkv_ref[:D, :]) + mm(kvh_ref[...], wkv_ref[D:, :])
+    cut = ql_ref.shape[1]
+    value = value + mm(ql_ref[...], wq_ref[:cut, :]) + mm(qh_ref[...], wq_ref[cut:, :])
+    value = value + mm(kvl_ref[...], wkv_ref[: 2 * cut, :])
+    value = value + mm(kvh_ref[...], wkv_ref[2 * cut :, :])
     grads = blocks_ref[pl.ds(pl.multiple_of(pl.program_id(0) * per, per), per), :].astype(BF16)
     block = mm(grads[:, :D], wq_ref[...]) + mm(widen_keys(grads[:, D:]), wkv_ref[...])
     value = value + jnp.broadcast_to(block[:, None, :], (per, BLOCK, D)).reshape(rows, D)
@@ -1238,7 +1261,7 @@
         functools.partial(finish_kernel, skip),
         grid=(tok // tile,),
         in_specs=[
-            rows(D), rows(D // 2), rows(D // 2), rows(D), rows(D), once((D, D)), once((2 * D, D)),
+            rows(D), *(rows(v.shape[1]) for v in (*gq, *gkv)), once((D, D)), once((2 * D, D)),
             once(gm.shape), *(once(f.shape) for f in far),
             pl.BlockSpec((BLOCK, 8, D), lambda i: (0, i, 0)),
             pl.BlockSpec((BLOCK, 8, D), lambda i: (0, jnp.maximum(i - skip, 0), 0)),
@@ -1489,29 +1512,33 @@
     parameters = (w_qkv, w_sort, w_in, w_down, w_out)
 
     three = range(1, 4)
+    tail = second * BLOCK
     if fast:
-        one, two = pack(w_qkv, w_sort, vectors, w_in, w_down, w_out)
-        ones = [one] + [grid.send(one, grid.swap_head(r)) for r in three]
-        x_send = after(x, *ones)
+        one, two, x_tail = pack(w_qkv, w_sort, vectors, w_in, w_down, w_out, x, tail)
+        ones = [one] + [grid.send(one, grid.swap_plane(r)) for r in three]
         ones = jnp.stack(ones)
-        ones = [ones] + [grid.send(ones, grid.swap_plane(r)) for r in three]
+        ones = [ones] + [grid.send(ones, grid.swap_head(r)) for r in three]
+        x_send, x_tail = lax.optimization_barrier((x, x_tail, *ones))[:2]
     else:
-        x_send = x
+        x_send, x_tail = x, x[tok - tail :]
     halo_one = grid.send(x_send, grid.along(1))
-    halo_two = grid.send(x_send[tok - second * BLOCK :], grid.along(2))
+    halo_two = grid.send(x_tail, grid.along(2))
     if fast:
-        two = after(two, *ones)
         ones = jnp.stack(ones)
         other = grid.send(ones, grid.swap_core())
+        two = after(two, other)
         twos = [two] + [grid.send(two, grid.swap_plane(r)) for r in three]
         wt_q, wt_kv, w_pairs, *rows = assemble(at, ones, other)
     else:
         wt_q, wt_kv, w_pairs, rows, feed_weights = weights_slow(grid, vectors, parameters)
+        twos = []
     gain_one, bias_out, gain_two, bias_in, bias_down = rows
 
     normed, q, kv, means, means_head, means_tail = project(x, gain_one, wt_q, wt_kv, second)
+    blocked = lambda value: value.reshape(-1, BLOCK, D)
+    (kv_own,) = context_project((blocked(x),), after(gain_one, means), wt_kv, False)
     means_send, means_head, means_tail = lax.optimization_barrier(
-        (means, means_head, means_tail, halo_one, halo_two)
+        (means, means_head, means_tail, halo_one, halo_two, kv_own, *twos)
     )[:3]
     pieces = (
         grid.send(means_tail, grid.along(2)),
@@ -1520,12 +1547,11 @@
         grid.send(means_send, grid.along(-1)),
         grid.send(means_head, grid.along(-2)),
     )
-    blocked = lambda value: value.reshape(-1, BLOCK, D)
-    kvx, normed_halo = context_project(
-        blocked(halo_two), blocked(halo_one), blocked(x), gain_one, wt_kv
+    kv_halo, normed_halo = context_project(
+        (blocked(halo_two), blocked(halo_one)), after(gain_one, kv_own), wt_kv, True
     )
     if fast:
-        twos = jnp.stack(lax.optimization_barrier((*twos, *pieces))[:4])
+        twos = jnp.stack(lax.optimization_barrier((*twos, *pieces, kv_halo))[:4])
         twos = [twos] + [grid.send(twos, grid.swap_head(r)) for r in three]
 
     begin = grid.place * own
@@ -1542,11 +1568,11 @@
     live = (doc[HALO:context] == doc[HALO - 1 : context - 1]) & (doc[HALO:context] >= 0)
     live = jnp.repeat(live.astype(F32), BLOCK).reshape(tok // LANES, LANES)
 
-    plan, *kept = sink_forward(pieces, after(w_pairs, kvx), docn, docc, own, context)
+    plan, *kept = sink_forward(pieces, after(w_pairs, kv_halo), docn, docc, own, context)
+    attended, skv = attend(q, kv, kv_halo, kv_own, plan, live)
     if fast:
-        twos = jnp.stack(lax.optimization_barrier((*twos, plan))[:4], axis=1)
+        twos = jnp.stack(lax.optimization_barrier((*twos, attended))[:4])
         feed_weights = (twos, grid.send(twos, grid.swap_core()))
-    attended, skv = attend(q, kv, kvx, plan, live)
 
     if fast:
         output, g_middle, g_att, keep, send = feed_fast(
@@ -1560,45 +1586,49 @@
         g_in, g_down, g_out, g_b_out, g_gain_two, g_b_in, g_b_down = gradients_two_slow(
             grid, *sums, parameters, vectors
         )
+        twos = []
 
     gq_low, gkv_low, gh_low, gplan_low = attend_back(
-        q, kv, skv, g_att, kvx, plan, live, 0, PAIRS // 2
+        q, kv, skv, g_att, kv_halo, kv_own, plan, live, 0, 1
     )
     if fast:
-        twos = split_sum(at, 1, after(keep, gh_low), got)
+        twos = split_sum(at, 0, after(keep, gh_low), got)
         g_att = after(g_att, *twos)
+        twos = [twos[0]] + [grid.send(twos[r], grid.swap_head(r)) for r in three]
+    gq_high, gkv_high, gh_high, gplan_high = attend_back(
+        q, kv, skv, g_att, kv_halo, kv_own, plan, live, 1, PAIRS - 1
+    )
+    gq, gkv = (gq_low, gq_high), (gkv_low, gkv_high)
+    gmeans, gsort, *sends = sink_backward(
+        pieces, w_pairs, *kept, gplan_low, gplan_high, own, context
+    )
+    if fast:
+        twos = merge_sum(at, 1, lax.optimization_barrier((*twos, gmeans))[:4])
+        gh_high = after(gh_high, *twos)
         twos = [twos[0]] + [grid.send(twos[r], grid.swap_plane(r)) for r in three]
-    gq_high, gkv_high, gh_high, gplan_high = attend_back(
-        q, kv, skv, g_att, kvx, plan, live, PAIRS // 2, PAIRS // 2
-    )
-    gq, gkv = (gq_low, gq_high), (gkv_low, gkv_high)
-    gn_far, gn_near, g_kv_halo = halo_back(gh_low, gh_high, normed_halo, wt_kv, second)
+    gn_far, gn_near, g_kv_halo = halo_back(
+        gh_low, gh_high, normed_halo, wt_q, wt_kv, gmeans, second
+    )
+    sends = lax.optimization_barrier((*sends, gn_near))[:2]
+    far = [grid.send(value, grid.along(step)) for value, step in zip(sends, (1, 2))]
+    gn_far, gn_near = lax.optimization_barrier((gn_far, gn_near, *far, *twos))[:2]
     back_one = grid.send(gn_near, grid.along(-1))
     back_two = grid.send(gn_far, grid.along(-2))
-    gmeans, gsort, *sends = sink_backward(
-        pieces, w_pairs, *kept, gplan_low, after(gplan_high, gn_near), own, context
-    )
-    gmeans_here = after(gmeans, *twos) if fast else gmeans
+    gmeans = after(gmeans, gn_near)
     keep, send = weight_back(
-        at, gq, gkv, normed, wt_q, wt_kv, gmeans_here, pieces, g_kv_halo, gain_one, gsort, fast
+        at, gq, gkv, normed, wt_q, wt_kv, gmeans, pieces, g_kv_halo, gain_one, gsort, fast
     )
     if fast:
         got = grid.send(send, grid.swap_core())
-        ones = split_sum(at, 0, keep, got)
+        ones = split_sum(at, 1, keep, got)
+        ones = [ones[0]] + [grid.send(ones[r], grid.swap_plane(r)) for r in three]
+        ones = merge_sum(at, 0, ones)
         ones = [ones[0]] + [grid.send(ones[r], grid.swap_head(r)) for r in three]
-        sends = lax.optimization_barrier((*sends, ones[0]))[:4]
-        twos = merge_sum(at, 0, lax.optimization_barrier((*twos, ones[0]))[:4])
-        twos = [twos[0]] + [grid.send(twos[r], grid.swap_head(r)) for r in three]
-    steps = (-2, -1, 1, 2)
-    far = [grid.send(value, grid.along(step)) for value, step in zip(sends, steps)]
-    if fast:
-        ones = merge_sum(at, 1, ones)
-        ones = [ones[0]] + [grid.send(ones[r], grid.swap_plane(r)) for r in three]
     input_grad = finish(
         x, gq, gkv, wt_q, wt_kv, gmeans, far, back_one, back_two, g_middle, gain_one
     )
     if fast:
-        g_wqkv, g_sort, g_gain_one = last_one(ones)
+        g_wqkv, g_sort, g_gain_one = last_one(lax.optimization_barrier((*ones, input_grad))[:4])
         g_in, g_down, g_out, *small = last_two(twos)
         g_wqkv, g_sort, g_down, g_out = g_wqkv.T, g_sort.T, g_down.T, g_out.T
         g_gain_one = g_gain_one[0]

time: 334 us -> 316 us (0.946)
  starting transfers between devices: 72.7 us -> 61.2 us
  waiting for transfers between devices: 71.9 us -> 60.6 us
  Pallas kernels: 169 us -> 174 us
    ppermute x40 -> x38, starting transfers between devices: 72.7 us -> 61.2 us  [send(): return lax.ppermute(value, ('head', 'plane', 'core'), pairs)]
    ppermute x40 -> x38, waiting for transfers between devices: 71.9 us -> 60.6 us  [send(): return lax.ppermute(value, ('head', 'plane', 'core'), pairs)]
    pallas_call x3 -> x4, Pallas kernels: 21.5 us -> 26.3 us  [the longest x2 14.7 us: context_project(): pl.pallas_call(functools.partial(context_kernel, len(values), keep), grid...]
  transfers between devices with their start and end apart: 40 -> 38, of which waited for: 16 -> 14; matrix products, arithmetic and copies ran while one was open for 2% -> 1% of each run, Pallas kernels for 37% -> 40%
where the time goes in v1:
time: 316 us; the launch traced here: 312 us
  Pallas kernels  174 us (55%)
  starting transfers between devices  61.2 us (19%)
  waiting for transfers between devices  60.6 us (19%)
  local copies, waits for them, and re-layouts  9.09 us (3%)
  other arithmetic  6.25 us (2%)
    ppermute x38, starting transfers between devices, send(): return lax.ppermute(value, ('head', 'plane', 'core'), pairs)  61.2 us
    ppermute x38, waiting for transfers between devices, send(): return lax.ppermute(value, ('head', 'plane', 'core'), pairs)  60.6 us
    pallas_call x1, Pallas kernels, feed_fast(): pl.pallas_call(feed_fast_kernel, grid=(tok // tile,), in_specs=[SMEM, til...  38.4 us
    pallas_call x2, Pallas kernels, attend_back(): pl.pallas_call(attend_back_kernel, grid=(pairs,), in_specs=[pl.BlockSpec(...  25.2 us
    pallas_call x2, Pallas kernels, context_project(): pl.pallas_call(functools.partial(context_kernel, len(values), keep), grid...  14.7 us
    pallas_call x1, Pallas kernels, attend(): pl.pallas_call(attend_kernel, grid=(PAIRS,), in_specs=[pl.BlockSpec((tok,...  12.7 us
    pallas_call x1, Pallas kernels, sink_forward(): pl.pallas_call(functools.partial(sink_forward_kernel, own, context), in_s...  12.6 us
    pallas_call x1, Pallas kernels, finish(): pl.pallas_call(functools.partial(finish_kernel, skip), grid=(tok // tile,...  12.2 us
  transfers between devices with their start and end apart: 38, of which 14 were waited for; matrix products, arithmetic and copies ran while one was open for 1% of the time, Pallas kernels for 40%

profile of v1, /device:TPU:12, one launch (start us, length us, event | category | flops | bytes accessed | tf_op | source)
XLA Modules:
  0.0 312.3 jit_solution(12892637579964790872)
XLA Ops:
  15.5 5.6 %collective-permute-done.5 = bf16[4,208,128]{2,1,0:T(8,128)(2,1)S(1)} collective-permute-done((bf16[4,208,128]{2,1,0:T(8,128)(2,1)S(1)}, bf16[4,208,128]{2,1,0:T(8,128)(2,1)S(1)}, u32[]{:S(2)}, u32[]{:S(2)}) %collective-permute-start.5) | collective-permute-done | bytes 213024 | tf_op jit(solution)/shard_map/ppermute | solution.py:1294
  38.6 8.3 %project.1 = (bf16[1536,512]{1,0:T(8,128)(2,1)}, bf16[1536,512]{1,0:T(8,128)(2,1)}, bf16[1536,1024]{1,0:T(8,128)(2,1)}, f32[48,1536]{1,0:T(8,128)}, f32[16,1536]{1,0:T(8,128)}, /*index=5*/f32[16,1536]{1,0:T(8,128)}) custom-call(bf16[1536,512]{1,0:T(8,128)(2,1)} %bitcast.52, f32[1,512]{1,0:T(1,128)} %get-tuple-element.129.gain_ref.refs_1_.refs_2_, ...), custom_call_target="tpu_custom_call" | custom-call | tf_op jit(solution)/shard_map/project/pallas_call | solution.py:710
  47.0 6.8 %context_own.1.kvo_ref = bf16[8,48,4096]{2,1,0:T(8,128)(2,1)} custom-call(bf16[48,32,512]{2,1,0:T(8,128)(2,1)} %bitcast.53, f32[1,512]{1,0:T(1,128)} %get-tuple-element.129.gain_ref.refs_1_.refs_2_, bf16[1024,512]{1,0:T(8,128)(2,1)} %get-tuple-element.121.wkv_ref.refs_2_.refs_3_.w_ref), custom_call_target="tpu_custom_call" | custom-call | tf_op jit(solution)/shard_map/context_own/pallas_call | solution.py:354
  53.8 20.0 %collective-permute-done.7 = bf16[512,512]{1,0:T(8,128)(2,1)} collective-permute-done((bf16[512,512]{1,0:T(8,128)(2,1)}, bf16[512,512]{1,0:T(8,128)(2,1)}, u32[]{:S(2)}, u32[]{:S(2)}) %collective-permute-start.7) | collective-permute-done | bytes 524320 | tf_op jit(solution)/shard_map/ppermute | solution.py:1294
  75.8 3.9 %collective-permute-start.13 = (f32[48,1536]{1,0:T(8,128)S(1)}, f32[48,1536]{1,0:T(8,128)S(1)}, u32[]{:S(2)}, u32[]{:S(2)}) collective-permute-start(f32[48,1536]{1,0:T(8,128)S(1)} %copy-done.3), channel_id=1, source_target_pairs={{0,8},{8,16},{16,24},{24,1},{1,9},{9,17},{17,25},{25,2},{2,10},{10... | collective-permute-start | bytes 884744 | tf_op jit(solution)/shard_map/ppermute | solution.py:1294
  81.7 3.9 %collective-permute-start.15 = (f32[16,1536]{1,0:T(8,128)S(1)}, f32[16,1536]{1,0:T(8,128)S(1)}, u32[]{:S(2)}, u32[]{:S(2)}) collective-permute-start(f32[16,1536]{1,0:T(8,128)S(1)} %copy-done.33), channel_id=1, source_target_pairs={{16,0},{24,8},{1,16},{9,24},{17,1},{25,9},{2,17},{10,25},{18,2},{2... | collective-permute-start | bytes 294920 | tf_op jit(solution)/shard_map/ppermute | solution.py:1294
  85.8 7.9 %context_halo.1 = (bf16[8,64,4096]{2,1,0:T(8,128)(2,1)}, bf16[32,64,512]{2,1,0:T(8,128)(2,1)}) custom-call(bf16[16,32,512]{2,1,0:T(8,128)(2,1)} %bitcast.21.refs_0_, bf16[48,32,512]{2,1,0:T(8,128)(2,1)} %bitcast.22.refs_1_, f32[1,512]{1,0:T(1,128)} %get-tuple-element.129.gain_ref.refs_1_.refs_2_, ...), custom_call_target="tpu_custom_call" | custom-call | tf_op jit(solution)/shard_map/context_halo/pallas_call | solution.py:354
  101.5 12.6 %sink_forward.1 = (bf16[8,48,128]{2,1,0:T(8,128)(2,1)}, f32[8,8,176,128]{3,2,1,0:T(8,128)}, f32[8,8,4,128]{3,2,1,0:T(4,128)}, f32[8,176,128]{2,1,0:T(8,128)}) custom-call(f32[16,1536]{1,0:T(8,128)} %copy-done.9, f32[48,1536]{1,0:T(8,128)} %copy-done.5, f32[48,1536]{1,0:T(8,128)} %get-tuple-element.136.c.pc, f32[48,1536]{1,0:T(8,128)} %copy-done.4, ...), custom_call_target="tpu_custom_call" | custom-call | tf_op jit(solution)/shard_map/sink_forward/pallas_call | solution.py:268
  114.1 12.7 %attend.1 = (bf16[1536,512]{1,0:T(8,128)(2,1)}, bf16[1536,1024]{1,0:T(8,128)(2,1)}) custom-call(bf16[1536,512]{1,0:T(8,128)(2,1)} %get-tuple-element.122.q_ref, bf16[1536,1024]{1,0:T(8,128)(2,1)} %get-tuple-element.123.kv_ref, bf16[8,64,4096]{2,1,0:T(8,128)(2,1)} %get-tuple-element.130.kvh_ref, bf16[8,48,4096]{2,1,0:T(8,128)(2,1)} %context_own.1.kvo_ref, ...), custom_call_target="tpu_custom_call" | custom-call | tf_op jit(solution)/shard_map/attend/pallas_call | solution.py:461
  128.6 4.5 %collective-permute-done.19.other_ref = bf16[4,4,576,128]{3,2,1,0:T(8,128)(2,1)S(1)} collective-permute-done((bf16[4,4,576,128]{3,2,1,0:T(8,128)(2,1)S(1)}, bf16[4,4,576,128]{3,2,1,0:T(8,128)(2,1)S(1)}, u32[]{:S(2)}, u32[]{:S(2)}) %collective-permute-start.19) | collective-permute-done | bytes 2359328 | tf_op jit(solution)/shard_map/ppermute | solution.py:1294
  134.7 38.4 %feed.1 = (bf16[1536,512]{1,0:T(8,128)(2,1)}, f32[1536,512]{1,0:T(8,128)}, bf16[1536,512]{1,0:T(8,128)(2,1)}, bf16[4,4,592,128]{3,2,1,0:T(8,128)(2,1)}, bf16[4,4,592,128]{3,2,1,0:T(8,128)(2,1)}) custom-call(s32[3]{0:T(128)} %pad_add_fusion.1.at_ref, bf16[1536,512]{1,0:T(8,128)(2,1)} %bitcast.54, bf16[1536,512]{1,0:T(8,128)(2,1)} %get-tuple-element.141.att_ref, ...), custom_call_target="tpu_custom_call" | custom-call | tf_op jit(solution)/shard_map/feed/pallas_call | solution.py:974
  173.3 7.9 %attend_back.2 = (bf16[1536,128]{1,0:T(8,128)(2,1)}, bf16[1536,256]{1,0:T(8,128)(2,1)}, bf16[2,64,4096]{2,1,0:T(8,128)(2,1)}, f32[2,48,128]{2,1,0:T(8,128)}) custom-call(bf16[1536,512]{1,0:T(8,128)(2,1)} %get-tuple-element.122.q_ref, bf16[1536,1024]{1,0:T(8,128)(2,1)} %get-tuple-element.123.kv_ref, bf16[1536,1024]{1,0:T(8,128)(2,1)} %get-tuple-element.155.skv_ref, ...), custom_call_target="tpu_custom_call" | custom-call | tf_op jit(solution)/shard_map/attend_back/pallas_call | solution.py:584
  182.7 4.4 %split_sum.2 = (bf16[4,592,128]{2,1,0:T(8,128)(2,1)}, bf16[4,592,128]{2,1,0:T(8,128)(2,1)}, bf16[4,592,128]{2,1,0:T(8,128)(2,1)}, bf16[4,592,128]{2,1,0:T(8,128)(2,1)}) custom-call(s32[3]{0:T(128)} %pad_add_fusion.1.at_ref, bf16[4,4,592,128]{3,2,1,0:T(8,128)(2,1)} %get-tuple-element.160.keep_ref, bf16[4,4,592,128]{3,2,1,0:T(8,128)(2,1)} %copy-done.6), custom_call_target="tpu_custom_call" | custom-call | tf_op jit(solution)/shard_map/split_sum/pallas_call | solution.py:1051
  190.6 17.3 %attend_back.3 = (bf16[1536,384]{1,0:T(8,128)(2,1)}, bf16[1536,768]{1,0:T(8,128)(2,1)}, bf16[6,64,4096]{2,1,0:T(8,128)(2,1)}, f32[6,48,128]{2,1,0:T(8,128)}) custom-call(bf16[1536,512]{1,0:T(8,128)(2,1)} %get-tuple-element.122.q_ref, bf16[1536,1024]{1,0:T(8,128)(2,1)} %get-tuple-element.123.kv_ref, bf16[1536,1024]{1,0:T(8,128)(2,1)} %get-tuple-element.155.skv_ref, ...), custom_call_target="tpu_custom_call" | custom-call | tf_op jit(solution)/shard_map/attend_back/pallas_call | solution.py:584
  207.9 9.2 %sink_backward.1 = (f32[176,1024]{1,0:T(8,128)}, f32[4,64,128]{2,1,0:T(8,128)}, bf16[48,1024]{1,0:T(8,128)(2,1)}, bf16[16,1024]{1,0:T(8,128)(2,1)}) custom-call(f32[16,1536]{1,0:T(8,128)} %copy-done.9, f32[48,1536]{1,0:T(8,128)} %copy-done.5, f32[48,1536]{1,0:T(8,128)} %get-tuple-element.136.c.pc, f32[48,1536]{1,0:T(8,128)} %copy-done.4, ...), custom_call_target="tpu_custom_call" | custom-call | tf_op jit(solution)/shard_map/sink_backward/pallas_call | solution.py:293
  224.5 9.2 %halo_back.1 = (bf16[32,16,512]{2,1,0:T(8,128)(2,1)}, bf16[32,48,512]{2,1,0:T(8,128)(2,1)}, f32[1024,512]{1,0:T(8,128)}) custom-call(bf16[2,64,4096]{2,1,0:T(8,128)(2,1)} %get-tuple-element.159.low_ref, bf16[6,64,4096]{2,1,0:T(8,128)(2,1)} %get-tuple-element.185.high_ref, bf16[32,64,512]{2,1,0:T(8,128)(2,1)} %get-tuple-element.186.nh_ref, ...), custom_call_target="tpu_custom_call" | custom-call | tf_op jit(solution)/shard_map/halo_back/pallas_call | solution.py:651
  238.3 3.9 %collective-permute-done.25.fe = bf16[16,1024]{1,0:T(8,128)(2,1)S(1)} collective-permute-done((bf16[16,1024]{1,0:T(8,128)(2,1)S(1)}, bf16[16,1024]{1,0:T(8,128)(2,1)S(1)}, u32[]{:S(2)}, u32[]{:S(2)}) %collective-permute-start.25) | collective-permute-done | bytes 32800 | tf_op jit(solution)/shard_map/ppermute | solution.py:1294
  242.3 4.5 %collective-permute-start.29 = (bf16[32,48,512]{2,1,0:T(8,128)(2,1)}, bf16[32,48,512]{2,1,0:T(8,128)(2,1)S(1)}, u32[]{:S(2)}, u32[]{:S(2)}) collective-permute-start(bf16[32,48,512]{2,1,0:T(8,128)(2,1)} %get-tuple-element.193), channel_id=1, source_target_pairs={{8,0},{16,8},{24,16},{1,24},{9,1},{17,9},{25,17},{2,25},{10,2},{18... | collective-permute-start | bytes 4718600 | tf_op jit(solution)/shard_map/ppermute | solution.py:1294
  246.8 9.9 %weight_back.1 = (bf16[4,4,208,128]{3,2,1,0:T(8,128)(2,1)}, bf16[4,4,208,128]{3,2,1,0:T(8,128)(2,1)}) custom-call(s32[3]{0:T(128)} %pad_add_fusion.1.at_ref, bf16[1536,128]{1,0:T(8,128)(2,1)} %get-tuple-element.157.ql_ref, bf16[1536,384]{1,0:T(8,128)(2,1)} %get-tuple-element.167.qh_ref, bf16[1536,256]{1,0:T(8,128)(2,1)} %get-tuple-element.168.kvl_ref, ...), custom_call_target="tpu_custom_call" | custom-call | tf_op jit(solution)/shard_map/weight_back/pallas_call | solution.py:1193
  267.3 5.5 %collective-permute-done.32.b_ref = bf16[4,208,128]{2,1,0:T(8,128)(2,1)S(1)} collective-permute-done((bf16[4,208,128]{2,1,0:T(8,128)(2,1)}, bf16[4,208,128]{2,1,0:T(8,128)(2,1)S(1)}, u32[]{:S(2)}, u32[]{:S(2)}) %collective-permute-start.32) | collective-permute-done | bytes 213024 | tf_op jit(solution)/shard_map/ppermute | solution.py:1294
  272.9 8.2 %collective-permute-done.33.c_ref = bf16[4,208,128]{2,1,0:T(8,128)(2,1)S(1)} collective-permute-done((bf16[4,208,128]{2,1,0:T(8,128)(2,1)}, bf16[4,208,128]{2,1,0:T(8,128)(2,1)S(1)}, u32[]{:S(2)}, u32[]{:S(2)}) %collective-permute-start.33) | collective-permute-done | bytes 213024 | tf_op jit(solution)/shard_map/ppermute | solution.py:1294
  281.0 5.3 %collective-permute-done.34.d_ref = bf16[4,208,128]{2,1,0:T(8,128)(2,1)S(1)} collective-permute-done((bf16[4,208,128]{2,1,0:T(8,128)(2,1)}, bf16[4,208,128]{2,1,0:T(8,128)(2,1)S(1)}, u32[]{:S(2)}, u32[]{:S(2)}) %collective-permute-start.34) | collective-permute-done | bytes 213024 | tf_op jit(solution)/shard_map/ppermute | solution.py:1294
  289.1 4.1 %collective-permute-start.36 = (bf16[208,128]{1,0:T(8,128)(2,1)}, bf16[208,128]{1,0:T(8,128)(2,1)S(1)}, u32[]{:S(2)}, u32[]{:S(2)}) collective-permute-start(bf16[208,128]{1,0:T(8,128)(2,1)} %get-tuple-element.208), channel_id=1, source_target_pairs={{0,16},{1,17},{2,18},{3,19},{4,20},{5,21},{6,22},{7,23},{8,24},{9,... | collective-permute-start | bytes 159752 | tf_op jit(solution)/shard_map/ppermute | solution.py:1294
  297.8 12.2 %finish.1 = f32[1536,512]{1,0:T(8,128)} custom-call(bf16[1536,512]{1,0:T(8,128)(2,1)} %bitcast.55, bf16[1536,128]{1,0:T(8,128)(2,1)} %get-tuple-element.157.ql_ref, bf16[1536,384]{1,0:T(8,128)(2,1)} %get-tuple-element.167.qh_ref, bf16[1536,256]{1,0:T(8,128)(2,1)} %get-tuple-element.168.kvl_ref, bf16[1536,768]{1,0:T(8,128)(2,1)} %get-tuple-element.169.kvh_ref, ...), custom_call_target="tpu_custom_call" | custom-call | tf_op jit(solution)/shard_map/finish/pallas_call | solution.py:1260
  (166 shorter events, 84.8 us)
Async XLA Ops:
  23.5 50.4 %collective-permute-start.8 = (bf16[1536,512]{1,0:T(8,128)(2,1)S(1)}, bf16[1536,512]{1,0:T(8,128)(2,1)}, u32[]{:S(2)}, u32[]{:S(2)}) collective-permute-start(bf16[1536,512]{1,0:T(8,128)(2,1)S(1)} %bitcast.56), channel_id=1, source_target_pairs={{0,8},{8,16},{16,24},{24,1},{1,9},{9,17},{17,25},{25,2},{2,10},{10... | collective-permute-start | bytes 4718600 | tf_op jit(solution)/shard_map/ppermute | solution.py:1294
  26.4 47.4 %collective-permute-start.7 = (bf16[512,512]{1,0:T(8,128)(2,1)}, bf16[512,512]{1,0:T(8,128)(2,1)}, u32[]{:S(2)}, u32[]{:S(2)}) collective-permute-start(bf16[512,512]{1,0:T(8,128)(2,1)} %get-tuple-element.125), channel_id=1, source_target_pairs={{0,16},{8,24},{16,1},{24,9},{1,17},{9,25},{17,2},{25,10},{2,18},{1... | collective-permute-start | bytes 1572872 | tf_op jit(solution)/shard_map/ppermute | solution.py:1294
  29.7 44.1 %collective-permute-start.11 = (bf16[576,128]{1,0:T(8,128)(2,1)S(1)}, bf16[576,128]{1,0:T(8,128)(2,1)}, u32[]{:S(2)}, u32[]{:S(2)}) collective-permute-start(bf16[576,128]{1,0:T(8,128)(2,1)S(1)} %copy-done.23), channel_id=1, source_target_pairs={{0,6},{1,7},{2,4},{3,5},{4,2},{5,3},{6,0},{7,1},{8,14},{9,15},{10,... | collective-permute-start | bytes 442376 | tf_op jit(solution)/shard_map/ppermute | solution.py:1294
  30.9 43.0 %collective-permute-start.10 = (bf16[576,128]{1,0:T(8,128)(2,1)S(1)}, bf16[576,128]{1,0:T(8,128)(2,1)}, u32[]{:S(2)}, u32[]{:S(2)}) collective-permute-start(bf16[576,128]{1,0:T(8,128)(2,1)S(1)} %copy-done.23), channel_id=1, source_target_pairs={{0,4},{1,5},{2,6},{3,7},{4,0},{5,1},{6,2},{7,3},{8,12},{9,13},{10,... | collective-permute-start | bytes 442376 | tf_op jit(solution)/shard_map/ppermute | solution.py:1294
  34.7 39.2 %collective-permute-start.9 = (bf16[576,128]{1,0:T(8,128)(2,1)S(1)}, bf16[576,128]{1,0:T(8,128)(2,1)}, u32[]{:S(2)}, u32[]{:S(2)}) collective-permute-start(bf16[576,128]{1,0:T(8,128)(2,1)S(1)} %copy-done.23), channel_id=1, source_target_pairs={{0,2},{1,3},{2,0},{3,1},{4,6},{5,7},{6,4},{7,5},{8,10},{9,11},{10,... | collective-permute-start | bytes 442376 | tf_op jit(solution)/shard_map/ppermute | solution.py:1294
  73.8 20.4 %collective-permute-start.14 = (f32[48,1536]{1,0:T(8,128)S(1)}, f32[48,1536]{1,0:T(8,128)S(1)}, u32[]{:S(2)}, u32[]{:S(2)}) collective-permute-start(f32[48,1536]{1,0:T(8,128)S(1)} %copy-done.3), channel_id=1, source_target_pairs={{8,0},{16,8},{24,16},{1,24},{9,1},{17,9},{25,17},{2,25},{10,2},{18... | collective-permute-start | bytes 884744 | tf_op jit(solution)/shard_map/ppermute | solution.py:1294
  75.8 18.5 %collective-permute-start.13 = (f32[48,1536]{1,0:T(8,128)S(1)}, f32[48,1536]{1,0:T(8,128)S(1)}, u32[]{:S(2)}, u32[]{:S(2)}) collective-permute-start(f32[48,1536]{1,0:T(8,128)S(1)} %copy-done.3), channel_id=1, source_target_pairs={{0,8},{8,16},{16,24},{24,1},{1,9},{9,17},{17,25},{25,2},{2,10},{10... | collective-permute-start | bytes 884744 | tf_op jit(solution)/shard_map/ppermute | solution.py:1294
  79.7 14.4 %collective-permute-start.12 = (f32[16,1536]{1,0:T(8,128)S(1)}, f32[16,1536]{1,0:T(8,128)S(1)}, u32[]{:S(2)}, u32[]{:S(2)}) collective-permute-start(f32[16,1536]{1,0:T(8,128)S(1)} %copy-done.34), channel_id=1, source_target_pairs={{0,16},{8,24},{16,1},{24,9},{1,17},{9,25},{17,2},{25,10},{2,18},{1... | collective-permute-start | bytes 294920 | tf_op jit(solution)/shard_map/ppermute | solution.py:1294
  95.7 31.1 %collective-permute-start.18 = (bf16[4,576,128]{2,1,0:T(8,128)(2,1)S(1)}, bf16[4,576,128]{2,1,0:T(8,128)(2,1)}, u32[]{:S(2)}, u32[]{:S(2)}) collective-permute-start(bf16[4,576,128]{2,1,0:T(8,128)(2,1)S(1)} %pad_maximum_fusion.2), channel_id=1, source_target_pairs={{0,24},{1,25},{2,26},{3,27},{4,28},{5,29},{6,30},{7,31},{8,16},{9,... | collective-permute-start | bytes 1769480 | tf_op jit(solution)/shard_map/ppermute | solution.py:1294
  96.8 30.0 %collective-permute-start.17 = (bf16[4,576,128]{2,1,0:T(8,128)(2,1)S(1)}, bf16[4,576,128]{2,1,0:T(8,128)(2,1)}, u32[]{:S(2)}, u32[]{:S(2)}) collective-permute-start(bf16[4,576,128]{2,1,0:T(8,128)(2,1)S(1)} %pad_maximum_fusion.2), channel_id=1, source_target_pairs={{0,16},{1,17},{2,18},{3,19},{4,20},{5,21},{6,22},{7,23},{8,24},{9,... | collective-permute-start | bytes 1769480 | tf_op jit(solution)/shard_map/ppermute | solution.py:1294
  96.8 30.1 %collective-permute-start.16 = (bf16[4,576,128]{2,1,0:T(8,128)(2,1)S(1)}, bf16[4,576,128]{2,1,0:T(8,128)(2,1)}, u32[]{:S(2)}, u32[]{:S(2)}) collective-permute-start(bf16[4,576,128]{2,1,0:T(8,128)(2,1)S(1)} %pad_maximum_fusion.2), channel_id=1, source_target_pairs={{0,8},{1,9},{2,10},{3,11},{4,12},{5,13},{6,14},{7,15},{8,0},{9,1},... | collective-permute-start | bytes 1769480 | tf_op jit(solution)/shard_map/ppermute | solution.py:1294
  187.1 30.0 %collective-permute-start.21 = (bf16[4,592,128]{2,1,0:T(8,128)(2,1)}, bf16[4,592,128]{2,1,0:T(8,128)(2,1)S(1)}, u32[]{:S(2)}, u32[]{:S(2)}) collective-permute-start(bf16[4,592,128]{2,1,0:T(8,128)(2,1)} %get-tuple-element.163), channel_id=1, source_target_pairs={{0,8},{1,9},{2,10},{3,11},{4,12},{5,13},{6,14},{7,15},{8,0},{9,1},... | collective-permute-start | bytes 1818632 | tf_op jit(solution)/shard_map/ppermute | solution.py:1294
  187.1 30.0 %collective-permute-start.22 = (bf16[4,592,128]{2,1,0:T(8,128)(2,1)}, bf16[4,592,128]{2,1,0:T(8,128)(2,1)S(1)}, u32[]{:S(2)}, u32[]{:S(2)}) collective-permute-start(bf16[4,592,128]{2,1,0:T(8,128)(2,1)} %get-tuple-element.164), channel_id=1, source_target_pairs={{0,16},{1,17},{2,18},{3,19},{4,20},{5,21},{6,22},{7,23},{8,24},{9,... | collective-permute-start | bytes 1818632 | tf_op jit(solution)/shard_map/ppermute | solution.py:1294
  188.7 28.4 %collective-permute-start.23 = (bf16[4,592,128]{2,1,0:T(8,128)(2,1)}, bf16[4,592,128]{2,1,0:T(8,128)(2,1)S(1)}, u32[]{:S(2)}, u32[]{:S(2)}) collective-permute-start(bf16[4,592,128]{2,1,0:T(8,128)(2,1)} %get-tuple-element.165), channel_id=1, source_target_pairs={{0,24},{1,25},{2,26},{3,27},{4,28},{5,29},{6,30},{7,31},{8,16},{9,... | collective-permute-start | bytes 1818632 | tf_op jit(solution)/shard_map/ppermute | solution.py:1294
  221.1 21.2 %collective-permute-start.26 = (bf16[592,128]{1,0:T(8,128)(2,1)}, bf16[592,128]{1,0:T(8,128)(2,1)S(1)}, u32[]{:S(2)}, u32[]{:S(2)}) collective-permute-start(bf16[592,128]{1,0:T(8,128)(2,1)} %get-tuple-element.182), channel_id=1, source_target_pairs={{0,2},{1,3},{2,0},{3,1},{4,6},{5,7},{6,4},{7,5},{8,10},{9,11},{10,... | collective-permute-start | bytes 454664 | tf_op jit(solution)/shard_map/ppermute | solution.py:1294
  222.1 20.1 %collective-permute-start.27 = (bf16[592,128]{1,0:T(8,128)(2,1)}, bf16[592,128]{1,0:T(8,128)(2,1)S(1)}, u32[]{:S(2)}, u32[]{:S(2)}) collective-permute-start(bf16[592,128]{1,0:T(8,128)(2,1)} %get-tuple-element.183), channel_id=1, source_target_pairs={{0,4},{1,5},{2,6},{3,7},{4,0},{5,1},{6,2},{7,3},{8,12},{9,13},{10,... | collective-permute-start | bytes 454664 | tf_op jit(solution)/shard_map/ppermute | solution.py:1294
  222.8 19.4 %collective-permute-start.28 = (bf16[592,128]{1,0:T(8,128)(2,1)}, bf16[592,128]{1,0:T(8,128)(2,1)S(1)}, u32[]{:S(2)}, u32[]{:S(2)}) collective-permute-start(bf16[592,128]{1,0:T(8,128)(2,1)} %get-tuple-element.184), channel_id=1, source_target_pairs={{0,6},{1,7},{2,4},{3,5},{4,2},{5,3},{6,0},{7,1},{8,14},{9,15},{10,... | collective-permute-start | bytes 454664 | tf_op jit(solution)/shard_map/ppermute | solution.py:1294
  242.3 54.2 %collective-permute-start.29 = (bf16[32,48,512]{2,1,0:T(8,128)(2,1)}, bf16[32,48,512]{2,1,0:T(8,128)(2,1)S(1)}, u32[]{:S(2)}, u32[]{:S(2)}) collective-permute-start(bf16[32,48,512]{2,1,0:T(8,128)(2,1)} %get-tuple-element.193), channel_id=1, source_target_pairs={{8,0},{16,8},{24,16},{1,24},{9,1},{17,9},{25,17},{2,25},{10,2},{18... | collective-permute-start | bytes 4718600 | tf_op jit(solution)/shard_map/ppermute | solution.py:1294
  256.8 39.7 %collective-permute-start.30 = (bf16[32,16,512]{2,1,0:T(8,128)(2,1)S(1)}, bf16[32,16,512]{2,1,0:T(8,128)(2,1)S(1)}, u32[]{:S(2)}, u32[]{:S(2)}) collective-permute-start(bf16[32,16,512]{2,1,0:T(8,128)(2,1)S(1)} %copy-done.31), channel_id=1, source_target_pairs={{16,0},{24,8},{1,16},{9,24},{17,1},{25,9},{2,17},{10,25},{18,2},{2... | collective-permute-start | bytes 1572872 | tf_op jit(solution)/shard_map/ppermute | solution.py:1294
  264.3 16.7 %collective-permute-start.33 = (bf16[4,208,128]{2,1,0:T(8,128)(2,1)}, bf16[4,208,128]{2,1,0:T(8,128)(2,1)S(1)}, u32[]{:S(2)}, u32[]{:S(2)}) collective-permute-start(bf16[4,208,128]{2,1,0:T(8,128)(2,1)} %get-tuple-element.204), channel_id=1, source_target_pairs={{0,4},{1,5},{2,6},{3,7},{4,0},{5,1},{6,2},{7,3},{8,12},{9,13},{10,... | collective-permute-start | bytes 638984 | tf_op jit(solution)/shard_map/ppermute | solution.py:1294
  265.9 20.4 %collective-permute-start.34 = (bf16[4,208,128]{2,1,0:T(8,128)(2,1)}, bf16[4,208,128]{2,1,0:T(8,128)(2,1)S(1)}, u32[]{:S(2)}, u32[]{:S(2)}) collective-permute-start(bf16[4,208,128]{2,1,0:T(8,128)(2,1)} %get-tuple-element.205), channel_id=1, source_target_pairs={{0,6},{1,7},{2,4},{3,5},{4,2},{5,3},{6,0},{7,1},{8,14},{9,15},{10,... | collective-permute-start | bytes 638984 | tf_op jit(solution)/shard_map/ppermute | solution.py:1294
  289.0 21.1 %collective-permute-start.35 = (bf16[208,128]{1,0:T(8,128)(2,1)}, bf16[208,128]{1,0:T(8,128)(2,1)S(1)}, u32[]{:S(2)}, u32[]{:S(2)}) collective-permute-start(bf16[208,128]{1,0:T(8,128)(2,1)} %get-tuple-element.207), channel_id=1, source_target_pairs={{0,8},{1,9},{2,10},{3,11},{4,12},{5,13},{6,14},{7,15},{8,0},{9,1},... | collective-permute-start | bytes 159752 | tf_op jit(solution)/shard_map/ppermute | solution.py:1294
  289.1 21.0 %collective-permute-start.36 = (bf16[208,128]{1,0:T(8,128)(2,1)}, bf16[208,128]{1,0:T(8,128)(2,1)S(1)}, u32[]{:S(2)}, u32[]{:S(2)}) collective-permute-start(bf16[208,128]{1,0:T(8,128)(2,1)} %get-tuple-element.208), channel_id=1, source_target_pairs={{0,16},{1,17},{2,18},{3,19},{4,20},{5,21},{6,22},{7,23},{8,24},{9,... | collective-permute-start | bytes 159752 | tf_op jit(solution)/shard_map/ppermute | solution.py:1294
  293.2 16.9 %collective-permute-start.37 = (bf16[208,128]{1,0:T(8,128)(2,1)}, bf16[208,128]{1,0:T(8,128)(2,1)S(1)}, u32[]{:S(2)}, u32[]{:S(2)}) collective-permute-start(bf16[208,128]{1,0:T(8,128)(2,1)} %get-tuple-element.209), channel_id=1, source_target_pairs={{0,24},{1,25},{2,26},{3,27},{4,28},{5,29},{6,30},{7,31},{8,16},{9,... | collective-permute-start | bytes 159752 | tf_op jit(solution)/shard_map/ppermute | solution.py:1294
  (50 other events, 501.5 us)

commit v2 on v1

--- a/solution.py
+++ b/solution.py
@@ -1210,11 +1210,10 @@
     )(at, *gq, *gkv, normed, wt_q, wt_kv, gm, *pieces, halo, gain, gsort)
 
 
-def finish_kernel(
-    skip, x_ref, ql_ref, qh_ref, kvl_ref, kvh_ref, wq_ref, wkv_ref, gm_ref, fd, fe,
-    one_ref, two_ref, g_ref, gain_ref, out_ref, total, blocks_ref,
+def inner_kernel(
+    ql_ref, qh_ref, kvl_ref, kvh_ref, wq_ref, wkv_ref, gm_ref, fd, fe, out_ref, blocks_ref
 ):
-    rows = x_ref.shape[0]
+    rows = ql_ref.shape[0]
     per = rows // BLOCK
 
     @pl.when(pl.program_id(0) == 0)
@@ -1224,18 +1223,41 @@
         blocks_ref[...] = gm_ref[halo : halo + own, :] + fd[...].astype(F32)
         blocks_ref[:ends, :] += fe[...].astype(F32)
 
-    at = lax.broadcasted_iota(jnp.int32, (rows, rows), 0)
-    lane = lax.broadcasted_iota(jnp.int32, (rows, rows), 1)
-    order = (lane == lax.rem(at, BLOCK) * 8 + at // BLOCK).astype(F32).astype(BF16)
-    value = mm(order, one_ref[...].reshape(rows, D))
     cut = ql_ref.shape[1]
-    value = value + mm(ql_ref[...], wq_ref[:cut, :]) + mm(qh_ref[...], wq_ref[cut:, :])
+    value = mm(ql_ref[...], wq_ref[:cut, :]) + mm(qh_ref[...], wq_ref[cut:, :])
     value = value + mm(kvl_ref[...], wkv_ref[: 2 * cut, :])
     value = value + mm(kvh_ref[...], wkv_ref[2 * cut :, :])
     grads = blocks_ref[pl.ds(pl.multiple_of(pl.program_id(0) * per, per), per), :].astype(BF16)
     block = mm(grads[:, :D], wq_ref[...]) + mm(widen_keys(grads[:, D:]), wkv_ref[...])
-    value = value + jnp.broadcast_to(block[:, None, :], (per, BLOCK, D)).reshape(rows, D)
-    total[...] = value
+    out_ref[...] = value + jnp.broadcast_to(block[:, None, :], (per, BLOCK, D)).reshape(rows, D)
+
+
+def inner_gradient(gq, gkv, wt_q, wt_kv, gm, far):
+    tok = gq[0].shape[0]
+    tile = 8 * BLOCK
+    rows = lambda width: pl.BlockSpec((tile, width), lambda i: (i, 0))
+    return pl.pallas_call(
+        inner_kernel,
+        grid=(tok // tile,),
+        in_specs=[
+            *(rows(v.shape[1]) for v in (*gq, *gkv)), once((D, D)), once((2 * D, D)),
+            once(gm.shape), *(once(f.shape) for f in far),
+        ],
+        out_specs=rows(D),
+        out_shape=jax.ShapeDtypeStruct((tok, D), F32),
+        scratch_shapes=[pltpu.VMEM((tok // BLOCK, 2 * D), F32)],
+        cost_estimate=CHEAP,
+        compiler_params=vmem(),
+        name="inner_gradient",
+    )(*gq, *gkv, wt_q, wt_kv, gm, *far)
+
+
+def finish_kernel(skip, x_ref, u_ref, one_ref, two_ref, g_ref, gain_ref, out_ref, total):
+    rows = x_ref.shape[0]
+    at = lax.broadcasted_iota(jnp.int32, (rows, rows), 0)
+    lane = lax.broadcasted_iota(jnp.int32, (rows, rows), 1)
+    order = (lane == lax.rem(at, BLOCK) * 8 + at // BLOCK).astype(F32).astype(BF16)
+    total[...] = u_ref[...] + mm(order, one_ref[...].reshape(rows, D))
 
     @pl.when(pl.program_id(0) >= skip)
     def _():
@@ -1252,7 +1274,7 @@
     )
 
 
-def finish(x, gq, gkv, wt_q, wt_kv, gm, far, one, two, g_middle, gain):
+def finish(x, u, one, two, g_middle, gain):
     tok = x.shape[0]
     tile = 8 * BLOCK
     skip = (tok // BLOCK - two.shape[1]) // 8
@@ -1261,22 +1283,18 @@
         functools.partial(finish_kernel, skip),
         grid=(tok // tile,),
         in_specs=[
-            rows(D), *(rows(v.shape[1]) for v in (*gq, *gkv)), once((D, D)), once((2 * D, D)),
-            once(gm.shape), *(once(f.shape) for f in far),
+            rows(D), rows(D),
             pl.BlockSpec((BLOCK, 8, D), lambda i: (0, i, 0)),
             pl.BlockSpec((BLOCK, 8, D), lambda i: (0, jnp.maximum(i - skip, 0), 0)),
             rows(D), once((1, D)),
         ],
         out_specs=rows(D),
         out_shape=jax.ShapeDtypeStruct((tok, D), F32),
-        scratch_shapes=[
-            pltpu.VMEM((tile, D), F32),
-            pltpu.VMEM((tok // BLOCK, 2 * D), F32),
-        ],
+        scratch_shapes=[pltpu.VMEM((tile, D), F32)],
         cost_estimate=CHEAP,
         compiler_params=vmem(),
         name="finish",
-    )(x, *gq, *gkv, wt_q, wt_kv, gm, *far, one, two, g_middle, gain)
+    )(x, u, one, two, g_middle, gain)
 
 
 class Grid:
@@ -1534,26 +1552,6 @@
         twos = []
     gain_one, bias_out, gain_two, bias_in, bias_down = rows
 
-    normed, q, kv, means, means_head, means_tail = project(x, gain_one, wt_q, wt_kv, second)
-    blocked = lambda value: value.reshape(-1, BLOCK, D)
-    (kv_own,) = context_project((blocked(x),), after(gain_one, means), wt_kv, False)
-    means_send, means_head, means_tail = lax.optimization_barrier(
-        (means, means_head, means_tail, halo_one, halo_two, kv_own, *twos)
-    )[:3]
-    pieces = (
-        grid.send(means_tail, grid.along(2)),
-        grid.send(means_send, grid.along(1)),
-        means,
-        grid.send(means_send, grid.along(-1)),
-        grid.send(means_head, grid.along(-2)),
-    )
-    kv_halo, normed_halo = context_project(
-        (blocked(halo_two), blocked(halo_one)), after(gain_one, kv_own), wt_kv, True
-    )
-    if fast:
-        twos = jnp.stack(lax.optimization_barrier((*twos, *pieces, kv_halo))[:4])
-        twos = [twos] + [grid.send(twos, grid.swap_head(r)) for r in three]
-
     begin = grid.place * own
     position = begin - HALO + jnp.arange(window, dtype=jnp.int32)
     doc_ends = jnp.cumsum(doc_lengths, dtype=jnp.int32)
@@ -1567,6 +1565,26 @@
     docn = doc[:, None]
     live = (doc[HALO:context] == doc[HALO - 1 : context - 1]) & (doc[HALO:context] >= 0)
     live = jnp.repeat(live.astype(F32), BLOCK).reshape(tok // LANES, LANES)
+
+    normed, q, kv, means, means_head, means_tail = project(x, gain_one, wt_q, wt_kv, second)
+    blocked = lambda value: value.reshape(-1, BLOCK, D)
+    (kv_own,) = context_project((blocked(x),), after(gain_one, means), wt_kv, False)
+    means_send, means_head, means_tail, docn, docc, live = lax.optimization_barrier(
+        (means, means_head, means_tail, docn, docc, live, halo_one, halo_two, kv_own, *twos)
+    )[:6]
+    pieces = (
+        grid.send(means_tail, grid.along(2)),
+        grid.send(means_send, grid.along(1)),
+        means,
+        grid.send(means_send, grid.along(-1)),
+        grid.send(means_head, grid.along(-2)),
+    )
+    kv_halo, normed_halo = context_project(
+        (blocked(halo_two), blocked(halo_one)), after(gain_one, kv_own), wt_kv, True
+    )
+    if fast:
+        twos = jnp.stack(lax.optimization_barrier((*twos, *pieces, kv_halo))[:4])
+        twos = [twos] + [grid.send(twos, grid.swap_head(r)) for r in three]
 
     plan, *kept = sink_forward(pieces, after(w_pairs, kv_halo), docn, docc, own, context)
     attended, skv = attend(q, kv, kv_halo, kv_own, plan, live)
@@ -1621,12 +1639,13 @@
     if fast:
         got = grid.send(send, grid.swap_core())
         ones = split_sum(at, 1, keep, got)
-        ones = [ones[0]] + [grid.send(ones[r], grid.swap_plane(r)) for r in three]
-        ones = merge_sum(at, 0, ones)
+        waiting = [ones[0]] + [grid.send(ones[r], grid.swap_plane(r)) for r in three]
+        inner = inner_gradient((gq[0], after(gq[1], *ones)), gkv, wt_q, wt_kv, gmeans, far)
+        ones = merge_sum(at, 0, lax.optimization_barrier((*waiting, inner))[:4])
         ones = [ones[0]] + [grid.send(ones[r], grid.swap_head(r)) for r in three]
-    input_grad = finish(
-        x, gq, gkv, wt_q, wt_kv, gmeans, far, back_one, back_two, g_middle, gain_one
-    )
+    else:
+        inner = inner_gradient(gq, gkv, wt_q, wt_kv, gmeans, far)
+    input_grad = finish(x, inner, back_one, back_two, g_middle, gain_one)
     if fast:
         g_wqkv, g_sort, g_gain_one = last_one(lax.optimization_barrier((*ones, input_grad))[:4])
         g_in, g_down, g_out, *small = last_two(twos)

time: 316 us -> 308 us (0.975)
  waiting for transfers between devices: 60.6 us -> 49.2 us
  Pallas kernels: 174 us -> 179 us
    ppermute x38, waiting for transfers between devices: 60.6 us -> 49.2 us  [send(): return lax.ppermute(value, ('head', 'plane', 'core'), pairs)]
    pallas_call x0 -> x1, Pallas kernels: none -> 9.08 us  [inner_gradient(): pl.pallas_call(inner_kernel, grid=(tok // tile,), in_specs=[*(rows(v.shap...]
    pallas_call x1, Pallas kernels: 12.2 us -> 8.35 us  [finish(): pl.pallas_call(functools.partial(finish_kernel, skip), grid=(tok // tile,...]
    unnamed x72 -> x70, local copies, waits for them, and re-layouts: 7.8 us -> 7.82 us
  transfers between devices with their start and end apart: 38 -> 38, of which waited for: 14 -> 13; matrix products, arithmetic and copies ran while one was open for 1% -> 1% of each run, Pallas kernels for 40% -> 43%
where the time goes in v2:
time: 308 us; the launch traced here: 305 us
  Pallas kernels  179 us (58%)
  starting transfers between devices  61.3 us (20%)
  waiting for transfers between devices  49.2 us (16%)
  local copies, waits for them, and re-layouts  9.14 us (3%)
  other arithmetic  4.77 us (2%)
    ppermute x38, starting transfers between devices, send(): return lax.ppermute(value, ('head', 'plane', 'core'), pairs)  61.3 us
    ppermute x38, waiting for transfers between devices, send(): return lax.ppermute(value, ('head', 'plane', 'core'), pairs)  49.2 us
    pallas_call x1, Pallas kernels, feed_fast(): pl.pallas_call(feed_fast_kernel, grid=(tok // tile,), in_specs=[SMEM, til...  38.4 us
    pallas_call x2, Pallas kernels, attend_back(): pl.pallas_call(attend_back_kernel, grid=(pairs,), in_specs=[pl.BlockSpec(...  25.2 us
    pallas_call x2, Pallas kernels, context_project(): pl.pallas_call(functools.partial(context_kernel, len(values), keep), grid...  14.7 us
    pallas_call x1, Pallas kernels, attend(): pl.pallas_call(attend_kernel, grid=(PAIRS,), in_specs=[pl.BlockSpec((tok,...  12.8 us
    pallas_call x1, Pallas kernels, sink_forward(): pl.pallas_call(functools.partial(sink_forward_kernel, own, context), in_s...  12.5 us
    pallas_call x1, Pallas kernels, weight_back(): pl.pallas_call(functools.partial(weight_kernel, fast), grid=(tok // tile,...  9.89 us
  transfers between devices with their start and end apart: 38, of which 13 were waited for; matrix products, arithmetic and copies ran while one was open for 1% of the time, Pallas kernels for 43%

profile of v2, /device:TPU:12, one launch (start us, length us, event | category | flops | bytes accessed | tf_op | source)
XLA Modules:
  0.0 304.8 jit_solution(311018737868572682)
XLA Ops:
  15.8 5.3 %collective-permute-done.5 = bf16[4,208,128]{2,1,0:T(8,128)(2,1)S(1)} collective-permute-done((bf16[4,208,128]{2,1,0:T(8,128)(2,1)S(1)}, bf16[4,208,128]{2,1,0:T(8,128)(2,1)S(1)}, u32[]{:S(2)}, u32[]{:S(2)}) %collective-permute-start.5) | collective-permute-done | bytes 213024 | tf_op jit(solution)/shard_map/ppermute | solution.py:1312
  40.8 8.3 %project.1 = (bf16[1536,512]{1,0:T(8,128)(2,1)}, bf16[1536,512]{1,0:T(8,128)(2,1)}, bf16[1536,1024]{1,0:T(8,128)(2,1)}, f32[48,1536]{1,0:T(8,128)}, f32[16,1536]{1,0:T(8,128)}, /*index=5*/f32[16,1536]{1,0:T(8,128)}) custom-call(bf16[1536,512]{1,0:T(8,128)(2,1)} %bitcast.52, f32[1,512]{1,0:T(1,128)} %get-tuple-element.137.gain_ref.refs_1_.refs_2_, ...), custom_call_target="tpu_custom_call" | custom-call | tf_op jit(solution)/shard_map/project/pallas_call | solution.py:710
  49.1 6.8 %context_own.1.kvo_ref = bf16[8,48,4096]{2,1,0:T(8,128)(2,1)} custom-call(bf16[48,32,512]{2,1,0:T(8,128)(2,1)} %bitcast.53, f32[1,512]{1,0:T(1,128)} %get-tuple-element.137.gain_ref.refs_1_.refs_2_, bf16[1024,512]{1,0:T(8,128)(2,1)} %get-tuple-element.129.wkv_ref.refs_2_.refs_3_.w_ref), custom_call_target="tpu_custom_call" | custom-call | tf_op jit(solution)/shard_map/context_own/pallas_call | solution.py:354
  55.9 17.9 %collective-permute-done.7 = bf16[512,512]{1,0:T(8,128)(2,1)} collective-permute-done((bf16[512,512]{1,0:T(8,128)(2,1)}, bf16[512,512]{1,0:T(8,128)(2,1)}, u32[]{:S(2)}, u32[]{:S(2)}) %collective-permute-start.7) | collective-permute-done | bytes 524320 | tf_op jit(solution)/shard_map/ppermute | solution.py:1312
  75.8 3.9 %collective-permute-start.13 = (f32[48,1536]{1,0:T(8,128)S(1)}, f32[48,1536]{1,0:T(8,128)S(1)}, u32[]{:S(2)}, u32[]{:S(2)}) collective-permute-start(f32[48,1536]{1,0:T(8,128)S(1)} %copy-done.3), channel_id=1, source_target_pairs={{0,8},{8,16},{16,24},{24,1},{1,9},{9,17},{17,25},{25,2},{2,10},{10... | collective-permute-start | bytes 884744 | tf_op jit(solution)/shard_map/ppermute | solution.py:1312
  81.6 3.9 %collective-permute-start.15 = (f32[16,1536]{1,0:T(8,128)S(1)}, f32[16,1536]{1,0:T(8,128)S(1)}, u32[]{:S(2)}, u32[]{:S(2)}) collective-permute-start(f32[16,1536]{1,0:T(8,128)S(1)} %copy-done.32), channel_id=1, source_target_pairs={{16,0},{24,8},{1,16},{9,24},{17,1},{25,9},{2,17},{10,25},{18,2},{2... | collective-permute-start | bytes 294920 | tf_op jit(solution)/shard_map/ppermute | solution.py:1312
  85.6 7.9 %context_halo.1 = (bf16[8,64,4096]{2,1,0:T(8,128)(2,1)}, bf16[32,64,512]{2,1,0:T(8,128)(2,1)}) custom-call(bf16[16,32,512]{2,1,0:T(8,128)(2,1)} %bitcast.21.refs_0_, bf16[48,32,512]{2,1,0:T(8,128)(2,1)} %bitcast.22.refs_1_, f32[1,512]{1,0:T(1,128)} %get-tuple-element.137.gain_ref.refs_1_.refs_2_, ...), custom_call_target="tpu_custom_call" | custom-call | tf_op jit(solution)/shard_map/context_halo/pallas_call | solution.py:354
  99.2 12.5 %sink_forward.1 = (bf16[8,48,128]{2,1,0:T(8,128)(2,1)}, f32[8,8,176,128]{3,2,1,0:T(8,128)}, f32[8,8,4,128]{3,2,1,0:T(4,128)}, f32[8,176,128]{2,1,0:T(8,128)}) custom-call(f32[16,1536]{1,0:T(8,128)} %copy-done.9, f32[48,1536]{1,0:T(8,128)} %copy-done.5, f32[48,1536]{1,0:T(8,128)} %get-tuple-element.144.c.pc, f32[48,1536]{1,0:T(8,128)} %copy-done.4, ...), custom_call_target="tpu_custom_call" | custom-call | tf_op jit(solution)/shard_map/sink_forward/pallas_call | solution.py:268
  111.7 12.8 %attend.1 = (bf16[1536,512]{1,0:T(8,128)(2,1)}, bf16[1536,1024]{1,0:T(8,128)(2,1)}) custom-call(bf16[1536,512]{1,0:T(8,128)(2,1)} %get-tuple-element.130.q_ref, bf16[1536,1024]{1,0:T(8,128)(2,1)} %get-tuple-element.131.kv_ref, bf16[8,64,4096]{2,1,0:T(8,128)(2,1)} %get-tuple-element.138.kvh_ref, bf16[8,48,4096]{2,1,0:T(8,128)(2,1)} %context_own.1.kvo_ref, ...), custom_call_target="tpu_custom_call" | custom-call | tf_op jit(solution)/shard_map/attend/pallas_call | solution.py:461
  125.0 4.5 %collective-permute-done.19.other_ref = bf16[4,4,576,128]{3,2,1,0:T(8,128)(2,1)S(1)} collective-permute-done((bf16[4,4,576,128]{3,2,1,0:T(8,128)(2,1)S(1)}, bf16[4,4,576,128]{3,2,1,0:T(8,128)(2,1)S(1)}, u32[]{:S(2)}, u32[]{:S(2)}) %collective-permute-start.19) | collective-permute-done | bytes 2359328 | tf_op jit(solution)/shard_map/ppermute | solution.py:1312
  131.0 38.4 %feed.1 = (bf16[1536,512]{1,0:T(8,128)(2,1)}, f32[1536,512]{1,0:T(8,128)}, bf16[1536,512]{1,0:T(8,128)(2,1)}, bf16[4,4,592,128]{3,2,1,0:T(8,128)(2,1)}, bf16[4,4,592,128]{3,2,1,0:T(8,128)(2,1)}) custom-call(s32[3]{0:T(128)} %pad_add_fusion.1.at_ref, bf16[1536,512]{1,0:T(8,128)(2,1)} %bitcast.54, bf16[1536,512]{1,0:T(8,128)(2,1)} %get-tuple-element.152.att_ref, ...), custom_call_target="tpu_custom_call" | custom-call | tf_op jit(solution)/shard_map/feed/pallas_call | solution.py:974
  169.6 7.9 %attend_back.2 = (bf16[1536,128]{1,0:T(8,128)(2,1)}, bf16[1536,256]{1,0:T(8,128)(2,1)}, bf16[2,64,4096]{2,1,0:T(8,128)(2,1)}, f32[2,48,128]{2,1,0:T(8,128)}) custom-call(bf16[1536,512]{1,0:T(8,128)(2,1)} %get-tuple-element.130.q_ref, bf16[1536,1024]{1,0:T(8,128)(2,1)} %get-tuple-element.131.kv_ref, bf16[1536,1024]{1,0:T(8,128)(2,1)} %get-tuple-element.166.skv_ref, ...), custom_call_target="tpu_custom_call" | custom-call | tf_op jit(solution)/shard_map/attend_back/pallas_call | solution.py:584
  179.0 4.4 %split_sum.2 = (bf16[4,592,128]{2,1,0:T(8,128)(2,1)}, bf16[4,592,128]{2,1,0:T(8,128)(2,1)}, bf16[4,592,128]{2,1,0:T(8,128)(2,1)}, bf16[4,592,128]{2,1,0:T(8,128)(2,1)}) custom-call(s32[3]{0:T(128)} %pad_add_fusion.1.at_ref, bf16[4,4,592,128]{3,2,1,0:T(8,128)(2,1)} %get-tuple-element.171.keep_ref, bf16[4,4,592,128]{3,2,1,0:T(8,128)(2,1)} %copy-done.6), custom_call_target="tpu_custom_call" | custom-call | tf_op jit(solution)/shard_map/split_sum/pallas_call | solution.py:1051
  186.9 17.3 %attend_back.3 = (bf16[1536,384]{1,0:T(8,128)(2,1)}, bf16[1536,768]{1,0:T(8,128)(2,1)}, bf16[6,64,4096]{2,1,0:T(8,128)(2,1)}, f32[6,48,128]{2,1,0:T(8,128)}) custom-call(bf16[1536,512]{1,0:T(8,128)(2,1)} %get-tuple-element.130.q_ref, bf16[1536,1024]{1,0:T(8,128)(2,1)} %get-tuple-element.131.kv_ref, bf16[1536,1024]{1,0:T(8,128)(2,1)} %get-tuple-element.166.skv_ref, ...), custom_call_target="tpu_custom_call" | custom-call | tf_op jit(solution)/shard_map/attend_back/pallas_call | solution.py:584
  204.2 9.2 %sink_backward.1 = (f32[176,1024]{1,0:T(8,128)}, f32[4,64,128]{2,1,0:T(8,128)}, bf16[48,1024]{1,0:T(8,128)(2,1)}, bf16[16,1024]{1,0:T(8,128)(2,1)}) custom-call(f32[16,1536]{1,0:T(8,128)} %copy-done.9, f32[48,1536]{1,0:T(8,128)} %copy-done.5, f32[48,1536]{1,0:T(8,128)} %get-tuple-element.144.c.pc, f32[48,1536]{1,0:T(8,128)} %copy-done.4, ...), custom_call_target="tpu_custom_call" | custom-call | tf_op jit(solution)/shard_map/sink_backward/pallas_call | solution.py:293
  220.8 9.2 %halo_back.1 = (bf16[32,16,512]{2,1,0:T(8,128)(2,1)}, bf16[32,48,512]{2,1,0:T(8,128)(2,1)}, f32[1024,512]{1,0:T(8,128)}) custom-call(bf16[2,64,4096]{2,1,0:T(8,128)(2,1)} %get-tuple-element.170.low_ref, bf16[6,64,4096]{2,1,0:T(8,128)(2,1)} %get-tuple-element.197.high_ref, bf16[32,64,512]{2,1,0:T(8,128)(2,1)} %get-tuple-element.198.nh_ref, ...), custom_call_target="tpu_custom_call" | custom-call | tf_op jit(solution)/shard_map/halo_back/pallas_call | solution.py:651
  234.7 3.9 %collective-permute-done.25.fe = bf16[16,1024]{1,0:T(8,128)(2,1)S(1)} collective-permute-done((bf16[16,1024]{1,0:T(8,128)(2,1)S(1)}, bf16[16,1024]{1,0:T(8,128)(2,1)S(1)}, u32[]{:S(2)}, u32[]{:S(2)}) %collective-permute-start.25) | collective-permute-done | bytes 32800 | tf_op jit(solution)/shard_map/ppermute | solution.py:1312
  238.6 4.5 %collective-permute-start.30 = (bf16[32,48,512]{2,1,0:T(8,128)(2,1)}, bf16[32,48,512]{2,1,0:T(8,128)(2,1)S(1)}, u32[]{:S(2)}, u32[]{:S(2)}) collective-permute-start(bf16[32,48,512]{2,1,0:T(8,128)(2,1)} %get-tuple-element.205), channel_id=1, source_target_pairs={{8,0},{16,8},{24,16},{1,24},{9,1},{17,9},{25,17},{2,25},{10,2},{18... | collective-permute-start | bytes 4718600 | tf_op jit(solution)/shard_map/ppermute | solution.py:1312
  243.1 9.9 %weight_back.1 = (bf16[4,4,208,128]{3,2,1,0:T(8,128)(2,1)}, bf16[4,4,208,128]{3,2,1,0:T(8,128)(2,1)}) custom-call(s32[3]{0:T(128)} %pad_add_fusion.1.at_ref, bf16[1536,128]{1,0:T(8,128)(2,1)} %get-tuple-element.168.ql_ref, bf16[1536,384]{1,0:T(8,128)(2,1)} %get-tuple-element.215.qh_ref, bf16[1536,256]{1,0:T(8,128)(2,1)} %get-tuple-element.179.kvl_ref, ...), custom_call_target="tpu_custom_call" | custom-call | tf_op jit(solution)/shard_map/weight_back/pallas_call | solution.py:1193
  263.7 9.1 %inner_gradient.1.u_ref = f32[1536,512]{1,0:T(8,128)} custom-call(bf16[1536,128]{1,0:T(8,128)(2,1)} %get-tuple-element.168.ql_ref, bf16[1536,384]{1,0:T(8,128)(2,1)} %get-tuple-element.215.qh_ref, bf16[1536,256]{1,0:T(8,128)(2,1)} %get-tuple-element.179.kvl_ref, bf16[1536,768]{1,0:T(8,128)(2,1)} %get-tuple-element.180.kvh_ref, ...), custom_call_target="tpu_custom_call" | custom-call | tf_op jit(solution)/shard_map/inner_gradient/pallas_call | solution.py:1239
  272.7 4.4 %collective-permute-done.33.c_ref = bf16[4,208,128]{2,1,0:T(8,128)(2,1)S(1)} collective-permute-done((bf16[4,208,128]{2,1,0:T(8,128)(2,1)}, bf16[4,208,128]{2,1,0:T(8,128)(2,1)S(1)}, u32[]{:S(2)}, u32[]{:S(2)}) %collective-permute-start.33) | collective-permute-done | bytes 213024 | tf_op jit(solution)/shard_map/ppermute | solution.py:1312
  277.1 5.5 %collective-permute-done.34.d_ref = bf16[4,208,128]{2,1,0:T(8,128)(2,1)S(1)} collective-permute-done((bf16[4,208,128]{2,1,0:T(8,128)(2,1)}, bf16[4,208,128]{2,1,0:T(8,128)(2,1)S(1)}, u32[]{:S(2)}, u32[]{:S(2)}) %collective-permute-start.34) | collective-permute-done | bytes 213024 | tf_op jit(solution)/shard_map/ppermute | solution.py:1312
  285.3 4.2 %collective-permute-start.36 = (bf16[208,128]{1,0:T(8,128)(2,1)}, bf16[208,128]{1,0:T(8,128)(2,1)S(1)}, u32[]{:S(2)}, u32[]{:S(2)}) collective-permute-start(bf16[208,128]{1,0:T(8,128)(2,1)} %get-tuple-element.224), channel_id=1, source_target_pairs={{0,16},{1,17},{2,18},{3,19},{4,20},{5,21},{6,22},{7,23},{8,24},{9,... | collective-permute-start | bytes 159752 | tf_op jit(solution)/shard_map/ppermute | solution.py:1312
  294.2 8.3 %finish.1 = f32[1536,512]{1,0:T(8,128)} custom-call(bf16[1536,512]{1,0:T(8,128)(2,1)} %bitcast.55, f32[1536,512]{1,0:T(8,128)} %inner_gradient.1.u_ref, bf16[32,48,512]{2,1,0:T(8,128)(2,1)} %copy-done.8, bf16[32,16,512]{2,1,0:T(8,128)(2,1)} %copy-done.16, f32[1536,512]{1,0:T(8,128)} %get-tuple-element.217.g_ref, ...), custom_call_target="tpu_custom_call" | custom-call | tf_op jit(solution)/shard_map/finish/pallas_call | solution.py:1282
  (165 shorter events, 83.4 us)
Async XLA Ops:
  23.4 50.4 %collective-permute-start.8 = (bf16[1536,512]{1,0:T(8,128)(2,1)S(1)}, bf16[1536,512]{1,0:T(8,128)(2,1)}, u32[]{:S(2)}, u32[]{:S(2)}) collective-permute-start(bf16[1536,512]{1,0:T(8,128)(2,1)S(1)} %bitcast.56), channel_id=1, source_target_pairs={{0,8},{8,16},{16,24},{24,1},{1,9},{9,17},{17,25},{25,2},{2,10},{10... | collective-permute-start | bytes 4718600 | tf_op jit(solution)/shard_map/ppermute | solution.py:1312
  26.8 47.0 %collective-permute-start.7 = (bf16[512,512]{1,0:T(8,128)(2,1)}, bf16[512,512]{1,0:T(8,128)(2,1)}, u32[]{:S(2)}, u32[]{:S(2)}) collective-permute-start(bf16[512,512]{1,0:T(8,128)(2,1)} %get-tuple-element.133), channel_id=1, source_target_pairs={{0,16},{8,24},{16,1},{24,9},{1,17},{9,25},{17,2},{25,10},{2,18},{1... | collective-permute-start | bytes 1572872 | tf_op jit(solution)/shard_map/ppermute | solution.py:1312
  31.0 42.8 %collective-permute-start.11 = (bf16[576,128]{1,0:T(8,128)(2,1)S(1)}, bf16[576,128]{1,0:T(8,128)(2,1)}, u32[]{:S(2)}, u32[]{:S(2)}) collective-permute-start(bf16[576,128]{1,0:T(8,128)(2,1)S(1)} %copy-done.23), channel_id=1, source_target_pairs={{0,6},{1,7},{2,4},{3,5},{4,2},{5,3},{6,0},{7,1},{8,14},{9,15},{10,... | collective-permute-start | bytes 442376 | tf_op jit(solution)/shard_map/ppermute | solution.py:1312
  32.1 41.7 %collective-permute-start.10 = (bf16[576,128]{1,0:T(8,128)(2,1)S(1)}, bf16[576,128]{1,0:T(8,128)(2,1)}, u32[]{:S(2)}, u32[]{:S(2)}) collective-permute-start(bf16[576,128]{1,0:T(8,128)(2,1)S(1)} %copy-done.23), channel_id=1, source_target_pairs={{0,4},{1,5},{2,6},{3,7},{4,0},{5,1},{6,2},{7,3},{8,12},{9,13},{10,... | collective-permute-start | bytes 442376 | tf_op jit(solution)/shard_map/ppermute | solution.py:1312
  35.9 37.9 %collective-permute-start.9 = (bf16[576,128]{1,0:T(8,128)(2,1)S(1)}, bf16[576,128]{1,0:T(8,128)(2,1)}, u32[]{:S(2)}, u32[]{:S(2)}) collective-permute-start(bf16[576,128]{1,0:T(8,128)(2,1)S(1)} %copy-done.23), channel_id=1, source_target_pairs={{0,2},{1,3},{2,0},{3,1},{4,6},{5,7},{6,4},{7,5},{8,10},{9,11},{10,... | collective-permute-start | bytes 442376 | tf_op jit(solution)/shard_map/ppermute | solution.py:1312
  73.8 20.4 %collective-permute-start.14 = (f32[48,1536]{1,0:T(8,128)S(1)}, f32[48,1536]{1,0:T(8,128)S(1)}, u32[]{:S(2)}, u32[]{:S(2)}) collective-permute-start(f32[48,1536]{1,0:T(8,128)S(1)} %copy-done.3), channel_id=1, source_target_pairs={{8,0},{16,8},{24,16},{1,24},{9,1},{17,9},{25,17},{2,25},{10,2},{18... | collective-permute-start | bytes 884744 | tf_op jit(solution)/shard_map/ppermute | solution.py:1312
  75.8 18.5 %collective-permute-start.13 = (f32[48,1536]{1,0:T(8,128)S(1)}, f32[48,1536]{1,0:T(8,128)S(1)}, u32[]{:S(2)}, u32[]{:S(2)}) collective-permute-start(f32[48,1536]{1,0:T(8,128)S(1)} %copy-done.3), channel_id=1, source_target_pairs={{0,8},{8,16},{16,24},{24,1},{1,9},{9,17},{17,25},{25,2},{2,10},{10... | collective-permute-start | bytes 884744 | tf_op jit(solution)/shard_map/ppermute | solution.py:1312
  79.7 14.4 %collective-permute-start.12 = (f32[16,1536]{1,0:T(8,128)S(1)}, f32[16,1536]{1,0:T(8,128)S(1)}, u32[]{:S(2)}, u32[]{:S(2)}) collective-permute-start(f32[16,1536]{1,0:T(8,128)S(1)} %copy-done.33), channel_id=1, source_target_pairs={{0,16},{8,24},{16,1},{24,9},{1,17},{9,25},{17,2},{25,10},{2,18},{1... | collective-permute-start | bytes 294920 | tf_op jit(solution)/shard_map/ppermute | solution.py:1312
  95.6 28.9 %collective-permute-start.18 = (bf16[4,576,128]{2,1,0:T(8,128)(2,1)S(1)}, bf16[4,576,128]{2,1,0:T(8,128)(2,1)S(1)}, u32[]{:S(2)}, u32[]{:S(2)}) collective-permute-start(bf16[4,576,128]{2,1,0:T(8,128)(2,1)S(1)} %pad_maximum_fusion.2), channel_id=1, source_target_pairs={{0,24},{1,25},{2,26},{3,27},{4,28},{5,29},{6,30},{7,31},{8,16},{9,... | collective-permute-start | bytes 1769480 | tf_op jit(solution)/shard_map/ppermute | solution.py:1312
  96.5 28.1 %collective-permute-start.17 = (bf16[4,576,128]{2,1,0:T(8,128)(2,1)S(1)}, bf16[4,576,128]{2,1,0:T(8,128)(2,1)S(1)}, u32[]{:S(2)}, u32[]{:S(2)}) collective-permute-start(bf16[4,576,128]{2,1,0:T(8,128)(2,1)S(1)} %pad_maximum_fusion.2), channel_id=1, source_target_pairs={{0,16},{1,17},{2,18},{3,19},{4,20},{5,21},{6,22},{7,23},{8,24},{9,... | collective-permute-start | bytes 1769480 | tf_op jit(solution)/shard_map/ppermute | solution.py:1312
  96.5 28.1 %collective-permute-start.16 = (bf16[4,576,128]{2,1,0:T(8,128)(2,1)S(1)}, bf16[4,576,128]{2,1,0:T(8,128)(2,1)S(1)}, u32[]{:S(2)}, u32[]{:S(2)}) collective-permute-start(bf16[4,576,128]{2,1,0:T(8,128)(2,1)S(1)} %pad_maximum_fusion.2), channel_id=1, source_target_pairs={{0,8},{1,9},{2,10},{3,11},{4,12},{5,13},{6,14},{7,15},{8,0},{9,1},... | collective-permute-start | bytes 1769480 | tf_op jit(solution)/shard_map/ppermute | solution.py:1312
  183.4 30.0 %collective-permute-start.21 = (bf16[4,592,128]{2,1,0:T(8,128)(2,1)}, bf16[4,592,128]{2,1,0:T(8,128)(2,1)S(1)}, u32[]{:S(2)}, u32[]{:S(2)}) collective-permute-start(bf16[4,592,128]{2,1,0:T(8,128)(2,1)} %get-tuple-element.174), channel_id=1, source_target_pairs={{0,8},{1,9},{2,10},{3,11},{4,12},{5,13},{6,14},{7,15},{8,0},{9,1},... | collective-permute-start | bytes 1818632 | tf_op jit(solution)/shard_map/ppermute | solution.py:1312
  183.5 30.0 %collective-permute-start.22 = (bf16[4,592,128]{2,1,0:T(8,128)(2,1)}, bf16[4,592,128]{2,1,0:T(8,128)(2,1)S(1)}, u32[]{:S(2)}, u32[]{:S(2)}) collective-permute-start(bf16[4,592,128]{2,1,0:T(8,128)(2,1)} %get-tuple-element.175), channel_id=1, source_target_pairs={{0,16},{1,17},{2,18},{3,19},{4,20},{5,21},{6,22},{7,23},{8,24},{9,... | collective-permute-start | bytes 1818632 | tf_op jit(solution)/shard_map/ppermute | solution.py:1312
  184.8 28.6 %collective-permute-start.23 = (bf16[4,592,128]{2,1,0:T(8,128)(2,1)}, bf16[4,592,128]{2,1,0:T(8,128)(2,1)S(1)}, u32[]{:S(2)}, u32[]{:S(2)}) collective-permute-start(bf16[4,592,128]{2,1,0:T(8,128)(2,1)} %get-tuple-element.176), channel_id=1, source_target_pairs={{0,24},{1,25},{2,26},{3,27},{4,28},{5,29},{6,30},{7,31},{8,16},{9,... | collective-permute-start | bytes 1818632 | tf_op jit(solution)/shard_map/ppermute | solution.py:1312
  217.4 21.2 %collective-permute-start.26 = (bf16[592,128]{1,0:T(8,128)(2,1)}, bf16[592,128]{1,0:T(8,128)(2,1)S(1)}, u32[]{:S(2)}, u32[]{:S(2)}) collective-permute-start(bf16[592,128]{1,0:T(8,128)(2,1)} %get-tuple-element.194), channel_id=1, source_target_pairs={{0,2},{1,3},{2,0},{3,1},{4,6},{5,7},{6,4},{7,5},{8,10},{9,11},{10,... | collective-permute-start | bytes 454664 | tf_op jit(solution)/shard_map/ppermute | solution.py:1312
  218.4 20.2 %collective-permute-start.27 = (bf16[592,128]{1,0:T(8,128)(2,1)}, bf16[592,128]{1,0:T(8,128)(2,1)S(1)}, u32[]{:S(2)}, u32[]{:S(2)}) collective-permute-start(bf16[592,128]{1,0:T(8,128)(2,1)} %get-tuple-element.195), channel_id=1, source_target_pairs={{0,4},{1,5},{2,6},{3,7},{4,0},{5,1},{6,2},{7,3},{8,12},{9,13},{10,... | collective-permute-start | bytes 454664 | tf_op jit(solution)/shard_map/ppermute | solution.py:1312
  219.2 19.4 %collective-permute-start.28 = (bf16[592,128]{1,0:T(8,128)(2,1)}, bf16[592,128]{1,0:T(8,128)(2,1)S(1)}, u32[]{:S(2)}, u32[]{:S(2)}) collective-permute-start(bf16[592,128]{1,0:T(8,128)(2,1)} %get-tuple-element.196), channel_id=1, source_target_pairs={{0,6},{1,7},{2,4},{3,5},{4,2},{5,3},{6,0},{7,1},{8,14},{9,15},{10,... | collective-permute-start | bytes 454664 | tf_op jit(solution)/shard_map/ppermute | solution.py:1312
  238.6 54.2 %collective-permute-start.30 = (bf16[32,48,512]{2,1,0:T(8,128)(2,1)}, bf16[32,48,512]{2,1,0:T(8,128)(2,1)S(1)}, u32[]{:S(2)}, u32[]{:S(2)}) collective-permute-start(bf16[32,48,512]{2,1,0:T(8,128)(2,1)} %get-tuple-element.205), channel_id=1, source_target_pairs={{8,0},{16,8},{24,16},{1,24},{9,1},{17,9},{25,17},{2,25},{10,2},{18... | collective-permute-start | bytes 4718600 | tf_op jit(solution)/shard_map/ppermute | solution.py:1312
  253.1 39.7 %collective-permute-start.31 = (bf16[32,16,512]{2,1,0:T(8,128)(2,1)S(1)}, bf16[32,16,512]{2,1,0:T(8,128)(2,1)S(1)}, u32[]{:S(2)}, u32[]{:S(2)}) collective-permute-start(bf16[32,16,512]{2,1,0:T(8,128)(2,1)S(1)} %copy-done.30), channel_id=1, source_target_pairs={{16,0},{24,8},{1,16},{9,24},{17,1},{25,9},{2,17},{10,25},{18,2},{2... | collective-permute-start | bytes 1572872 | tf_op jit(solution)/shard_map/ppermute | solution.py:1312
  260.6 16.5 %collective-permute-start.33 = (bf16[4,208,128]{2,1,0:T(8,128)(2,1)}, bf16[4,208,128]{2,1,0:T(8,128)(2,1)S(1)}, u32[]{:S(2)}, u32[]{:S(2)}) collective-permute-start(bf16[4,208,128]{2,1,0:T(8,128)(2,1)} %get-tuple-element.213), channel_id=1, source_target_pairs={{0,4},{1,5},{2,6},{3,7},{4,0},{5,1},{6,2},{7,3},{8,12},{9,13},{10,... | collective-permute-start | bytes 638984 | tf_op jit(solution)/shard_map/ppermute | solution.py:1312
  262.0 20.6 %collective-permute-start.34 = (bf16[4,208,128]{2,1,0:T(8,128)(2,1)}, bf16[4,208,128]{2,1,0:T(8,128)(2,1)S(1)}, u32[]{:S(2)}, u32[]{:S(2)}) collective-permute-start(bf16[4,208,128]{2,1,0:T(8,128)(2,1)} %get-tuple-element.214), channel_id=1, source_target_pairs={{0,6},{1,7},{2,4},{3,5},{4,2},{5,3},{6,0},{7,1},{8,14},{9,15},{10,... | collective-permute-start | bytes 638984 | tf_op jit(solution)/shard_map/ppermute | solution.py:1312
  285.3 17.2 %collective-permute-start.35 = (bf16[208,128]{1,0:T(8,128)(2,1)}, bf16[208,128]{1,0:T(8,128)(2,1)S(1)}, u32[]{:S(2)}, u32[]{:S(2)}) collective-permute-start(bf16[208,128]{1,0:T(8,128)(2,1)} %get-tuple-element.223), channel_id=1, source_target_pairs={{0,8},{1,9},{2,10},{3,11},{4,12},{5,13},{6,14},{7,15},{8,0},{9,1},... | collective-permute-start | bytes 159752 | tf_op jit(solution)/shard_map/ppermute | solution.py:1312
  285.3 17.3 %collective-permute-start.36 = (bf16[208,128]{1,0:T(8,128)(2,1)}, bf16[208,128]{1,0:T(8,128)(2,1)S(1)}, u32[]{:S(2)}, u32[]{:S(2)}) collective-permute-start(bf16[208,128]{1,0:T(8,128)(2,1)} %get-tuple-element.224), channel_id=1, source_target_pairs={{0,16},{1,17},{2,18},{3,19},{4,20},{5,21},{6,22},{7,23},{8,24},{9,... | collective-permute-start | bytes 159752 | tf_op jit(solution)/shard_map/ppermute | solution.py:1312
  289.5 13.0 %collective-permute-start.37 = (bf16[208,128]{1,0:T(8,128)(2,1)}, bf16[208,128]{1,0:T(8,128)(2,1)S(1)}, u32[]{:S(2)}, u32[]{:S(2)}) collective-permute-start(bf16[208,128]{1,0:T(8,128)(2,1)} %get-tuple-element.225), channel_id=1, source_target_pairs={{0,24},{1,25},{2,26},{3,27},{4,28},{5,29},{6,30},{7,31},{8,16},{9,... | collective-permute-start | bytes 159752 | tf_op jit(solution)/shard_map/ppermute | solution.py:1312
  (49 other events, 430.8 us)

commit v3 on v2

--- a/solution.py
+++ b/solution.py
@@ -322,9 +322,12 @@
 
 def context_kernel(count, keep, *refs):
     gain_ref, w_ref, kvx_ref = refs[count : count + 3]
-    x = jnp.concatenate([ref[...] for ref in refs[:count]], axis=0)
+    x = jnp.concatenate([ref[...].astype(F32) for ref in refs[:count]], axis=0)
+    short = -x.shape[0] % 16
+    if short:
+        x = jnp.concatenate([jnp.zeros((short, 8, D), F32), x], axis=0)
     blocks = x.shape[0]
-    normed = normalise(x.astype(F32)) * gain_ref[...].reshape(1, 1, D)
+    normed = normalise(x) * gain_ref[...].reshape(1, 1, D)
     normed = normed.astype(BF16).reshape(blocks * 8, D)
     row = lax.broadcasted_iota(jnp.int32, (LANES, LANES), 0)
     lane = lax.broadcasted_iota(jnp.int32, (LANES, LANES), 1)
@@ -350,6 +353,7 @@
 
 def context_project(values, gain, w_kv, keep):
     blocks = sum(v.shape[0] for v in values)
+    blocks += -blocks % 16
     outs = 2 if keep else 1
     return pl.pallas_call(
         functools.partial(context_kernel, len(values), keep),
@@ -755,7 +759,7 @@
     wqkv_ref, wsort_ref, g1, bo, g2, bi, bd, win_ref, wdown_ref, wout_ref, x_ref,
     one_ref, two_ref, tail_ref,
 ):
-    tail_ref[...] = x_ref[...]
+    tail_ref[...] = x_ref[x_ref.shape[0] - tail_ref.shape[0] :, :]
     one_ref[:192, :] = wqkv_ref[...]
     row = place(g1[...], 0) + place(bo[...], 16) + place(g2[...], 32)
     row = row + place(bi[...], 48) + place(bd[...], 112)
@@ -767,11 +771,12 @@
 
 
 def pack(w_qkv, w_sort, vectors, w_in, w_down, w_out, x, tail):
-    last = x.shape[0] // tail - 1
+    most = 512
+    last = x.shape[0] // most - 1
     return pl.pallas_call(
         pack_kernel,
         grid=(1,),
-        in_specs=[VMEM] * 10 + [pl.BlockSpec((tail, D), lambda i: (last, 0))],
+        in_specs=[VMEM] * 10 + [pl.BlockSpec((most, D), lambda i: (last, 0))],
         out_shape=[
             jax.ShapeDtypeStruct((PIECE_ONE, LANES), BF16),
             jax.ShapeDtypeStruct((PIECE_TWO, LANES), BF16),
@@ -1042,17 +1047,18 @@
 def split_kernel(which, at_ref, keep_ref, got_ref, *outs):
     for r, out in enumerate(outs):
         i = at_ref[which] ^ r
-        out[0] = (keep_ref[i, 0].astype(F32) + got_ref[i, 0].astype(F32)).astype(BF16)
+        out[...] = (keep_ref[i].astype(F32) + got_ref[i].astype(F32)).astype(BF16)
 
 
 def split_sum(at, which, keep, got):
     one, two, rows, lanes = keep.shape
-    block = pl.BlockSpec((one, 1, rows, lanes), lambda i: (0, i, 0, 0))
+    per = 1 if rows > 400 else 2
+    block = pl.BlockSpec((one, per, rows, lanes), lambda i: (0, i, 0, 0))
     return pl.pallas_call(
         functools.partial(split_kernel, which),
-        grid=(two,),
+        grid=(two // per,),
         in_specs=[SMEM, block, block],
-        out_specs=[pl.BlockSpec((1, rows, lanes), lambda i: (i, 0, 0))] * one,
+        out_specs=[pl.BlockSpec((per, rows, lanes), lambda i: (i, 0, 0))] * one,
         out_shape=[jax.ShapeDtypeStruct((two, rows, lanes), BF16)] * one,
         cost_estimate=CHEAP,
         compiler_params=vmem(),
@@ -1530,7 +1536,7 @@
     parameters = (w_qkv, w_sort, w_in, w_down, w_out)
 
     three = range(1, 4)
-    tail = second * BLOCK
+    tail = (DOC_MOST - 1 - own) * BLOCK
     if fast:
         one, two, x_tail = pack(w_qkv, w_sort, vectors, w_in, w_down, w_out, x, tail)
         ones = [one] + [grid.send(one, grid.swap_plane(r)) for r in three]

time: 308 us -> 306 us (level)
  waiting for transfers between devices: 49.2 us -> 45.5 us
    ppermute x38, waiting for transfers between devices: 49.2 us -> 45.5 us  [send(): return lax.ppermute(value, ('head', 'plane', 'core'), pairs)]
  transfers between devices with their start and end apart: 38 -> 38, of which waited for: 13 -> 13; matrix products, arithmetic and copies ran while one was open for 1% -> 2% of each run, Pallas kernels for 43% -> 42%
where the time goes in v3:
time: 306 us; the launch traced here: 303 us
  Pallas kernels  178 us (58%)
  starting transfers between devices  62.5 us (20%)
  waiting for transfers between devices  45.5 us (15%)
  local copies, waits for them, and re-layouts  10.2 us (3%)
  other arithmetic  5.51 us (2%)
    ppermute x38, starting transfers between devices, send(): return lax.ppermute(value, ('head', 'plane', 'core'), pairs)  62.5 us
    ppermute x38, waiting for transfers between devices, send(): return lax.ppermute(value, ('head', 'plane', 'core'), pairs)  45.5 us
    pallas_call x1, Pallas kernels, feed_fast(): pl.pallas_call(feed_fast_kernel, grid=(tok // tile,), in_specs=[SMEM, til...  38.4 us
    pallas_call x2, Pallas kernels, attend_back(): pl.pallas_call(attend_back_kernel, grid=(pairs,), in_specs=[pl.BlockSpec(...  25.2 us
    pallas_call x2, Pallas kernels, context_project(): pl.pallas_call(functools.partial(context_kernel, len(values), keep), grid...  14.7 us
    pallas_call x1, Pallas kernels, attend(): pl.pallas_call(attend_kernel, grid=(PAIRS,), in_specs=[pl.BlockSpec((tok,...  12.8 us
    pallas_call x1, Pallas kernels, sink_forward(): pl.pallas_call(functools.partial(sink_forward_kernel, own, context), in_s...  12.5 us
    pallas_call x1, Pallas kernels, weight_back(): pl.pallas_call(functools.partial(weight_kernel, fast), grid=(tok // tile,...  9.89 us
  transfers between devices with their start and end apart: 38, of which 13 were waited for; matrix products, arithmetic and copies ran while one was open for 2% of the time, Pallas kernels for 42%

profile of v3, /device:TPU:12, one launch (start us, length us, event | category | flops | bytes accessed | tf_op | source)
XLA Modules:
  0.0 302.6 jit_solution(3210810732997021084)
XLA Ops:
  15.8 5.3 %collective-permute-done.5 = bf16[4,208,128]{2,1,0:T(8,128)(2,1)S(1)} collective-permute-done((bf16[4,208,128]{2,1,0:T(8,128)(2,1)S(1)}, bf16[4,208,128]{2,1,0:T(8,128)(2,1)S(1)}, u32[]{:S(2)}, u32[]{:S(2)}) %collective-permute-start.5) | collective-permute-done | bytes 213024 | tf_op jit(solution)/shard_map/ppermute | solution.py:1318
  42.4 8.3 %project.1 = (bf16[1536,512]{1,0:T(8,128)(2,1)}, bf16[1536,512]{1,0:T(8,128)(2,1)}, bf16[1536,1024]{1,0:T(8,128)(2,1)}, f32[48,1536]{1,0:T(8,128)}, f32[16,1536]{1,0:T(8,128)}, /*index=5*/f32[16,1536]{1,0:T(8,128)}) custom-call(bf16[1536,512]{1,0:T(8,128)(2,1)} %bitcast.52, f32[1,512]{1,0:T(1,128)} %get-tuple-element.137.gain_ref.refs_1_.refs_2_, ...), custom_call_target="tpu_custom_call" | custom-call | tf_op jit(solution)/shard_map/project/pallas_call | solution.py:714
  50.8 6.8 %context_own.1.kvo_ref = bf16[8,48,4096]{2,1,0:T(8,128)(2,1)} custom-call(bf16[48,32,512]{2,1,0:T(8,128)(2,1)} %bitcast.53, f32[1,512]{1,0:T(1,128)} %get-tuple-element.137.gain_ref.refs_1_.refs_2_, bf16[1024,512]{1,0:T(8,128)(2,1)} %get-tuple-element.129.wkv_ref.refs_2_.refs_3_.w_ref), custom_call_target="tpu_custom_call" | custom-call | tf_op jit(solution)/shard_map/context_own/pallas_call | solution.py:358
  57.6 14.1 %collective-permute-done.7 = bf16[416,512]{1,0:T(8,128)(2,1)} collective-permute-done((bf16[416,512]{1,0:T(8,128)(2,1)}, bf16[416,512]{1,0:T(8,128)(2,1)}, u32[]{:S(2)}, u32[]{:S(2)}) %collective-permute-start.7) | collective-permute-done | bytes 426016 | tf_op jit(solution)/shard_map/ppermute | solution.py:1318
  73.6 3.9 %collective-permute-start.13 = (f32[48,1536]{1,0:T(8,128)S(1)}, f32[48,1536]{1,0:T(8,128)S(1)}, u32[]{:S(2)}, u32[]{:S(2)}) collective-permute-start(f32[48,1536]{1,0:T(8,128)S(1)} %copy-done.3), channel_id=1, source_target_pairs={{0,8},{8,16},{16,24},{24,1},{1,9},{9,17},{17,25},{25,2},{2,10},{10... | collective-permute-start | bytes 884744 | tf_op jit(solution)/shard_map/ppermute | solution.py:1318
  79.5 3.9 %collective-permute-start.15 = (f32[16,1536]{1,0:T(8,128)S(1)}, f32[16,1536]{1,0:T(8,128)S(1)}, u32[]{:S(2)}, u32[]{:S(2)}) collective-permute-start(f32[16,1536]{1,0:T(8,128)S(1)} %copy-done.32), channel_id=1, source_target_pairs={{16,0},{24,8},{1,16},{9,24},{17,1},{25,9},{2,17},{10,25},{18,2},{2... | collective-permute-start | bytes 294920 | tf_op jit(solution)/shard_map/ppermute | solution.py:1318
  83.4 7.9 %context_halo.1 = (bf16[8,64,4096]{2,1,0:T(8,128)(2,1)}, bf16[32,64,512]{2,1,0:T(8,128)(2,1)}) custom-call(bf16[13,32,512]{2,1,0:T(8,128)(2,1)} %bitcast.21.refs_0_, bf16[48,32,512]{2,1,0:T(8,128)(2,1)} %bitcast.22.refs_1_, f32[1,512]{1,0:T(1,128)} %get-tuple-element.137.gain_ref.refs_1_.refs_2_, ...), custom_call_target="tpu_custom_call" | custom-call | tf_op jit(solution)/shard_map/context_halo/pallas_call | solution.py:358
  97.0 12.5 %sink_forward.1 = (bf16[8,48,128]{2,1,0:T(8,128)(2,1)}, f32[8,8,176,128]{3,2,1,0:T(8,128)}, f32[8,8,4,128]{3,2,1,0:T(4,128)}, f32[8,176,128]{2,1,0:T(8,128)}) custom-call(f32[16,1536]{1,0:T(8,128)} %copy-done.9, f32[48,1536]{1,0:T(8,128)} %copy-done.5, f32[48,1536]{1,0:T(8,128)} %get-tuple-element.144.c.pc, f32[48,1536]{1,0:T(8,128)} %copy-done.4, ...), custom_call_target="tpu_custom_call" | custom-call | tf_op jit(solution)/shard_map/sink_forward/pallas_call | solution.py:268
  109.6 12.8 %attend.1 = (bf16[1536,512]{1,0:T(8,128)(2,1)}, bf16[1536,1024]{1,0:T(8,128)(2,1)}) custom-call(bf16[1536,512]{1,0:T(8,128)(2,1)} %get-tuple-element.130.q_ref, bf16[1536,1024]{1,0:T(8,128)(2,1)} %get-tuple-element.131.kv_ref, bf16[8,64,4096]{2,1,0:T(8,128)(2,1)} %get-tuple-element.138.kvh_ref, bf16[8,48,4096]{2,1,0:T(8,128)(2,1)} %context_own.1.kvo_ref, ...), custom_call_target="tpu_custom_call" | custom-call | tf_op jit(solution)/shard_map/attend/pallas_call | solution.py:465
  122.8 4.5 %collective-permute-done.19.other_ref = bf16[4,4,576,128]{3,2,1,0:T(8,128)(2,1)S(1)} collective-permute-done((bf16[4,4,576,128]{3,2,1,0:T(8,128)(2,1)S(1)}, bf16[4,4,576,128]{3,2,1,0:T(8,128)(2,1)S(1)}, u32[]{:S(2)}, u32[]{:S(2)}) %collective-permute-start.19) | collective-permute-done | bytes 2359328 | tf_op jit(solution)/shard_map/ppermute | solution.py:1318
  128.9 38.4 %feed.1 = (bf16[1536,512]{1,0:T(8,128)(2,1)}, f32[1536,512]{1,0:T(8,128)}, bf16[1536,512]{1,0:T(8,128)(2,1)}, bf16[4,4,592,128]{3,2,1,0:T(8,128)(2,1)}, bf16[4,4,592,128]{3,2,1,0:T(8,128)(2,1)}) custom-call(s32[3]{0:T(128)} %pad_add_fusion.1.at_ref, bf16[1536,512]{1,0:T(8,128)(2,1)} %bitcast.54, bf16[1536,512]{1,0:T(8,128)(2,1)} %get-tuple-element.152.att_ref, ...), custom_call_target="tpu_custom_call" | custom-call | tf_op jit(solution)/shard_map/feed/pallas_call | solution.py:979
  167.5 7.9 %attend_back.2 = (bf16[1536,128]{1,0:T(8,128)(2,1)}, bf16[1536,256]{1,0:T(8,128)(2,1)}, bf16[2,64,4096]{2,1,0:T(8,128)(2,1)}, f32[2,48,128]{2,1,0:T(8,128)}) custom-call(bf16[1536,512]{1,0:T(8,128)(2,1)} %get-tuple-element.130.q_ref, bf16[1536,1024]{1,0:T(8,128)(2,1)} %get-tuple-element.131.kv_ref, bf16[1536,1024]{1,0:T(8,128)(2,1)} %get-tuple-element.166.skv_ref, ...), custom_call_target="tpu_custom_call" | custom-call | tf_op jit(solution)/shard_map/attend_back/pallas_call | solution.py:588
  176.9 4.4 %split_sum.2 = (bf16[4,592,128]{2,1,0:T(8,128)(2,1)}, bf16[4,592,128]{2,1,0:T(8,128)(2,1)}, bf16[4,592,128]{2,1,0:T(8,128)(2,1)}, bf16[4,592,128]{2,1,0:T(8,128)(2,1)}) custom-call(s32[3]{0:T(128)} %pad_add_fusion.1.at_ref, bf16[4,4,592,128]{3,2,1,0:T(8,128)(2,1)} %get-tuple-element.171.keep_ref, bf16[4,4,592,128]{3,2,1,0:T(8,128)(2,1)} %copy-done.6), custom_call_target="tpu_custom_call" | custom-call | tf_op jit(solution)/shard_map/split_sum/pallas_call | solution.py:1057
  184.8 17.3 %attend_back.3 = (bf16[1536,384]{1,0:T(8,128)(2,1)}, bf16[1536,768]{1,0:T(8,128)(2,1)}, bf16[6,64,4096]{2,1,0:T(8,128)(2,1)}, f32[6,48,128]{2,1,0:T(8,128)}) custom-call(bf16[1536,512]{1,0:T(8,128)(2,1)} %get-tuple-element.130.q_ref, bf16[1536,1024]{1,0:T(8,128)(2,1)} %get-tuple-element.131.kv_ref, bf16[1536,1024]{1,0:T(8,128)(2,1)} %get-tuple-element.166.skv_ref, ...), custom_call_target="tpu_custom_call" | custom-call | tf_op jit(solution)/shard_map/attend_back/pallas_call | solution.py:588
  202.1 9.2 %sink_backward.1 = (f32[176,1024]{1,0:T(8,128)}, f32[4,64,128]{2,1,0:T(8,128)}, bf16[48,1024]{1,0:T(8,128)(2,1)}, bf16[16,1024]{1,0:T(8,128)(2,1)}) custom-call(f32[16,1536]{1,0:T(8,128)} %copy-done.9, f32[48,1536]{1,0:T(8,128)} %copy-done.5, f32[48,1536]{1,0:T(8,128)} %get-tuple-element.144.c.pc, f32[48,1536]{1,0:T(8,128)} %copy-done.4, ...), custom_call_target="tpu_custom_call" | custom-call | tf_op jit(solution)/shard_map/sink_backward/pallas_call | solution.py:293
  218.7 9.2 %halo_back.1 = (bf16[32,16,512]{2,1,0:T(8,128)(2,1)}, bf16[32,48,512]{2,1,0:T(8,128)(2,1)}, f32[1024,512]{1,0:T(8,128)}) custom-call(bf16[2,64,4096]{2,1,0:T(8,128)(2,1)} %get-tuple-element.170.low_ref, bf16[6,64,4096]{2,1,0:T(8,128)(2,1)} %get-tuple-element.197.high_ref, bf16[32,64,512]{2,1,0:T(8,128)(2,1)} %get-tuple-element.198.nh_ref, ...), custom_call_target="tpu_custom_call" | custom-call | tf_op jit(solution)/shard_map/halo_back/pallas_call | solution.py:655
  232.5 3.9 %collective-permute-done.25.fe = bf16[16,1024]{1,0:T(8,128)(2,1)S(1)} collective-permute-done((bf16[16,1024]{1,0:T(8,128)(2,1)S(1)}, bf16[16,1024]{1,0:T(8,128)(2,1)S(1)}, u32[]{:S(2)}, u32[]{:S(2)}) %collective-permute-start.25) | collective-permute-done | bytes 32800 | tf_op jit(solution)/shard_map/ppermute | solution.py:1318
  236.5 4.5 %collective-permute-start.30 = (bf16[32,48,512]{2,1,0:T(8,128)(2,1)}, bf16[32,48,512]{2,1,0:T(8,128)(2,1)S(1)}, u32[]{:S(2)}, u32[]{:S(2)}) collective-permute-start(bf16[32,48,512]{2,1,0:T(8,128)(2,1)} %get-tuple-element.205), channel_id=1, source_target_pairs={{8,0},{16,8},{24,16},{1,24},{9,1},{17,9},{25,17},{2,25},{10,2},{18... | collective-permute-start | bytes 4718600 | tf_op jit(solution)/shard_map/ppermute | solution.py:1318
  240.9 9.9 %weight_back.1 = (bf16[4,4,208,128]{3,2,1,0:T(8,128)(2,1)}, bf16[4,4,208,128]{3,2,1,0:T(8,128)(2,1)}) custom-call(s32[3]{0:T(128)} %pad_add_fusion.1.at_ref, bf16[1536,128]{1,0:T(8,128)(2,1)} %get-tuple-element.168.ql_ref, bf16[1536,384]{1,0:T(8,128)(2,1)} %get-tuple-element.215.qh_ref, bf16[1536,256]{1,0:T(8,128)(2,1)} %get-tuple-element.179.kvl_ref, ...), custom_call_target="tpu_custom_call" | custom-call | tf_op jit(solution)/shard_map/weight_back/pallas_call | solution.py:1199
  260.1 9.1 %inner_gradient.1.u_ref = f32[1536,512]{1,0:T(8,128)} custom-call(bf16[1536,128]{1,0:T(8,128)(2,1)} %get-tuple-element.168.ql_ref, bf16[1536,384]{1,0:T(8,128)(2,1)} %get-tuple-element.215.qh_ref, bf16[1536,256]{1,0:T(8,128)(2,1)} %get-tuple-element.179.kvl_ref, bf16[1536,768]{1,0:T(8,128)(2,1)} %get-tuple-element.180.kvh_ref, ...), custom_call_target="tpu_custom_call" | custom-call | tf_op jit(solution)/shard_map/inner_gradient/pallas_call | solution.py:1245
  269.2 4.4 %collective-permute-done.33.c_ref = bf16[4,208,128]{2,1,0:T(8,128)(2,1)S(1)} collective-permute-done((bf16[4,208,128]{2,1,0:T(8,128)(2,1)}, bf16[4,208,128]{2,1,0:T(8,128)(2,1)S(1)}, u32[]{:S(2)}, u32[]{:S(2)}) %collective-permute-start.33) | collective-permute-done | bytes 213024 | tf_op jit(solution)/shard_map/ppermute | solution.py:1318
  273.6 5.5 %collective-permute-done.34.d_ref = bf16[4,208,128]{2,1,0:T(8,128)(2,1)S(1)} collective-permute-done((bf16[4,208,128]{2,1,0:T(8,128)(2,1)}, bf16[4,208,128]{2,1,0:T(8,128)(2,1)S(1)}, u32[]{:S(2)}, u32[]{:S(2)}) %collective-permute-start.34) | collective-permute-done | bytes 213024 | tf_op jit(solution)/shard_map/ppermute | solution.py:1318
  281.8 5.6 %collective-permute-start.36 = (bf16[208,128]{1,0:T(8,128)(2,1)}, bf16[208,128]{1,0:T(8,128)(2,1)S(1)}, u32[]{:S(2)}, u32[]{:S(2)}) collective-permute-start(bf16[208,128]{1,0:T(8,128)(2,1)} %get-tuple-element.224), channel_id=1, source_target_pairs={{0,16},{1,17},{2,18},{3,19},{4,20},{5,21},{6,22},{7,23},{8,24},{9,... | collective-permute-start | bytes 159752 | tf_op jit(solution)/shard_map/ppermute | solution.py:1318
  292.0 8.3 %finish.1 = f32[1536,512]{1,0:T(8,128)} custom-call(bf16[1536,512]{1,0:T(8,128)(2,1)} %bitcast.55, f32[1536,512]{1,0:T(8,128)} %inner_gradient.1.u_ref, bf16[32,48,512]{2,1,0:T(8,128)(2,1)} %copy-done.8, bf16[32,16,512]{2,1,0:T(8,128)(2,1)} %copy-done.16, f32[1536,512]{1,0:T(8,128)} %get-tuple-element.217.g_ref, ...), custom_call_target="tpu_custom_call" | custom-call | tf_op jit(solution)/shard_map/finish/pallas_call | solution.py:1288
  (165 shorter events, 83.8 us)
Async XLA Ops:
  23.4 48.3 %collective-permute-start.8 = (bf16[1536,512]{1,0:T(8,128)(2,1)S(1)}, bf16[1536,512]{1,0:T(8,128)(2,1)}, u32[]{:S(2)}, u32[]{:S(2)}) collective-permute-start(bf16[1536,512]{1,0:T(8,128)(2,1)S(1)} %bitcast.56), channel_id=1, source_target_pairs={{0,8},{8,16},{16,24},{24,1},{1,9},{9,17},{17,25},{25,2},{2,10},{10... | collective-permute-start | bytes 4718600 | tf_op jit(solution)/shard_map/ppermute | solution.py:1318
  28.6 43.1 %collective-permute-start.7 = (bf16[416,512]{1,0:T(8,128)(2,1)}, bf16[416,512]{1,0:T(8,128)(2,1)}, u32[]{:S(2)}, u32[]{:S(2)}) collective-permute-start(bf16[416,512]{1,0:T(8,128)(2,1)} %get-tuple-element.133), channel_id=1, source_target_pairs={{0,16},{8,24},{16,1},{24,9},{1,17},{9,25},{17,2},{25,10},{2,18},{1... | collective-permute-start | bytes 1277960 | tf_op jit(solution)/shard_map/ppermute | solution.py:1318
  32.6 39.1 %collective-permute-start.11 = (bf16[576,128]{1,0:T(8,128)(2,1)S(1)}, bf16[576,128]{1,0:T(8,128)(2,1)}, u32[]{:S(2)}, u32[]{:S(2)}) collective-permute-start(bf16[576,128]{1,0:T(8,128)(2,1)S(1)} %copy-done.23), channel_id=1, source_target_pairs={{0,6},{1,7},{2,4},{3,5},{4,2},{5,3},{6,0},{7,1},{8,14},{9,15},{10,... | collective-permute-start | bytes 442376 | tf_op jit(solution)/shard_map/ppermute | solution.py:1318
  33.7 38.0 %collective-permute-start.10 = (bf16[576,128]{1,0:T(8,128)(2,1)S(1)}, bf16[576,128]{1,0:T(8,128)(2,1)}, u32[]{:S(2)}, u32[]{:S(2)}) collective-permute-start(bf16[576,128]{1,0:T(8,128)(2,1)S(1)} %copy-done.23), channel_id=1, source_target_pairs={{0,4},{1,5},{2,6},{3,7},{4,0},{5,1},{6,2},{7,3},{8,12},{9,13},{10,... | collective-permute-start | bytes 442376 | tf_op jit(solution)/shard_map/ppermute | solution.py:1318
  37.5 34.2 %collective-permute-start.9 = (bf16[576,128]{1,0:T(8,128)(2,1)S(1)}, bf16[576,128]{1,0:T(8,128)(2,1)}, u32[]{:S(2)}, u32[]{:S(2)}) collective-permute-start(bf16[576,128]{1,0:T(8,128)(2,1)S(1)} %copy-done.23), channel_id=1, source_target_pairs={{0,2},{1,3},{2,0},{3,1},{4,6},{5,7},{6,4},{7,5},{8,10},{9,11},{10,... | collective-permute-start | bytes 442376 | tf_op jit(solution)/shard_map/ppermute | solution.py:1318
  71.7 20.4 %collective-permute-start.14 = (f32[48,1536]{1,0:T(8,128)S(1)}, f32[48,1536]{1,0:T(8,128)S(1)}, u32[]{:S(2)}, u32[]{:S(2)}) collective-permute-start(f32[48,1536]{1,0:T(8,128)S(1)} %copy-done.3), channel_id=1, source_target_pairs={{8,0},{16,8},{24,16},{1,24},{9,1},{17,9},{25,17},{2,25},{10,2},{18... | collective-permute-start | bytes 884744 | tf_op jit(solution)/shard_map/ppermute | solution.py:1318
  73.6 18.5 %collective-permute-start.13 = (f32[48,1536]{1,0:T(8,128)S(1)}, f32[48,1536]{1,0:T(8,128)S(1)}, u32[]{:S(2)}, u32[]{:S(2)}) collective-permute-start(f32[48,1536]{1,0:T(8,128)S(1)} %copy-done.3), channel_id=1, source_target_pairs={{0,8},{8,16},{16,24},{24,1},{1,9},{9,17},{17,25},{25,2},{2,10},{10... | collective-permute-start | bytes 884744 | tf_op jit(solution)/shard_map/ppermute | solution.py:1318
  77.6 14.4 %collective-permute-start.12 = (f32[16,1536]{1,0:T(8,128)S(1)}, f32[16,1536]{1,0:T(8,128)S(1)}, u32[]{:S(2)}, u32[]{:S(2)}) collective-permute-start(f32[16,1536]{1,0:T(8,128)S(1)} %copy-done.33), channel_id=1, source_target_pairs={{0,16},{8,24},{16,1},{24,9},{1,17},{9,25},{17,2},{25,10},{2,18},{1... | collective-permute-start | bytes 294920 | tf_op jit(solution)/shard_map/ppermute | solution.py:1318
  93.5 28.9 %collective-permute-start.18 = (bf16[4,576,128]{2,1,0:T(8,128)(2,1)S(1)}, bf16[4,576,128]{2,1,0:T(8,128)(2,1)S(1)}, u32[]{:S(2)}, u32[]{:S(2)}) collective-permute-start(bf16[4,576,128]{2,1,0:T(8,128)(2,1)S(1)} %pad_maximum_fusion.2), channel_id=1, source_target_pairs={{0,24},{1,25},{2,26},{3,27},{4,28},{5,29},{6,30},{7,31},{8,16},{9,... | collective-permute-start | bytes 1769480 | tf_op jit(solution)/shard_map/ppermute | solution.py:1318
  94.3 28.1 %collective-permute-start.17 = (bf16[4,576,128]{2,1,0:T(8,128)(2,1)S(1)}, bf16[4,576,128]{2,1,0:T(8,128)(2,1)S(1)}, u32[]{:S(2)}, u32[]{:S(2)}) collective-permute-start(bf16[4,576,128]{2,1,0:T(8,128)(2,1)S(1)} %pad_maximum_fusion.2), channel_id=1, source_target_pairs={{0,16},{1,17},{2,18},{3,19},{4,20},{5,21},{6,22},{7,23},{8,24},{9,... | collective-permute-start | bytes 1769480 | tf_op jit(solution)/shard_map/ppermute | solution.py:1318
  94.3 28.1 %collective-permute-start.16 = (bf16[4,576,128]{2,1,0:T(8,128)(2,1)S(1)}, bf16[4,576,128]{2,1,0:T(8,128)(2,1)S(1)}, u32[]{:S(2)}, u32[]{:S(2)}) collective-permute-start(bf16[4,576,128]{2,1,0:T(8,128)(2,1)S(1)} %pad_maximum_fusion.2), channel_id=1, source_target_pairs={{0,8},{1,9},{2,10},{3,11},{4,12},{5,13},{6,14},{7,15},{8,0},{9,1},... | collective-permute-start | bytes 1769480 | tf_op jit(solution)/shard_map/ppermute | solution.py:1318
  181.3 30.0 %collective-permute-start.21 = (bf16[4,592,128]{2,1,0:T(8,128)(2,1)}, bf16[4,592,128]{2,1,0:T(8,128)(2,1)S(1)}, u32[]{:S(2)}, u32[]{:S(2)}) collective-permute-start(bf16[4,592,128]{2,1,0:T(8,128)(2,1)} %get-tuple-element.174), channel_id=1, source_target_pairs={{0,8},{1,9},{2,10},{3,11},{4,12},{5,13},{6,14},{7,15},{8,0},{9,1},... | collective-permute-start | bytes 1818632 | tf_op jit(solution)/shard_map/ppermute | solution.py:1318
  181.3 30.0 %collective-permute-start.22 = (bf16[4,592,128]{2,1,0:T(8,128)(2,1)}, bf16[4,592,128]{2,1,0:T(8,128)(2,1)S(1)}, u32[]{:S(2)}, u32[]{:S(2)}) collective-permute-start(bf16[4,592,128]{2,1,0:T(8,128)(2,1)} %get-tuple-element.175), channel_id=1, source_target_pairs={{0,16},{1,17},{2,18},{3,19},{4,20},{5,21},{6,22},{7,23},{8,24},{9,... | collective-permute-start | bytes 1818632 | tf_op jit(solution)/shard_map/ppermute | solution.py:1318
  182.7 28.6 %collective-permute-start.23 = (bf16[4,592,128]{2,1,0:T(8,128)(2,1)}, bf16[4,592,128]{2,1,0:T(8,128)(2,1)S(1)}, u32[]{:S(2)}, u32[]{:S(2)}) collective-permute-start(bf16[4,592,128]{2,1,0:T(8,128)(2,1)} %get-tuple-element.176), channel_id=1, source_target_pairs={{0,24},{1,25},{2,26},{3,27},{4,28},{5,29},{6,30},{7,31},{8,16},{9,... | collective-permute-start | bytes 1818632 | tf_op jit(solution)/shard_map/ppermute | solution.py:1318
  215.2 21.2 %collective-permute-start.26 = (bf16[592,128]{1,0:T(8,128)(2,1)}, bf16[592,128]{1,0:T(8,128)(2,1)S(1)}, u32[]{:S(2)}, u32[]{:S(2)}) collective-permute-start(bf16[592,128]{1,0:T(8,128)(2,1)} %get-tuple-element.194), channel_id=1, source_target_pairs={{0,2},{1,3},{2,0},{3,1},{4,6},{5,7},{6,4},{7,5},{8,10},{9,11},{10,... | collective-permute-start | bytes 454664 | tf_op jit(solution)/shard_map/ppermute | solution.py:1318
  216.3 20.1 %collective-permute-start.27 = (bf16[592,128]{1,0:T(8,128)(2,1)}, bf16[592,128]{1,0:T(8,128)(2,1)S(1)}, u32[]{:S(2)}, u32[]{:S(2)}) collective-permute-start(bf16[592,128]{1,0:T(8,128)(2,1)} %get-tuple-element.195), channel_id=1, source_target_pairs={{0,4},{1,5},{2,6},{3,7},{4,0},{5,1},{6,2},{7,3},{8,12},{9,13},{10,... | collective-permute-start | bytes 454664 | tf_op jit(solution)/shard_map/ppermute | solution.py:1318
  217.0 19.4 %collective-permute-start.28 = (bf16[592,128]{1,0:T(8,128)(2,1)}, bf16[592,128]{1,0:T(8,128)(2,1)S(1)}, u32[]{:S(2)}, u32[]{:S(2)}) collective-permute-start(bf16[592,128]{1,0:T(8,128)(2,1)} %get-tuple-element.196), channel_id=1, source_target_pairs={{0,6},{1,7},{2,4},{3,5},{4,2},{5,3},{6,0},{7,1},{8,14},{9,15},{10,... | collective-permute-start | bytes 454664 | tf_op jit(solution)/shard_map/ppermute | solution.py:1318
  236.5 54.2 %collective-permute-start.30 = (bf16[32,48,512]{2,1,0:T(8,128)(2,1)}, bf16[32,48,512]{2,1,0:T(8,128)(2,1)S(1)}, u32[]{:S(2)}, u32[]{:S(2)}) collective-permute-start(bf16[32,48,512]{2,1,0:T(8,128)(2,1)} %get-tuple-element.205), channel_id=1, source_target_pairs={{8,0},{16,8},{24,16},{1,24},{9,1},{17,9},{25,17},{2,25},{10,2},{18... | collective-permute-start | bytes 4718600 | tf_op jit(solution)/shard_map/ppermute | solution.py:1318
  250.9 39.7 %collective-permute-start.31 = (bf16[32,16,512]{2,1,0:T(8,128)(2,1)S(1)}, bf16[32,16,512]{2,1,0:T(8,128)(2,1)S(1)}, u32[]{:S(2)}, u32[]{:S(2)}) collective-permute-start(bf16[32,16,512]{2,1,0:T(8,128)(2,1)S(1)} %copy-done.30), channel_id=1, source_target_pairs={{16,0},{24,8},{1,16},{9,24},{17,1},{25,9},{2,17},{10,25},{18,2},{2... | collective-permute-start | bytes 1572872 | tf_op jit(solution)/shard_map/ppermute | solution.py:1318
  257.1 16.5 %collective-permute-start.33 = (bf16[4,208,128]{2,1,0:T(8,128)(2,1)}, bf16[4,208,128]{2,1,0:T(8,128)(2,1)S(1)}, u32[]{:S(2)}, u32[]{:S(2)}) collective-permute-start(bf16[4,208,128]{2,1,0:T(8,128)(2,1)} %get-tuple-element.213), channel_id=1, source_target_pairs={{0,4},{1,5},{2,6},{3,7},{4,0},{5,1},{6,2},{7,3},{8,12},{9,13},{10,... | collective-permute-start | bytes 638984 | tf_op jit(solution)/shard_map/ppermute | solution.py:1318
  258.5 20.6 %collective-permute-start.34 = (bf16[4,208,128]{2,1,0:T(8,128)(2,1)}, bf16[4,208,128]{2,1,0:T(8,128)(2,1)S(1)}, u32[]{:S(2)}, u32[]{:S(2)}) collective-permute-start(bf16[4,208,128]{2,1,0:T(8,128)(2,1)} %get-tuple-element.214), channel_id=1, source_target_pairs={{0,6},{1,7},{2,4},{3,5},{4,2},{5,3},{6,0},{7,1},{8,14},{9,15},{10,... | collective-permute-start | bytes 638984 | tf_op jit(solution)/shard_map/ppermute | solution.py:1318
  281.8 18.6 %collective-permute-start.35 = (bf16[208,128]{1,0:T(8,128)(2,1)}, bf16[208,128]{1,0:T(8,128)(2,1)S(1)}, u32[]{:S(2)}, u32[]{:S(2)}) collective-permute-start(bf16[208,128]{1,0:T(8,128)(2,1)} %get-tuple-element.223), channel_id=1, source_target_pairs={{0,8},{1,9},{2,10},{3,11},{4,12},{5,13},{6,14},{7,15},{8,0},{9,1},... | collective-permute-start | bytes 159752 | tf_op jit(solution)/shard_map/ppermute | solution.py:1318
  281.8 18.6 %collective-permute-start.36 = (bf16[208,128]{1,0:T(8,128)(2,1)}, bf16[208,128]{1,0:T(8,128)(2,1)S(1)}, u32[]{:S(2)}, u32[]{:S(2)}) collective-permute-start(bf16[208,128]{1,0:T(8,128)(2,1)} %get-tuple-element.224), channel_id=1, source_target_pairs={{0,16},{1,17},{2,18},{3,19},{4,20},{5,21},{6,22},{7,23},{8,24},{9,... | collective-permute-start | bytes 159752 | tf_op jit(solution)/shard_map/ppermute | solution.py:1318
  287.3 13.0 %collective-permute-start.37 = (bf16[208,128]{1,0:T(8,128)(2,1)}, bf16[208,128]{1,0:T(8,128)(2,1)S(1)}, u32[]{:S(2)}, u32[]{:S(2)}) collective-permute-start(bf16[208,128]{1,0:T(8,128)(2,1)} %get-tuple-element.225), channel_id=1, source_target_pairs={{0,24},{1,25},{2,26},{3,27},{4,28},{5,29},{6,30},{7,31},{8,16},{9,... | collective-permute-start | bytes 159752 | tf_op jit(solution)/shard_map/ppermute | solution.py:1318
  (49 other events, 423.3 us)

commit v4 on v3

--- a/solution.py
+++ b/solution.py
@@ -18,7 +18,7 @@
 LANES = 128
 PAIRS = HEADS // 2
 HALO = 64
-GROUPS = 4
+GROUPS = 6
 CHEAP = pl.CostEstimate(flops=0, transcendentals=0, bytes_accessed=0)
 EPSILON = 1e-05
 NEGATIVE = -1e30

time: 306 us -> 305 us (level)
  transfers between devices with their start and end apart: 38 -> 38, of which waited for: 13 -> 14; matrix products, arithmetic and copies ran while one was open for 2% -> 2% of each run, Pallas kernels for 42% -> 42%
where the time goes in v4:
time: 305 us; the launch traced here: 301 us
  Pallas kernels  175 us (57%)
  starting transfers between devices  64.4 us (21%)
  waiting for transfers between devices  45.5 us (15%)
  local copies, waits for them, and re-layouts  10 us (3%)
  other arithmetic  5.51 us (2%)
    ppermute x38, starting transfers between devices, send(): return lax.ppermute(value, ('head', 'plane', 'core'), pairs)  64.4 us
    ppermute x38, waiting for transfers between devices, send(): return lax.ppermute(value, ('head', 'plane', 'core'), pairs)  45.5 us
    pallas_call x1, Pallas kernels, feed_fast(): pl.pallas_call(feed_fast_kernel, grid=(tok // tile,), in_specs=[SMEM, til...  38.4 us
    pallas_call x2, Pallas kernels, attend_back(): pl.pallas_call(attend_back_kernel, grid=(pairs,), in_specs=[pl.BlockSpec(...  23.7 us
    pallas_call x2, Pallas kernels, context_project(): pl.pallas_call(functools.partial(context_kernel, len(values), keep), grid...  14.7 us
    pallas_call x1, Pallas kernels, sink_forward(): pl.pallas_call(functools.partial(sink_forward_kernel, own, context), in_s...  12.5 us
    pallas_call x1, Pallas kernels, attend(): pl.pallas_call(attend_kernel, grid=(PAIRS,), in_specs=[pl.BlockSpec((tok,...  11.4 us
    pallas_call x1, Pallas kernels, weight_back(): pl.pallas_call(functools.partial(weight_kernel, fast), grid=(tok // tile,...  9.89 us
  transfers between devices with their start and end apart: 38, of which 14 were waited for; matrix products, arithmetic and copies ran while one was open for 2% of the time, Pallas kernels for 42%

profile of v4, /device:TPU:12, one launch (start us, length us, event | category | flops | bytes accessed | tf_op | source)
XLA Modules:
  0.0 301.5 jit_solution(18303896138291509861)
XLA Ops:
  15.8 5.3 %collective-permute-done.5 = bf16[4,208,128]{2,1,0:T(8,128)(2,1)S(1)} collective-permute-done((bf16[4,208,128]{2,1,0:T(8,128)(2,1)S(1)}, bf16[4,208,128]{2,1,0:T(8,128)(2,1)S(1)}, u32[]{:S(2)}, u32[]{:S(2)}) %collective-permute-start.5) | collective-permute-done | bytes 213024 | tf_op jit(solution)/shard_map/ppermute | solution.py:1318
  33.7 3.8 %collective-permute-start.10 = (bf16[576,128]{1,0:T(8,128)(2,1)S(1)}, bf16[576,128]{1,0:T(8,128)(2,1)}, u32[]{:S(2)}, u32[]{:S(2)}) collective-permute-start(bf16[576,128]{1,0:T(8,128)(2,1)S(1)} %copy-done.23), channel_id=1, source_target_pairs={{0,4},{1,5},{2,6},{3,7},{4,0},{5,1},{6,2},{7,3},{8,12},{9,13},{10,... | collective-permute-start | bytes 442376 | tf_op jit(solution)/shard_map/ppermute | solution.py:1318
  42.4 8.3 %project.1 = (bf16[1536,512]{1,0:T(8,128)(2,1)}, bf16[1536,512]{1,0:T(8,128)(2,1)}, bf16[1536,1024]{1,0:T(8,128)(2,1)}, f32[48,1536]{1,0:T(8,128)}, f32[16,1536]{1,0:T(8,128)}, /*index=5*/f32[16,1536]{1,0:T(8,128)}) custom-call(bf16[1536,512]{1,0:T(8,128)(2,1)} %bitcast.52, f32[1,512]{1,0:T(1,128)} %get-tuple-element.137.gain_ref.refs_1_.refs_2_, ...), custom_call_target="tpu_custom_call" | custom-call | tf_op jit(solution)/shard_map/project/pallas_call | solution.py:714
  50.8 6.8 %context_own.1.kvo_ref = bf16[8,48,4096]{2,1,0:T(8,128)(2,1)} custom-call(bf16[48,32,512]{2,1,0:T(8,128)(2,1)} %bitcast.53, f32[1,512]{1,0:T(1,128)} %get-tuple-element.137.gain_ref.refs_1_.refs_2_, bf16[1024,512]{1,0:T(8,128)(2,1)} %get-tuple-element.129.wkv_ref.refs_2_.refs_3_.w_ref), custom_call_target="tpu_custom_call" | custom-call | tf_op jit(solution)/shard_map/context_own/pallas_call | solution.py:358
  57.6 14.1 %collective-permute-done.7 = bf16[416,512]{1,0:T(8,128)(2,1)} collective-permute-done((bf16[416,512]{1,0:T(8,128)(2,1)}, bf16[416,512]{1,0:T(8,128)(2,1)}, u32[]{:S(2)}, u32[]{:S(2)}) %collective-permute-start.7) | collective-permute-done | bytes 426016 | tf_op jit(solution)/shard_map/ppermute | solution.py:1318
  73.6 3.9 %collective-permute-start.13 = (f32[48,1536]{1,0:T(8,128)S(1)}, f32[48,1536]{1,0:T(8,128)S(1)}, u32[]{:S(2)}, u32[]{:S(2)}) collective-permute-start(f32[48,1536]{1,0:T(8,128)S(1)} %copy-done.3), channel_id=1, source_target_pairs={{0,8},{8,16},{16,24},{24,1},{1,9},{9,17},{17,25},{25,2},{2,10},{10... | collective-permute-start | bytes 884744 | tf_op jit(solution)/shard_map/ppermute | solution.py:1318
  79.5 3.9 %collective-permute-start.15 = (f32[16,1536]{1,0:T(8,128)S(1)}, f32[16,1536]{1,0:T(8,128)S(1)}, u32[]{:S(2)}, u32[]{:S(2)}) collective-permute-start(f32[16,1536]{1,0:T(8,128)S(1)} %copy-done.32), channel_id=1, source_target_pairs={{16,0},{24,8},{1,16},{9,24},{17,1},{25,9},{2,17},{10,25},{18,2},{2... | collective-permute-start | bytes 294920 | tf_op jit(solution)/shard_map/ppermute | solution.py:1318
  83.4 7.9 %context_halo.1 = (bf16[8,64,4096]{2,1,0:T(8,128)(2,1)}, bf16[32,64,512]{2,1,0:T(8,128)(2,1)}) custom-call(bf16[13,32,512]{2,1,0:T(8,128)(2,1)} %bitcast.21.refs_0_, bf16[48,32,512]{2,1,0:T(8,128)(2,1)} %bitcast.22.refs_1_, f32[1,512]{1,0:T(1,128)} %get-tuple-element.137.gain_ref.refs_1_.refs_2_, ...), custom_call_target="tpu_custom_call" | custom-call | tf_op jit(solution)/shard_map/context_halo/pallas_call | solution.py:358
  97.0 12.5 %sink_forward.1 = (bf16[8,48,128]{2,1,0:T(8,128)(2,1)}, f32[8,8,176,128]{3,2,1,0:T(8,128)}, f32[8,8,4,128]{3,2,1,0:T(4,128)}, f32[8,176,128]{2,1,0:T(8,128)}) custom-call(f32[16,1536]{1,0:T(8,128)} %copy-done.9, f32[48,1536]{1,0:T(8,128)} %copy-done.5, f32[48,1536]{1,0:T(8,128)} %get-tuple-element.144.c.pc, f32[48,1536]{1,0:T(8,128)} %copy-done.4, ...), custom_call_target="tpu_custom_call" | custom-call | tf_op jit(solution)/shard_map/sink_forward/pallas_call | solution.py:268
  109.6 11.4 %attend.1 = (bf16[1536,512]{1,0:T(8,128)(2,1)}, bf16[1536,1024]{1,0:T(8,128)(2,1)}) custom-call(bf16[1536,512]{1,0:T(8,128)(2,1)} %get-tuple-element.130.q_ref, bf16[1536,1024]{1,0:T(8,128)(2,1)} %get-tuple-element.131.kv_ref, bf16[8,64,4096]{2,1,0:T(8,128)(2,1)} %get-tuple-element.138.kvh_ref, bf16[8,48,4096]{2,1,0:T(8,128)(2,1)} %context_own.1.kvo_ref, ...), custom_call_target="tpu_custom_call" | custom-call | tf_op jit(solution)/shard_map/attend/pallas_call | solution.py:465
  121.5 4.5 %collective-permute-done.19.other_ref = bf16[4,4,576,128]{3,2,1,0:T(8,128)(2,1)S(1)} collective-permute-done((bf16[4,4,576,128]{3,2,1,0:T(8,128)(2,1)S(1)}, bf16[4,4,576,128]{3,2,1,0:T(8,128)(2,1)S(1)}, u32[]{:S(2)}, u32[]{:S(2)}) %collective-permute-start.19) | collective-permute-done | bytes 2359328 | tf_op jit(solution)/shard_map/ppermute | solution.py:1318
  127.5 38.4 %feed.1 = (bf16[1536,512]{1,0:T(8,128)(2,1)}, f32[1536,512]{1,0:T(8,128)}, bf16[1536,512]{1,0:T(8,128)(2,1)}, bf16[4,4,592,128]{3,2,1,0:T(8,128)(2,1)}, bf16[4,4,592,128]{3,2,1,0:T(8,128)(2,1)}) custom-call(s32[3]{0:T(128)} %pad_add_fusion.1.at_ref, bf16[1536,512]{1,0:T(8,128)(2,1)} %bitcast.54, bf16[1536,512]{1,0:T(8,128)(2,1)} %get-tuple-element.152.att_ref, ...), custom_call_target="tpu_custom_call" | custom-call | tf_op jit(solution)/shard_map/feed/pallas_call | solution.py:979
  166.1 7.6 %attend_back.2 = (bf16[1536,128]{1,0:T(8,128)(2,1)}, bf16[1536,256]{1,0:T(8,128)(2,1)}, bf16[2,64,4096]{2,1,0:T(8,128)(2,1)}, f32[2,48,128]{2,1,0:T(8,128)}) custom-call(bf16[1536,512]{1,0:T(8,128)(2,1)} %get-tuple-element.130.q_ref, bf16[1536,1024]{1,0:T(8,128)(2,1)} %get-tuple-element.131.kv_ref, bf16[1536,1024]{1,0:T(8,128)(2,1)} %get-tuple-element.166.skv_ref, ...), custom_call_target="tpu_custom_call" | custom-call | tf_op jit(solution)/shard_map/attend_back/pallas_call | solution.py:588
  175.2 4.4 %split_sum.2 = (bf16[4,592,128]{2,1,0:T(8,128)(2,1)}, bf16[4,592,128]{2,1,0:T(8,128)(2,1)}, bf16[4,592,128]{2,1,0:T(8,128)(2,1)}, bf16[4,592,128]{2,1,0:T(8,128)(2,1)}) custom-call(s32[3]{0:T(128)} %pad_add_fusion.1.at_ref, bf16[4,4,592,128]{3,2,1,0:T(8,128)(2,1)} %get-tuple-element.171.keep_ref, bf16[4,4,592,128]{3,2,1,0:T(8,128)(2,1)} %copy-done.6), custom_call_target="tpu_custom_call" | custom-call | tf_op jit(solution)/shard_map/split_sum/pallas_call | solution.py:1057
  183.1 16.2 %attend_back.3 = (bf16[1536,384]{1,0:T(8,128)(2,1)}, bf16[1536,768]{1,0:T(8,128)(2,1)}, bf16[6,64,4096]{2,1,0:T(8,128)(2,1)}, f32[6,48,128]{2,1,0:T(8,128)}) custom-call(bf16[1536,512]{1,0:T(8,128)(2,1)} %get-tuple-element.130.q_ref, bf16[1536,1024]{1,0:T(8,128)(2,1)} %get-tuple-element.131.kv_ref, bf16[1536,1024]{1,0:T(8,128)(2,1)} %get-tuple-element.166.skv_ref, ...), custom_call_target="tpu_custom_call" | custom-call | tf_op jit(solution)/shard_map/attend_back/pallas_call | solution.py:588
  199.2 9.2 %sink_backward.1 = (f32[176,1024]{1,0:T(8,128)}, f32[4,64,128]{2,1,0:T(8,128)}, bf16[48,1024]{1,0:T(8,128)(2,1)}, bf16[16,1024]{1,0:T(8,128)(2,1)}) custom-call(f32[16,1536]{1,0:T(8,128)} %copy-done.9, f32[48,1536]{1,0:T(8,128)} %copy-done.5, f32[48,1536]{1,0:T(8,128)} %get-tuple-element.144.c.pc, f32[48,1536]{1,0:T(8,128)} %copy-done.4, ...), custom_call_target="tpu_custom_call" | custom-call | tf_op jit(solution)/shard_map/sink_backward/pallas_call | solution.py:293
  216.0 9.2 %halo_back.1 = (bf16[32,16,512]{2,1,0:T(8,128)(2,1)}, bf16[32,48,512]{2,1,0:T(8,128)(2,1)}, f32[1024,512]{1,0:T(8,128)}) custom-call(bf16[2,64,4096]{2,1,0:T(8,128)(2,1)} %get-tuple-element.170.low_ref, bf16[6,64,4096]{2,1,0:T(8,128)(2,1)} %get-tuple-element.197.high_ref, bf16[32,64,512]{2,1,0:T(8,128)(2,1)} %get-tuple-element.198.nh_ref, ...), custom_call_target="tpu_custom_call" | custom-call | tf_op jit(solution)/shard_map/halo_back/pallas_call | solution.py:655
  230.8 3.9 %collective-permute-done.25.fe = bf16[16,1024]{1,0:T(8,128)(2,1)S(1)} collective-permute-done((bf16[16,1024]{1,0:T(8,128)(2,1)S(1)}, bf16[16,1024]{1,0:T(8,128)(2,1)S(1)}, u32[]{:S(2)}, u32[]{:S(2)}) %collective-permute-start.25) | collective-permute-done | bytes 32800 | tf_op jit(solution)/shard_map/ppermute | solution.py:1318
  238.3 9.9 %weight_back.1 = (bf16[4,4,208,128]{3,2,1,0:T(8,128)(2,1)}, bf16[4,4,208,128]{3,2,1,0:T(8,128)(2,1)}) custom-call(s32[3]{0:T(128)} %pad_add_fusion.1.at_ref, bf16[1536,128]{1,0:T(8,128)(2,1)} %get-tuple-element.168.ql_ref, bf16[1536,384]{1,0:T(8,128)(2,1)} %get-tuple-element.215.qh_ref, bf16[1536,256]{1,0:T(8,128)(2,1)} %get-tuple-element.179.kvl_ref, ...), custom_call_target="tpu_custom_call" | custom-call | tf_op jit(solution)/shard_map/weight_back/pallas_call | solution.py:1199
  257.5 9.1 %inner_gradient.1.u_ref = f32[1536,512]{1,0:T(8,128)} custom-call(bf16[1536,128]{1,0:T(8,128)(2,1)} %get-tuple-element.168.ql_ref, bf16[1536,384]{1,0:T(8,128)(2,1)} %get-tuple-element.215.qh_ref, bf16[1536,256]{1,0:T(8,128)(2,1)} %get-tuple-element.179.kvl_ref, bf16[1536,768]{1,0:T(8,128)(2,1)} %get-tuple-element.180.kvh_ref, ...), custom_call_target="tpu_custom_call" | custom-call | tf_op jit(solution)/shard_map/inner_gradient/pallas_call | solution.py:1245
  266.6 5.1 %collective-permute-done.33.c_ref = bf16[4,208,128]{2,1,0:T(8,128)(2,1)S(1)} collective-permute-done((bf16[4,208,128]{2,1,0:T(8,128)(2,1)}, bf16[4,208,128]{2,1,0:T(8,128)(2,1)S(1)}, u32[]{:S(2)}, u32[]{:S(2)}) %collective-permute-start.33) | collective-permute-done | bytes 213024 | tf_op jit(solution)/shard_map/ppermute | solution.py:1318
  271.7 4.7 %collective-permute-done.34.d_ref = bf16[4,208,128]{2,1,0:T(8,128)(2,1)S(1)} collective-permute-done((bf16[4,208,128]{2,1,0:T(8,128)(2,1)}, bf16[4,208,128]{2,1,0:T(8,128)(2,1)S(1)}, u32[]{:S(2)}, u32[]{:S(2)}) %collective-permute-start.34) | collective-permute-done | bytes 213024 | tf_op jit(solution)/shard_map/ppermute | solution.py:1318
  279.8 6.4 %collective-permute-start.36 = (bf16[208,128]{1,0:T(8,128)(2,1)}, bf16[208,128]{1,0:T(8,128)(2,1)S(1)}, u32[]{:S(2)}, u32[]{:S(2)}) collective-permute-start(bf16[208,128]{1,0:T(8,128)(2,1)} %get-tuple-element.224), channel_id=1, source_target_pairs={{0,16},{1,17},{2,18},{3,19},{4,20},{5,21},{6,22},{7,23},{8,24},{9,... | collective-permute-start | bytes 159752 | tf_op jit(solution)/shard_map/ppermute | solution.py:1318
  290.9 8.3 %finish.1 = f32[1536,512]{1,0:T(8,128)} custom-call(bf16[1536,512]{1,0:T(8,128)(2,1)} %bitcast.55, f32[1536,512]{1,0:T(8,128)} %inner_gradient.1.u_ref, bf16[32,48,512]{2,1,0:T(8,128)(2,1)} %copy-done.8, bf16[32,16,512]{2,1,0:T(8,128)(2,1)} %copy-done.16, f32[1536,512]{1,0:T(8,128)} %get-tuple-element.217.g_ref, ...), custom_call_target="tpu_custom_call" | custom-call | tf_op jit(solution)/shard_map/finish/pallas_call | solution.py:1288
  (165 shorter events, 85.3 us)
Async XLA Ops:
  23.4 48.3 %collective-permute-start.8 = (bf16[1536,512]{1,0:T(8,128)(2,1)S(1)}, bf16[1536,512]{1,0:T(8,128)(2,1)}, u32[]{:S(2)}, u32[]{:S(2)}) collective-permute-start(bf16[1536,512]{1,0:T(8,128)(2,1)S(1)} %bitcast.56), channel_id=1, source_target_pairs={{0,8},{8,16},{16,24},{24,1},{1,9},{9,17},{17,25},{25,2},{2,10},{10... | collective-permute-start | bytes 4718600 | tf_op jit(solution)/shard_map/ppermute | solution.py:1318
  28.6 43.1 %collective-permute-start.7 = (bf16[416,512]{1,0:T(8,128)(2,1)}, bf16[416,512]{1,0:T(8,128)(2,1)}, u32[]{:S(2)}, u32[]{:S(2)}) collective-permute-start(bf16[416,512]{1,0:T(8,128)(2,1)} %get-tuple-element.133), channel_id=1, source_target_pairs={{0,16},{8,24},{16,1},{24,9},{1,17},{9,25},{17,2},{25,10},{2,18},{1... | collective-permute-start | bytes 1277960 | tf_op jit(solution)/shard_map/ppermute | solution.py:1318
  32.6 39.1 %collective-permute-start.11 = (bf16[576,128]{1,0:T(8,128)(2,1)S(1)}, bf16[576,128]{1,0:T(8,128)(2,1)}, u32[]{:S(2)}, u32[]{:S(2)}) collective-permute-start(bf16[576,128]{1,0:T(8,128)(2,1)S(1)} %copy-done.23), channel_id=1, source_target_pairs={{0,6},{1,7},{2,4},{3,5},{4,2},{5,3},{6,0},{7,1},{8,14},{9,15},{10,... | collective-permute-start | bytes 442376 | tf_op jit(solution)/shard_map/ppermute | solution.py:1318
  33.7 38.0 %collective-permute-start.10 = (bf16[576,128]{1,0:T(8,128)(2,1)S(1)}, bf16[576,128]{1,0:T(8,128)(2,1)}, u32[]{:S(2)}, u32[]{:S(2)}) collective-permute-start(bf16[576,128]{1,0:T(8,128)(2,1)S(1)} %copy-done.23), channel_id=1, source_target_pairs={{0,4},{1,5},{2,6},{3,7},{4,0},{5,1},{6,2},{7,3},{8,12},{9,13},{10,... | collective-permute-start | bytes 442376 | tf_op jit(solution)/shard_map/ppermute | solution.py:1318
  37.5 34.2 %collective-permute-start.9 = (bf16[576,128]{1,0:T(8,128)(2,1)S(1)}, bf16[576,128]{1,0:T(8,128)(2,1)}, u32[]{:S(2)}, u32[]{:S(2)}) collective-permute-start(bf16[576,128]{1,0:T(8,128)(2,1)S(1)} %copy-done.23), channel_id=1, source_target_pairs={{0,2},{1,3},{2,0},{3,1},{4,6},{5,7},{6,4},{7,5},{8,10},{9,11},{10,... | collective-permute-start | bytes 442376 | tf_op jit(solution)/shard_map/ppermute | solution.py:1318
  71.7 20.4 %collective-permute-start.14 = (f32[48,1536]{1,0:T(8,128)S(1)}, f32[48,1536]{1,0:T(8,128)S(1)}, u32[]{:S(2)}, u32[]{:S(2)}) collective-permute-start(f32[48,1536]{1,0:T(8,128)S(1)} %copy-done.3), channel_id=1, source_target_pairs={{8,0},{16,8},{24,16},{1,24},{9,1},{17,9},{25,17},{2,25},{10,2},{18... | collective-permute-start | bytes 884744 | tf_op jit(solution)/shard_map/ppermute | solution.py:1318
  73.6 18.5 %collective-permute-start.13 = (f32[48,1536]{1,0:T(8,128)S(1)}, f32[48,1536]{1,0:T(8,128)S(1)}, u32[]{:S(2)}, u32[]{:S(2)}) collective-permute-start(f32[48,1536]{1,0:T(8,128)S(1)} %copy-done.3), channel_id=1, source_target_pairs={{0,8},{8,16},{16,24},{24,1},{1,9},{9,17},{17,25},{25,2},{2,10},{10... | collective-permute-start | bytes 884744 | tf_op jit(solution)/shard_map/ppermute | solution.py:1318
  77.6 14.4 %collective-permute-start.12 = (f32[16,1536]{1,0:T(8,128)S(1)}, f32[16,1536]{1,0:T(8,128)S(1)}, u32[]{:S(2)}, u32[]{:S(2)}) collective-permute-start(f32[16,1536]{1,0:T(8,128)S(1)} %copy-done.33), channel_id=1, source_target_pairs={{0,16},{8,24},{16,1},{24,9},{1,17},{9,25},{17,2},{25,10},{2,18},{1... | collective-permute-start | bytes 294920 | tf_op jit(solution)/shard_map/ppermute | solution.py:1318
  93.5 27.6 %collective-permute-start.18 = (bf16[4,576,128]{2,1,0:T(8,128)(2,1)S(1)}, bf16[4,576,128]{2,1,0:T(8,128)(2,1)S(1)}, u32[]{:S(2)}, u32[]{:S(2)}) collective-permute-start(bf16[4,576,128]{2,1,0:T(8,128)(2,1)S(1)} %pad_maximum_fusion.2), channel_id=1, source_target_pairs={{0,24},{1,25},{2,26},{3,27},{4,28},{5,29},{6,30},{7,31},{8,16},{9,... | collective-permute-start | bytes 1769480 | tf_op jit(solution)/shard_map/ppermute | solution.py:1318
  94.3 26.7 %collective-permute-start.17 = (bf16[4,576,128]{2,1,0:T(8,128)(2,1)S(1)}, bf16[4,576,128]{2,1,0:T(8,128)(2,1)S(1)}, u32[]{:S(2)}, u32[]{:S(2)}) collective-permute-start(bf16[4,576,128]{2,1,0:T(8,128)(2,1)S(1)} %pad_maximum_fusion.2), channel_id=1, source_target_pairs={{0,16},{1,17},{2,18},{3,19},{4,20},{5,21},{6,22},{7,23},{8,24},{9,... | collective-permute-start | bytes 1769480 | tf_op jit(solution)/shard_map/ppermute | solution.py:1318
  94.3 26.7 %collective-permute-start.16 = (bf16[4,576,128]{2,1,0:T(8,128)(2,1)S(1)}, bf16[4,576,128]{2,1,0:T(8,128)(2,1)S(1)}, u32[]{:S(2)}, u32[]{:S(2)}) collective-permute-start(bf16[4,576,128]{2,1,0:T(8,128)(2,1)S(1)} %pad_maximum_fusion.2), channel_id=1, source_target_pairs={{0,8},{1,9},{2,10},{3,11},{4,12},{5,13},{6,14},{7,15},{8,0},{9,1},... | collective-permute-start | bytes 1769480 | tf_op jit(solution)/shard_map/ppermute | solution.py:1318
  179.6 28.8 %collective-permute-start.21 = (bf16[4,592,128]{2,1,0:T(8,128)(2,1)}, bf16[4,592,128]{2,1,0:T(8,128)(2,1)S(1)}, u32[]{:S(2)}, u32[]{:S(2)}) collective-permute-start(bf16[4,592,128]{2,1,0:T(8,128)(2,1)} %get-tuple-element.174), channel_id=1, source_target_pairs={{0,8},{1,9},{2,10},{3,11},{4,12},{5,13},{6,14},{7,15},{8,0},{9,1},... | collective-permute-start | bytes 1818632 | tf_op jit(solution)/shard_map/ppermute | solution.py:1318
  179.7 29.1 %collective-permute-start.22 = (bf16[4,592,128]{2,1,0:T(8,128)(2,1)}, bf16[4,592,128]{2,1,0:T(8,128)(2,1)S(1)}, u32[]{:S(2)}, u32[]{:S(2)}) collective-permute-start(bf16[4,592,128]{2,1,0:T(8,128)(2,1)} %get-tuple-element.175), channel_id=1, source_target_pairs={{0,16},{1,17},{2,18},{3,19},{4,20},{5,21},{6,22},{7,23},{8,24},{9,... | collective-permute-start | bytes 1818632 | tf_op jit(solution)/shard_map/ppermute | solution.py:1318
  181.1 27.7 %collective-permute-start.23 = (bf16[4,592,128]{2,1,0:T(8,128)(2,1)}, bf16[4,592,128]{2,1,0:T(8,128)(2,1)S(1)}, u32[]{:S(2)}, u32[]{:S(2)}) collective-permute-start(bf16[4,592,128]{2,1,0:T(8,128)(2,1)} %get-tuple-element.176), channel_id=1, source_target_pairs={{0,24},{1,25},{2,26},{3,27},{4,28},{5,29},{6,30},{7,31},{8,16},{9,... | collective-permute-start | bytes 1818632 | tf_op jit(solution)/shard_map/ppermute | solution.py:1318
  212.5 22.1 %collective-permute-start.26 = (bf16[592,128]{1,0:T(8,128)(2,1)}, bf16[592,128]{1,0:T(8,128)(2,1)S(1)}, u32[]{:S(2)}, u32[]{:S(2)}) collective-permute-start(bf16[592,128]{1,0:T(8,128)(2,1)} %get-tuple-element.194), channel_id=1, source_target_pairs={{0,2},{1,3},{2,0},{3,1},{4,6},{5,7},{6,4},{7,5},{8,10},{9,11},{10,... | collective-permute-start | bytes 454664 | tf_op jit(solution)/shard_map/ppermute | solution.py:1318
  213.6 21.2 %collective-permute-start.27 = (bf16[592,128]{1,0:T(8,128)(2,1)}, bf16[592,128]{1,0:T(8,128)(2,1)S(1)}, u32[]{:S(2)}, u32[]{:S(2)}) collective-permute-start(bf16[592,128]{1,0:T(8,128)(2,1)} %get-tuple-element.195), channel_id=1, source_target_pairs={{0,4},{1,5},{2,6},{3,7},{4,0},{5,1},{6,2},{7,3},{8,12},{9,13},{10,... | collective-permute-start | bytes 454664 | tf_op jit(solution)/shard_map/ppermute | solution.py:1318
  215.1 19.6 %collective-permute-start.28 = (bf16[592,128]{1,0:T(8,128)(2,1)}, bf16[592,128]{1,0:T(8,128)(2,1)S(1)}, u32[]{:S(2)}, u32[]{:S(2)}) collective-permute-start(bf16[592,128]{1,0:T(8,128)(2,1)} %get-tuple-element.196), channel_id=1, source_target_pairs={{0,6},{1,7},{2,4},{3,5},{4,2},{5,3},{6,0},{7,1},{8,14},{9,15},{10,... | collective-permute-start | bytes 454664 | tf_op jit(solution)/shard_map/ppermute | solution.py:1318
  234.8 54.8 %collective-permute-start.30 = (bf16[32,48,512]{2,1,0:T(8,128)(2,1)}, bf16[32,48,512]{2,1,0:T(8,128)(2,1)S(1)}, u32[]{:S(2)}, u32[]{:S(2)}) collective-permute-start(bf16[32,48,512]{2,1,0:T(8,128)(2,1)} %get-tuple-element.205), channel_id=1, source_target_pairs={{8,0},{16,8},{24,16},{1,24},{9,1},{17,9},{25,17},{2,25},{10,2},{18... | collective-permute-start | bytes 4718600 | tf_op jit(solution)/shard_map/ppermute | solution.py:1318
  248.3 41.2 %collective-permute-start.31 = (bf16[32,16,512]{2,1,0:T(8,128)(2,1)S(1)}, bf16[32,16,512]{2,1,0:T(8,128)(2,1)S(1)}, u32[]{:S(2)}, u32[]{:S(2)}) collective-permute-start(bf16[32,16,512]{2,1,0:T(8,128)(2,1)S(1)} %copy-done.30), channel_id=1, source_target_pairs={{16,0},{24,8},{1,16},{9,24},{17,1},{25,9},{2,17},{10,25},{18,2},{2... | collective-permute-start | bytes 1572872 | tf_op jit(solution)/shard_map/ppermute | solution.py:1318
  255.3 16.4 %collective-permute-start.33 = (bf16[4,208,128]{2,1,0:T(8,128)(2,1)}, bf16[4,208,128]{2,1,0:T(8,128)(2,1)S(1)}, u32[]{:S(2)}, u32[]{:S(2)}) collective-permute-start(bf16[4,208,128]{2,1,0:T(8,128)(2,1)} %get-tuple-element.213), channel_id=1, source_target_pairs={{0,4},{1,5},{2,6},{3,7},{4,0},{5,1},{6,2},{7,3},{8,12},{9,13},{10,... | collective-permute-start | bytes 638984 | tf_op jit(solution)/shard_map/ppermute | solution.py:1318
  256.6 19.8 %collective-permute-start.34 = (bf16[4,208,128]{2,1,0:T(8,128)(2,1)}, bf16[4,208,128]{2,1,0:T(8,128)(2,1)S(1)}, u32[]{:S(2)}, u32[]{:S(2)}) collective-permute-start(bf16[4,208,128]{2,1,0:T(8,128)(2,1)} %get-tuple-element.214), channel_id=1, source_target_pairs={{0,6},{1,7},{2,4},{3,5},{4,2},{5,3},{6,0},{7,1},{8,14},{9,15},{10,... | collective-permute-start | bytes 638984 | tf_op jit(solution)/shard_map/ppermute | solution.py:1318
  279.1 20.1 %collective-permute-start.35 = (bf16[208,128]{1,0:T(8,128)(2,1)}, bf16[208,128]{1,0:T(8,128)(2,1)S(1)}, u32[]{:S(2)}, u32[]{:S(2)}) collective-permute-start(bf16[208,128]{1,0:T(8,128)(2,1)} %get-tuple-element.223), channel_id=1, source_target_pairs={{0,8},{1,9},{2,10},{3,11},{4,12},{5,13},{6,14},{7,15},{8,0},{9,1},... | collective-permute-start | bytes 159752 | tf_op jit(solution)/shard_map/ppermute | solution.py:1318
  279.8 19.4 %collective-permute-start.36 = (bf16[208,128]{1,0:T(8,128)(2,1)}, bf16[208,128]{1,0:T(8,128)(2,1)S(1)}, u32[]{:S(2)}, u32[]{:S(2)}) collective-permute-start(bf16[208,128]{1,0:T(8,128)(2,1)} %get-tuple-element.224), channel_id=1, source_target_pairs={{0,16},{1,17},{2,18},{3,19},{4,20},{5,21},{6,22},{7,23},{8,24},{9,... | collective-permute-start | bytes 159752 | tf_op jit(solution)/shard_map/ppermute | solution.py:1318
  286.2 13.0 %collective-permute-start.37 = (bf16[208,128]{1,0:T(8,128)(2,1)}, bf16[208,128]{1,0:T(8,128)(2,1)S(1)}, u32[]{:S(2)}, u32[]{:S(2)}) collective-permute-start(bf16[208,128]{1,0:T(8,128)(2,1)} %get-tuple-element.225), channel_id=1, source_target_pairs={{0,24},{1,25},{2,26},{3,27},{4,28},{5,29},{6,30},{7,31},{8,16},{9,... | collective-permute-start | bytes 159752 | tf_op jit(solution)/shard_map/ppermute | solution.py:1318
  (49 other events, 419.1 us)
